TPU v7x, 32 devices: a whole 2x2x4 slice. The times are simulated.
32 devices in a mesh: groups: 2 (over x), space: 16 (over z, y, core).
Axes of the slice: x: 2, y: 2, z: 4, core: 2. Of those that a mesh axis runs over, the one named last changes fastest.
Arguments:
- volume: bfloat16 [96, 8, 8, 16, 128], P(('groups', 'space')), parts along dimension 0, may hold values from -6 to 6
- labels: int32 [96, 1024], P(('groups', 'space')), parts along dimension 0, may hold values 0 or 1
- run_lengths: int32 [4, 4], P('groups'), parts along dimension 0, may hold values from 1 to 3, 10 in all within a row
- run_owner: int32 [32], P('groups'), parts along dimension 0, may hold values from 0 to 15, each once
- reduce_one: bfloat16 [32, 128], replicated, may hold values from -0.5 to 0.5
- core_one: bfloat16 [27, 1024], replicated, may hold values from -0.21875 to 0.21875
- expand_one: bfloat16 [32, 128], replicated, may hold values from -1 to 1
- reduce_two: bfloat16 [32, 128], replicated, may hold values from -0.5 to 0.5
- core_two: bfloat16 [27, 1024], replicated, may hold values from -0.21875 to 0.21875
- expand_two: bfloat16 [32, 128], replicated, may hold values from -1 to 1
- head_vector: bfloat16 [128], replicated, may hold values from -0.5 to 0.5
Outputs:
- fault_prob: float32 [96, 1024], P(('groups', 'space')), parts along dimension 0
- reduce_one_grad: float32 [64, 128], P('groups'), parts along dimension 0
- core_one_grad: float32 [54, 1024], P('groups'), parts along dimension 0
- expand_one_grad: float32 [64, 128], P('groups'), parts along dimension 0
- reduce_two_grad: float32 [64, 128], P('groups'), parts along dimension 0
- core_two_grad: float32 [54, 1024], P('groups'), parts along dimension 0
- expand_two_grad: float32 [64, 128], P('groups'), parts along dimension 0
- head_grad: float32 [256], P('groups'), parts along dimension 0
There are 2 independent parts, one for each index of `groups`. A program takes and returns all parts, laid end to end along the dimension named above; an argument that names none is the same for every part. Nothing has to cross between parts.
Inputs may be any that keep to these rules, and one draw needn't show every extreme that they name: run_lengths[j] cuts both crossline rows 2j and 2j+1, each of 10 pillars, into 4 runs in order from the low inline end; every row has a run of exactly 3 pillars. A permutation: run k (crossline row k // 4, the (k % 4)-th run of that row) is held by device run_owner[k] of the space axis, its pillars in that device's slots 0, 1, ... in inline order.
All inputs are finite; a program needn't handle non-finite values. No bound on the sum of `labels` on one device may be relied on, other than what follows from the above.
Results may differ from a plain program's by a relative error of at most 0.0049.
Values may be sent and summed in bfloat16 or wider, within the bound.
No kernel may reach another device: no remote copies, remote signals or barrier semaphores. Data moves between devices by JAX's collectives and lax.ppermute only.
A program may use at most 128 MiB of HBM per device.

v0:
```python
import jax
import jax.numpy as jnp
from jax import lax
from jax.sharding import PartitionSpec as P

R_ROW = 4
PCELLS = 1024


def silu_slope(values):
    sigmoid = jax.nn.sigmoid(values)
    return sigmoid * (1.0 + values * (1.0 - sigmoid))


def gather_windows(widened, direction, edge_cells, time_cells, rank_width):
    padded = jnp.pad(widened, ((0, 0), (0, 0), (0, 0), (rank_width, rank_width)))
    merged = time_cells * rank_width
    windows = []
    for along_inline in (-1, 0, 1):
        for along_cross in (-1, 0, 1):
            for along_time in (-1, 0, 1):
                lower_inline = 1 + direction * along_inline
                lower_cross = 1 + direction * along_cross
                lower_time = (1 + direction * along_time) * rank_width
                piece = padded[
                    :,
                    lower_inline : lower_inline + edge_cells,
                    lower_cross : lower_cross + edge_cells,
                    lower_time : lower_time + merged,
                ]
                windows.append(piece.reshape(-1, time_cells, rank_width))
    return jnp.stack(windows, axis=1)


def build_layout(run_lengths, run_owner, nspace, my_index, slot_count):
    run_ids = jnp.arange(nspace, dtype=jnp.int32)
    my_run = jnp.sum(jnp.where(run_owner == my_index, run_ids, 0))
    row_count = nspace // R_ROW
    my_row = my_run // R_ROW
    my_place = my_run % R_ROW
    row_lengths = jnp.repeat(run_lengths, 2, axis=0)
    run_starts = jnp.cumsum(row_lengths, axis=1) - row_lengths
    my_length = row_lengths[my_row, my_place]
    my_first = run_starts[my_row, my_place]
    slot_ids = jnp.arange(slot_count, dtype=jnp.int32)
    alive_slots = slot_ids < my_length
    pillars = my_first + slot_ids

    def neighbour(target_row):
        clipped = jnp.clip(target_row, 0, row_count - 1)
        starts_there = run_starts[clipped]
        run_there = (
            jnp.sum((starts_there[None, :] <= pillars[:, None]).astype(jnp.int32), axis=1) - 1
        )
        slot_there = pillars - starts_there[run_there]
        owner_there = run_owner[clipped * R_ROW + run_there]
        return (owner_there * slot_count + slot_there, owner_there * slot_count + slot_ids)

    low_target, low_source = neighbour(my_row - 1)
    high_target, high_source = neighbour(my_row + 1)
    return {
        "alive_slots": alive_slots,
        "slot_ids": slot_ids,
        "last_slot": my_length - 1,
        "low_target": low_target,
        "low_source": low_source,
        "low_valid": alive_slots & (my_row > 0),
        "high_target": high_target,
        "high_source": high_source,
        "high_valid": alive_slots & (my_row < row_count - 1),
        "prev_owner": run_owner[jnp.maximum(my_run - 1, 0)],
        "has_prev": my_place > 0,
        "next_owner": run_owner[jnp.minimum(my_run + 1, nspace - 1)],
        "has_next": my_place < R_ROW - 1,
    }


def crossline_send(grid_part, layout, nspace):
    slot_count = grid_part.shape[0]
    face_rows = jnp.concatenate([grid_part[:, :, 0, :], grid_part[:, :, -1, :]], axis=0).reshape(
        2 * slot_count, -1
    )
    targets = jnp.concatenate(
        [
            jnp.where(layout["low_valid"], layout["low_target"], -1),
            jnp.where(layout["high_valid"], layout["high_target"], -1),
        ]
    )
    chooser = (
        jnp.arange(nspace * slot_count, dtype=jnp.int32)[:, None] == targets[None, :]
    ).astype(jnp.bfloat16)
    return jnp.dot(chooser, face_rows, preferred_element_type=jnp.float32).astype(jnp.bfloat16)


def crossline_receive(grid_part, received, layout):
    zero_value = jnp.zeros((), jnp.bfloat16)
    face_shape = (grid_part.shape[0], grid_part.shape[1], 1, grid_part.shape[3])
    from_low = jnp.where(
        layout["low_valid"][:, None], received[layout["low_source"]], zero_value
    ).reshape(face_shape)
    from_high = jnp.where(
        layout["high_valid"][:, None], received[layout["high_source"]], zero_value
    ).reshape(face_shape)
    return jnp.concatenate([from_low, grid_part, from_high], axis=2)


def inline_send(grid_part, layout, nspace):
    low_face = grid_part[0, 0]
    high_face = lax.dynamic_index_in_dim(grid_part, layout["last_slot"], 0, keepdims=False)[-1]
    face_rows = jnp.stack([low_face, high_face]).reshape(2, -1)
    targets = jnp.stack(
        [
            jnp.where(layout["has_prev"], layout["prev_owner"], -1),
            jnp.where(layout["has_next"], layout["next_owner"], -1),
        ]
    )
    chooser = (jnp.arange(nspace, dtype=jnp.int32)[:, None] == targets[None, :]).astype(
        jnp.bfloat16
    )
    return jnp.dot(chooser, face_rows, preferred_element_type=jnp.float32).astype(jnp.bfloat16)


def inline_receive(grid_part, received, layout):
    zero_value = jnp.zeros((), jnp.bfloat16)
    face_shape = grid_part.shape[2:]
    from_prev = jnp.where(layout["has_prev"], received[layout["prev_owner"]], zero_value).reshape(
        face_shape
    )
    from_next = jnp.where(layout["has_next"], received[layout["next_owner"]], zero_value).reshape(
        face_shape
    )
    lower_rim = jnp.concatenate([from_prev[None], grid_part[:-1, -1]], axis=0)
    upper_rim = jnp.concatenate([grid_part[1:, 0], jnp.zeros_like(grid_part[:1, 0])], axis=0)
    is_last = (layout["slot_ids"] == layout["last_slot"])[:, None, None]
    upper_rim = jnp.where(is_last, from_next[None], upper_rim)
    alive = layout["alive_slots"][:, None, None]
    lower_rim = jnp.where(alive, lower_rim, zero_value)
    upper_rim = jnp.where(alive, upper_rim, zero_value)
    return jnp.concatenate([lower_rim[:, None], grid_part, upper_rim[:, None]], axis=1)


def widen(grid_part, layout, nspace):
    received = lax.all_to_all(
        inline_send(grid_part, layout, nspace), "space", split_axis=0, concat_axis=0, tiled=True
    )
    widened = inline_receive(grid_part, received, layout)
    received = lax.all_to_all(
        crossline_send(widened, layout, nspace), "space", split_axis=0, concat_axis=0, tiled=True
    )
    return crossline_receive(widened, received, layout)


def on_device(
    volume,
    labels,
    run_lengths,
    run_owner,
    reduce_one,
    core_one,
    expand_one,
    reduce_two,
    core_two,
    expand_two,
    head_vector,
):
    nspace = lax.axis_size("space")
    slot_count = volume.shape[0]
    edge_cells = volume.shape[1]
    time_cells = volume.shape[3]
    channels = volume.shape[4]
    rank_width = reduce_one.shape[0]
    merged = time_cells * rank_width
    layout = build_layout(run_lengths, run_owner, nspace, lax.axis_index("space"), slot_count)
    alive_rows = jnp.repeat(layout["alive_slots"], edge_cells * edge_cells * time_cells)
    source_one = volume.reshape(-1, channels)
    kernels_one = core_one.reshape(27, rank_width, rank_width)
    kernels_two = core_two.reshape(27, rank_width, rank_width)

    def layer_forward(source_rows, reduce_weight, kernels, expand_weight):
        reduced = lax.dot_general(
            source_rows, reduce_weight, (((1,), (1,)), ((), ())), preferred_element_type=jnp.float32
        )
        reduced = jnp.where(alive_rows[:, None], reduced, 0.0).astype(jnp.bfloat16)
        widened = widen(reduced.reshape(slot_count, edge_cells, edge_cells, merged), layout, nspace)
        columns = gather_windows(widened, 1, edge_cells, time_cells, rank_width)
        mixed = jnp.einsum("nots,osr->ntr", columns, kernels, preferred_element_type=jnp.float32)
        mixed = mixed.astype(jnp.bfloat16).reshape(-1, rank_width)
        expanded = jnp.dot(mixed, expand_weight, preferred_element_type=jnp.float32)
        output = (source_rows.astype(jnp.float32) + jax.nn.silu(expanded)).astype(jnp.bfloat16)
        return (columns, mixed, expanded, output)

    def layer_backward(upstream, source_rows, columns, mixed, expanded, kernels, expand_weight):
        delta = (upstream * silu_slope(expanded)).astype(jnp.bfloat16)
        expand_grad = lax.dot_general(
            mixed, delta, (((0,), (0,)), ((), ())), preferred_element_type=jnp.float32
        )
        mixed_grad = lax.dot_general(
            delta, expand_weight, (((1,), (1,)), ((), ())), preferred_element_type=jnp.float32
        ).astype(jnp.bfloat16)
        grad_rows = mixed_grad.reshape(-1, time_cells, rank_width)
        core_grad = jnp.einsum(
            "notr,nts->ors", columns, grad_rows, preferred_element_type=jnp.float32
        ).reshape(27, rank_width * rank_width)
        widened = widen(
            mixed_grad.reshape(slot_count, edge_cells, edge_cells, merged), layout, nspace
        )
        back_columns = gather_windows(widened, -1, edge_cells, time_cells, rank_width)
        reduced_grad = jnp.einsum(
            "nots,ors->ntr", back_columns, kernels, preferred_element_type=jnp.float32
        )
        reduced_grad = reduced_grad.astype(jnp.bfloat16).reshape(-1, rank_width)
        reduce_grad = lax.dot_general(
            reduced_grad, source_rows, (((0,), (0,)), ((), ())), preferred_element_type=jnp.float32
        )
        return (reduce_grad, core_grad, expand_grad, reduced_grad)

    columns_one, mixed_one, expanded_one, source_two = layer_forward(
        source_one, reduce_one, kernels_one, expand_one
    )
    columns_two, mixed_two, expanded_two, source_out = layer_forward(
        source_two, reduce_two, kernels_two, expand_two
    )
    logits = jnp.dot(source_out, head_vector, preferred_element_type=jnp.float32)
    chance = jax.nn.sigmoid(logits)
    differ = jnp.where(alive_rows, chance - labels.reshape(-1).astype(jnp.float32), 0.0)
    head_grad = jnp.dot(differ, source_out, preferred_element_type=jnp.float32)
    upstream_two = differ[:, None] * head_vector.astype(jnp.float32)[None, :]
    grads_two = layer_backward(
        upstream_two, source_two, columns_two, mixed_two, expanded_two, kernels_two, expand_two
    )
    passed = jnp.dot(grads_two[3], reduce_two, preferred_element_type=jnp.float32)
    upstream_one = upstream_two + passed
    grads_one = layer_backward(
        upstream_one, source_one, columns_one, mixed_one, expanded_one, kernels_one, expand_one
    )
    summed = lax.psum(
        (
            grads_one[0],
            grads_one[1],
            grads_one[2],
            grads_two[0],
            grads_two[1],
            grads_two[2],
            head_grad,
        ),
        "space",
    )
    scaled = [summed_part / PCELLS for summed_part in summed]
    fault_prob = jnp.where(alive_rows, chance, 0.0).reshape(slot_count, -1)
    return (fault_prob, scaled[0], scaled[1], scaled[2], scaled[3], scaled[4], scaled[5], scaled[6])


def solution(mesh):
    in_specs = (
        P(("groups", "space"), None, None, None, None),
        P(("groups", "space"), None),
        P("groups", None),
        P("groups"),
        P(),
        P(),
        P(),
        P(),
        P(),
        P(),
        P(),
    )
    out_specs = (
        P(("groups", "space"), None),
        P("groups", None),
        P("groups", None),
        P("groups", None),
        P("groups", None),
        P("groups", None),
        P("groups", None),
        P("groups"),
    )
    return jax.shard_map(
        on_device, mesh=mesh, in_specs=in_specs, out_specs=out_specs, check_vma=False
    )
```

profile of v0, /device:TPU:0, one launch (start us, length us, event | category | flops | bytes accessed | tf_op | source)
XLA Modules:
  0.0 779.0 jit_solution(17930731080625684874)
XLA Ops:
  15.8 1.5 fusion.6
  23.3 7.4 all-to-all-start
  45.2 6.2 all-to-all-start.1
  55.2 12.5 %all-to-all-done.1 = bf16[16,3,5120]{2,1,0:T(4,128)(2,1)S(1)} async-done(((bf16[16,3,5120]{2,1,0:T(4,128)(2,1)}), bf16[16,3,5120]{2,1,0:T(4,128)(2,1)S(1)}, u32[]{:S(2)}, u32[]{:S(2)}) %all-to-all-start.1) | async-done | bytes 491552 | tf_op jit(solution)/shard_map/all_to_all | solution.py:147
  82.3 3.0 fusion.89
  112.8 1.5 copy.454
  150.5 2.8 copy-done.2
  155.3 1.7 add_convert_fusion.1
  160.7 1.6 reshape.773
  162.3 4.7 all-to-all-start.2
  167.6 7.3 all-to-all-done.2
  179.0 1.8 convolution_convert_fusion.2
  180.7 2.2 all_to_all.63
  183.0 4.7 all-to-all-start.3
  198.5 5.4 all-to-all-done.3
  203.8 1.5 all_to_all.65
  208.4 1.5 select_maximum_fusion.8
  209.9 1.9 pad_maximum_fusion.1
  212.6 2.3 stack_reshape.376
  214.9 2.4 copy.505
  217.3 2.0 fusion.95
  219.4 2.3 stack_reshape.370
  221.7 2.4 copy.499
  224.1 2.3 stack_reshape.361
  226.5 2.4 copy.490
  228.9 2.3 stack_reshape.352
  231.2 2.4 copy.481
  235.1 2.4 copy.496
  238.9 2.4 copy.487
  241.3 2.8 fusion.88
  273.0 1.8 copy.491
  307.4 2.9 copy-done.3
  319.6 1.6 reshape.775
  321.3 4.6 all-to-all-start.4
  326.8 1.7 reshape.743
  329.9 3.9 all-to-all-done.4
  336.7 1.7 convolution_convert_fusion.1
  338.4 2.2 all_to_all.68
  340.6 4.4 all-to-all-start.5
  345.0 2.1 fusion.106
  347.1 5.4 convolution_bitcast_fusion.4
  355.5 5.9 all-to-all-done.5
  370.2 2.4 fusion.93
  384.0 1.8 copy.524
  385.7 2.4 fusion.87
  414.4 1.5 copy.529
  449.9 2.9 fusion.5
  457.4 1.6 reshape.777
  459.1 4.6 all-to-all-start.6
  466.5 1.9 reshape.640
  468.3 3.3 all-to-all-done.6
  474.5 1.7 convolution_convert_fusion
  476.2 2.2 all_to_all.73
  478.4 4.3 all-to-all-start.7
  482.7 5.4 convolution_bitcast_fusion.5
  488.1 1.9 reshape.638
  490.5 2.1 fusion.105
  492.6 2.1 fusion.104
  495.3 85.9 %all-reduce.15.cloned.1.call-done = (f32[27,1024]{1,0:T(8,128)}, f32[27,1024]{1,0:T(8,128)}) async-done(((f32[27,1024]{1,0:T(8,128)}, f32[27,1024]{1,0:T(8,128)}), (f32[27,1024]{1,0:T(8,128)}, f32[27,1024]{1,0:T(8,128)})) %all-reduce.15.cloned.1.call-update) | async-done | bytes 221200 | tf_op jit(solution)/shard_map/psum | solution.py:236
  581.3 1.6 broadcast_multiply_fusion.1
  585.8 1.5 all_to_all.75
  605.1 2.6 fusion.86
  633.5 1.6 stack_reshape.416
  678.5 87.0 %all-reduce.13.cloned.1.call-done = (f32[32,128]{1,0:T(8,128)}, f32[32,128]{1,0:T(8,128)}, f32[32,128]{1,0:T(8,128)}, f32[32,128]{1,0:T(8,128)}, f32[128]{0:T(128)}) async-done(((f32[32,128]{1,0:T(8,128)}, f32[32,128]{1,0:T(8,128)}, f32[32,128]{1,0:T(8,128)}, f32[32,128]{1,0:T(8,128)}, f32[128]{0:T(128)}), (f32[32,128]{1,0:T(8,128)}, f32[32,128]{1,0:T(8,128)}, f32[32,128]{1,0:T(8,128)}, ...) | async-done | bytes 66064 | tf_op jit(solution)/shard_map/psum | solution.py:236
  (627 shorter events, 392.6 us)
Async XLA Ops:
  7.2 305.2 %copy-start = (bf16[32,128]{1,0:T(8,128)(2,1)S(1)}, bf16[32,128]{1,0:T(8,128)(2,1)}, u32[]{:S(2)}) copy-start(bf16[32,128]{1,0:T(8,128)(2,1)} %param.20) | copy-start | bytes 24580
  7.2 44.2 %copy-start.48 = (bf16[27,1024]{1,0:T(8,128)(2,1)S(1)}, bf16[27,1024]{1,0:T(8,128)(2,1)}, u32[]{:S(2)}) copy-start(bf16[27,1024]{1,0:T(8,128)(2,1)} %param.16) | copy-start | bytes 165892
  15.7 27.6 %copy-start.60 = (pred[3]{0:T(512)(128)(4,1)}, pred[3]{0:T(512)(128)(4,1)S(1)}, u32[]{:S(2)}) copy-start(pred[3]{0:T(512)(128)(4,1)S(1)} %get-tuple-element.181) | copy-start | bytes 13
  21.2 22.1 %copy-start.67 = (s32[2]{0:T(128)}, s32[2]{0:T(128)S(1)}, u32[]{:S(2)}) copy-start(s32[2]{0:T(128)S(1)} %pad_add_fusion.1) | copy-start | bytes 28
  23.3 19.6 %all-to-all-start = ((bf16[16,2,2048]{2,1,0:T(2,128)(2,1)}), bf16[16,2,2048]{2,1,0:T(2,128)(2,1)S(1)}, u32[]{:S(2)}, u32[]{:S(2)}) async-start(bf16[16,2,2048]{2,1,0:T(2,128)(2,1)} %reshape.771), calls=%async_computation | async-start | bytes 262144 | tf_op jit(solution)/shard_map/all_to_all | solution.py:143
  37.6 33.2 %copy-start.55 = (pred[3]{0:T(512)(128)(4,1)}, pred[3]{0:T(512)(128)(4,1)S(1)}, u32[]{:S(2)}) copy-start(pred[3]{0:T(512)(128)(4,1)S(1)} %get-tuple-element.34) | copy-start | bytes 13
  38.9 31.9 %copy-start.57 = (pred[3]{0:T(512)(128)(4,1)}, pred[3]{0:T(512)(128)(4,1)S(1)}, u32[]{:S(2)}) copy-start(pred[3]{0:T(512)(128)(4,1)S(1)} %get-tuple-element.36) | copy-start | bytes 13
  39.0 31.8 %copy-start.68 = (s32[6]{0:T(128)}, s32[6]{0:T(128)S(1)}, u32[]{:S(2)}) copy-start(s32[6]{0:T(128)S(1)} %pad_add_fusion) | copy-start | bytes 76
  45.2 22.6 %all-to-all-start.1 = ((bf16[16,3,5120]{2,1,0:T(4,128)(2,1)}), bf16[16,3,5120]{2,1,0:T(4,128)(2,1)S(1)}, u32[]{:S(2)}, u32[]{:S(2)}) async-start(bf16[16,3,5120]{2,1,0:T(4,128)(2,1)} %all_to_all.58), calls=%async_computation.1 | async-start | bytes 1310720 | tf_op jit(solution)/shard_map/all_to_all | solution.py:147
  52.9 18.6 %copy-start.61 = (s32[1024]{0:T(1024)}, s32[1024]{0:T(1024)S(1)}, u32[]{:S(2)}) copy-start(s32[1024]{0:T(1024)S(1)} %pad_clamp_fusion.1) | copy-start | bytes 12292
  53.0 18.6 %copy-start.62 = (s32[1024]{0:T(1024)}, s32[1024]{0:T(1024)S(1)}, u32[]{:S(2)}) copy-start(s32[1024]{0:T(1024)S(1)} %pad_clamp_fusion) | copy-start | bytes 12292
  73.4 7.1 copy-start.44
  132.6 20.7 %copy-start.42 = (bf16[27,32,32]{2,1,0:T(8,128)(2,1)S(1)}, bf16[27,32,32]{2,1,0:T(8,128)(2,1)}, u32[]{:S(2)}) copy-start(bf16[27,32,32]{2,1,0:T(8,128)(2,1)} %reshape.627) | copy-start | bytes 165892
  149.3 6.0 copy-start.4
  155.3 34.9 %copy-start.50 = (bf16[27,1024]{1,0:T(8,128)(2,1)S(1)}, bf16[27,1024]{1,0:T(8,128)(2,1)}, u32[]{:S(2)}) copy-start(bf16[27,1024]{1,0:T(8,128)(2,1)} %param.19) | copy-start | bytes 165892
  157.0 155.4 %copy-start.5 = (bf16[3072,128]{1,0:T(8,128)(2,1)}, bf16[3072,128]{1,0:T(8,128)(2,1)S(1)}, u32[]{:S(2)}) copy-start(bf16[3072,128]{1,0:T(8,128)(2,1)S(1)} %get-tuple-element.175) | copy-start | bytes 2359300
  162.3 12.6 %all-to-all-start.2 = ((bf16[16,2,2048]{2,1,0:T(2,128)(2,1)}), bf16[16,2,2048]{2,1,0:T(2,128)(2,1)S(1)}, u32[]{:S(2)}, u32[]{:S(2)}) async-start(bf16[16,2,2048]{2,1,0:T(2,128)(2,1)} %reshape.773), calls=%async_computation.2 | async-start | bytes 262144 | tf_op jit(solution)/shard_map/all_to_all | solution.py:143
  183.0 20.9 %all-to-all-start.3 = ((bf16[16,3,5120]{2,1,0:T(4,128)(2,1)}), bf16[16,3,5120]{2,1,0:T(4,128)(2,1)}, u32[]{:S(2)}, u32[]{:S(2)}) async-start(bf16[16,3,5120]{2,1,0:T(4,128)(2,1)} %all_to_all.63), calls=%async_computation.3 | async-start | bytes 1310720 | tf_op jit(solution)/shard_map/all_to_all | solution.py:147
  288.9 18.3 %copy-start.13 = (bf16[192,1,16,32]{0,3,1,2:T(8,128)(2,1)S(1)}, bf16[192,1,16,32]{0,3,1,2:T(8,128)(2,1)}, u32[]{:S(2)}) copy-start(bf16[192,1,16,32]{0,3,1,2:T(8,128)(2,1)} %copy.502) | copy-start | bytes 589828
  293.1 13.9 %copy-start.38 = (bf16[192,1,16,32]{0,3,1,2:T(8,128)(2,1)S(1)}, bf16[192,1,16,32]{0,3,1,2:T(8,128)(2,1)}, u32[]{:S(2)}) copy-start(bf16[192,1,16,32]{0,3,1,2:T(8,128)(2,1)} %copy.494) | copy-start | bytes 589828
  293.1 13.9 %copy-start.36 = (bf16[192,1,16,32]{0,3,1,2:T(8,128)(2,1)S(1)}, bf16[192,1,16,32]{0,3,1,2:T(8,128)(2,1)}, u32[]{:S(2)}) copy-start(bf16[192,1,16,32]{0,3,1,2:T(8,128)(2,1)} %copy.495) | copy-start | bytes 589828
  293.1 13.9 %copy-start.22 = (bf16[192,1,16,32]{0,3,1,2:T(8,128)(2,1)S(1)}, bf16[192,1,16,32]{0,3,1,2:T(8,128)(2,1)}, u32[]{:S(2)}) copy-start(bf16[192,1,16,32]{0,3,1,2:T(8,128)(2,1)} %copy.496) | copy-start | bytes 589828
  293.1 14.0 %copy-start.34 = (bf16[192,1,16,32]{0,3,1,2:T(8,128)(2,1)S(1)}, bf16[192,1,16,32]{0,3,1,2:T(8,128)(2,1)}, u32[]{:S(2)}) copy-start(bf16[192,1,16,32]{0,3,1,2:T(8,128)(2,1)} %copy.497) | copy-start | bytes 589828
  293.1 14.0 %copy-start.32 = (bf16[192,1,16,32]{0,3,1,2:T(8,128)(2,1)S(1)}, bf16[192,1,16,32]{0,3,1,2:T(8,128)(2,1)}, u32[]{:S(2)}) copy-start(bf16[192,1,16,32]{0,3,1,2:T(8,128)(2,1)} %copy.498) | copy-start | bytes 589828
  293.1 14.0 %copy-start.18 = (bf16[192,1,16,32]{0,3,1,2:T(8,128)(2,1)S(1)}, bf16[192,1,16,32]{0,3,1,2:T(8,128)(2,1)}, u32[]{:S(2)}) copy-start(bf16[192,1,16,32]{0,3,1,2:T(8,128)(2,1)} %copy.499) | copy-start | bytes 589828
  293.1 14.1 %copy-start.30 = (bf16[192,1,16,32]{0,3,1,2:T(8,128)(2,1)S(1)}, bf16[192,1,16,32]{0,3,1,2:T(8,128)(2,1)}, u32[]{:S(2)}) copy-start(bf16[192,1,16,32]{0,3,1,2:T(8,128)(2,1)} %copy.500) | copy-start | bytes 589828
  293.1 14.1 %copy-start.28 = (bf16[192,1,16,32]{0,3,1,2:T(8,128)(2,1)S(1)}, bf16[192,1,16,32]{0,3,1,2:T(8,128)(2,1)}, u32[]{:S(2)}) copy-start(bf16[192,1,16,32]{0,3,1,2:T(8,128)(2,1)} %copy.501) | copy-start | bytes 589828
  293.1 14.1 %copy-start.26 = (bf16[192,1,16,32]{0,3,1,2:T(8,128)(2,1)S(1)}, bf16[192,1,16,32]{0,3,1,2:T(8,128)(2,1)}, u32[]{:S(2)}) copy-start(bf16[192,1,16,32]{0,3,1,2:T(8,128)(2,1)} %copy.503) | copy-start | bytes 589828
  293.1 14.2 %copy-start.24 = (bf16[192,1,16,32]{0,3,1,2:T(8,128)(2,1)S(1)}, bf16[192,1,16,32]{0,3,1,2:T(8,128)(2,1)}, u32[]{:S(2)}) copy-start(bf16[192,1,16,32]{0,3,1,2:T(8,128)(2,1)} %copy.504) | copy-start | bytes 589828
  293.1 14.2 %copy-start.14 = (bf16[192,1,16,32]{0,3,1,2:T(8,128)(2,1)S(1)}, bf16[192,1,16,32]{0,3,1,2:T(8,128)(2,1)}, u32[]{:S(2)}) copy-start(bf16[192,1,16,32]{0,3,1,2:T(8,128)(2,1)} %copy.505) | copy-start | bytes 589828
  293.1 14.2 %copy-start.20 = (bf16[192,1,16,32]{0,3,1,2:T(8,128)(2,1)S(1)}, bf16[192,1,16,32]{0,3,1,2:T(8,128)(2,1)}, u32[]{:S(2)}) copy-start(bf16[192,1,16,32]{0,3,1,2:T(8,128)(2,1)} %copy.506) | copy-start | bytes 589828
  293.2 17.2 %copy-start.43 = (bf16[27,32,32]{2,1,0:T(8,128)(2,1)S(1)}, bf16[27,32,32]{2,1,0:T(8,128)(2,1)}, u32[]{:S(2)}) copy-start(bf16[27,32,32]{2,1,0:T(8,128)(2,1)} %reshape.630) | copy-start | bytes 165892
  312.4 13.5 %copy-start.49 = (bf16[27,1024]{1,0:T(8,128)(2,1)S(1)}, bf16[27,1024]{1,0:T(8,128)(2,1)}, u32[]{:S(2)}) copy-start(bf16[27,1024]{1,0:T(8,128)(2,1)} %param.16) | copy-start | bytes 165892
  321.3 12.5 %all-to-all-start.4 = ((bf16[16,2,2048]{2,1,0:T(2,128)(2,1)}), bf16[16,2,2048]{2,1,0:T(2,128)(2,1)S(1)}, u32[]{:S(2)}, u32[]{:S(2)}) async-start(bf16[16,2,2048]{2,1,0:T(2,128)(2,1)} %reshape.775), calls=%async_computation.4 | async-start | bytes 262144 | tf_op jit(solution)/shard_map/all_to_all | solution.py:143
  340.6 20.9 %all-to-all-start.5 = ((bf16[16,3,5120]{2,1,0:T(4,128)(2,1)}), bf16[16,3,5120]{2,1,0:T(4,128)(2,1)}, u32[]{:S(2)}, u32[]{:S(2)}) async-start(bf16[16,3,5120]{2,1,0:T(4,128)(2,1)} %all_to_all.68), calls=%async_computation.5 | async-start | bytes 1310720 | tf_op jit(solution)/shard_map/all_to_all | solution.py:147
  347.1 17.3 %copy-start.56 = (pred[3]{0:T(512)(128)(4,1)S(1)}, pred[3]{0:T(512)(128)(4,1)}, u32[]{:S(2)}) copy-start(pred[3]{0:T(512)(128)(4,1)} %copy-done.55) | copy-start | bytes 13
  347.1 17.4 %copy-start.58 = (pred[3]{0:T(512)(128)(4,1)S(1)}, pred[3]{0:T(512)(128)(4,1)}, u32[]{:S(2)}) copy-start(pred[3]{0:T(512)(128)(4,1)} %copy-done.57) | copy-start | bytes 13
  420.4 18.8 %copy-start.17 = (bf16[192,1,16,32]{0,3,1,2:T(8,128)(2,1)S(1)}, bf16[192,1,16,32]{0,3,1,2:T(8,128)(2,1)}, u32[]{:S(2)}) copy-start(bf16[192,1,16,32]{0,3,1,2:T(8,128)(2,1)} %copy.521) | copy-start | bytes 589828
  426.4 20.7 %copy-start.12 = (bf16[192,1,16,32]{0,3,1,2:T(8,128)(2,1)S(1)}, bf16[192,1,16,32]{0,3,1,2:T(8,128)(2,1)}, u32[]{:S(2)}) copy-start(bf16[192,1,16,32]{0,3,1,2:T(8,128)(2,1)} %copy.530) | copy-start | bytes 589828
  433.8 13.8 %copy-start.15 = (bf16[192,1,16,32]{0,3,1,2:T(8,128)(2,1)S(1)}, bf16[192,1,16,32]{0,3,1,2:T(8,128)(2,1)}, u32[]{:S(2)}) copy-start(bf16[192,1,16,32]{0,3,1,2:T(8,128)(2,1)} %copy.542) | copy-start | bytes 589828
  435.1 12.0 %copy-start.39 = (bf16[192,1,16,32]{0,3,1,2:T(8,128)(2,1)S(1)}, bf16[192,1,16,32]{0,3,1,2:T(8,128)(2,1)}, u32[]{:S(2)}) copy-start(bf16[192,1,16,32]{0,3,1,2:T(8,128)(2,1)} %copy.531) | copy-start | bytes 589828
  435.2 12.0 %copy-start.37 = (bf16[192,1,16,32]{0,3,1,2:T(8,128)(2,1)S(1)}, bf16[192,1,16,32]{0,3,1,2:T(8,128)(2,1)}, u32[]{:S(2)}) copy-start(bf16[192,1,16,32]{0,3,1,2:T(8,128)(2,1)} %copy.532) | copy-start | bytes 589828
  435.2 12.1 %copy-start.23 = (bf16[192,1,16,32]{0,3,1,2:T(8,128)(2,1)S(1)}, bf16[192,1,16,32]{0,3,1,2:T(8,128)(2,1)}, u32[]{:S(2)}) copy-start(bf16[192,1,16,32]{0,3,1,2:T(8,128)(2,1)} %copy.533) | copy-start | bytes 589828
  435.2 12.1 %copy-start.35 = (bf16[192,1,16,32]{0,3,1,2:T(8,128)(2,1)S(1)}, bf16[192,1,16,32]{0,3,1,2:T(8,128)(2,1)}, u32[]{:S(2)}) copy-start(bf16[192,1,16,32]{0,3,1,2:T(8,128)(2,1)} %copy.534) | copy-start | bytes 589828
  435.2 12.2 %copy-start.33 = (bf16[192,1,16,32]{0,3,1,2:T(8,128)(2,1)S(1)}, bf16[192,1,16,32]{0,3,1,2:T(8,128)(2,1)}, u32[]{:S(2)}) copy-start(bf16[192,1,16,32]{0,3,1,2:T(8,128)(2,1)} %copy.535) | copy-start | bytes 589828
  435.2 12.2 %copy-start.19 = (bf16[192,1,16,32]{0,3,1,2:T(8,128)(2,1)S(1)}, bf16[192,1,16,32]{0,3,1,2:T(8,128)(2,1)}, u32[]{:S(2)}) copy-start(bf16[192,1,16,32]{0,3,1,2:T(8,128)(2,1)} %copy.536) | copy-start | bytes 589828
  435.2 12.2 %copy-start.31 = (bf16[192,1,16,32]{0,3,1,2:T(8,128)(2,1)S(1)}, bf16[192,1,16,32]{0,3,1,2:T(8,128)(2,1)}, u32[]{:S(2)}) copy-start(bf16[192,1,16,32]{0,3,1,2:T(8,128)(2,1)} %copy.537) | copy-start | bytes 589828
  435.2 12.2 %copy-start.29 = (bf16[192,1,16,32]{0,3,1,2:T(8,128)(2,1)S(1)}, bf16[192,1,16,32]{0,3,1,2:T(8,128)(2,1)}, u32[]{:S(2)}) copy-start(bf16[192,1,16,32]{0,3,1,2:T(8,128)(2,1)} %copy.538) | copy-start | bytes 589828
  435.2 12.3 %copy-start.27 = (bf16[192,1,16,32]{0,3,1,2:T(8,128)(2,1)S(1)}, bf16[192,1,16,32]{0,3,1,2:T(8,128)(2,1)}, u32[]{:S(2)}) copy-start(bf16[192,1,16,32]{0,3,1,2:T(8,128)(2,1)} %copy.540) | copy-start | bytes 589828
  435.2 12.3 %copy-start.25 = (bf16[192,1,16,32]{0,3,1,2:T(8,128)(2,1)S(1)}, bf16[192,1,16,32]{0,3,1,2:T(8,128)(2,1)}, u32[]{:S(2)}) copy-start(bf16[192,1,16,32]{0,3,1,2:T(8,128)(2,1)} %copy.541) | copy-start | bytes 589828
  435.2 12.4 %copy-start.21 = (bf16[192,1,16,32]{0,3,1,2:T(8,128)(2,1)S(1)}, bf16[192,1,16,32]{0,3,1,2:T(8,128)(2,1)}, u32[]{:S(2)}) copy-start(bf16[192,1,16,32]{0,3,1,2:T(8,128)(2,1)} %copy.543) | copy-start | bytes 589828
  435.2 12.4 %copy-start.41 = (bf16[27,32,32,1]{2,1,0,3:T(8,128)(2,1)S(1)}, bf16[27,32,32,1]{2,1,0,3:T(8,128)(2,1)}, u32[]{:S(2)}) copy-start(bf16[27,32,32,1]{2,1,0,3:T(8,128)(2,1)} %reshape.743) | copy-start | bytes 165892
  449.8 13.9 %copy-start.10 = (bf16[3072,128]{1,0:T(8,128)(2,1)S(1)}, bf16[3072,128]{1,0:T(8,128)(2,1)}, u32[]{:S(2)}) copy-start(bf16[3072,128]{1,0:T(8,128)(2,1)} %copy-done.9) | copy-start | bytes 2359300
  459.1 12.5 %all-to-all-start.6 = ((bf16[16,2,2048]{2,1,0:T(2,128)(2,1)}), bf16[16,2,2048]{2,1,0:T(2,128)(2,1)S(1)}, u32[]{:S(2)}, u32[]{:S(2)}) async-start(bf16[16,2,2048]{2,1,0:T(2,128)(2,1)} %reshape.777), calls=%async_computation.6 | async-start | bytes 262144 | tf_op jit(solution)/shard_map/all_to_all | solution.py:143
  468.3 22.1 %copy-start.6 = (bf16[3072,128]{1,0:T(8,128)(2,1)S(1)}, bf16[3072,128]{1,0:T(8,128)(2,1)}, u32[]{:S(2)}) copy-start(bf16[3072,128]{1,0:T(8,128)(2,1)} %copy-done.5) | copy-start | bytes 2359300
  478.4 107.4 %all-to-all-start.7 = ((bf16[16,3,5120]{2,1,0:T(4,128)(2,1)}), bf16[16,3,5120]{2,1,0:T(4,128)(2,1)}, u32[]{:S(2)}, u32[]{:S(2)}) async-start(bf16[16,3,5120]{2,1,0:T(4,128)(2,1)} %all_to_all.73), calls=%async_computation.7 | async-start | bytes 1310720 | tf_op jit(solution)/shard_map/all_to_all | solution.py:147
  482.7 98.6 %all-reduce.15.cloned.1.call-start = ((), (), s32[]{:S(2)}) async-start(), calls=%async_computation.9 | async-start | bytes 524288 | tf_op jit(solution)/shard_map/psum | solution.py:236
  488.1 100.8 %copy-start.59 = (pred[3]{0:T(512)(128)(4,1)S(1)}, pred[3]{0:T(512)(128)(4,1)}, u32[]{:S(2)}) copy-start(pred[3]{0:T(512)(128)(4,1)} %copy-done.57) | copy-start | bytes 13
  490.0 275.5 %all-reduce.13.cloned.1.call-start = ((), (), s32[]{:S(2)}) async-start(), calls=%async_computation.8 | async-start | bytes 132096 | tf_op jit(solution)/shard_map/psum | solution.py:236
  593.0 10.3 %copy-start.45 = (bf16[3,8,8,512]{3,2,1,0:T(8,128)(2,1)S(1)}, bf16[3,8,8,512]{3,2,1,0:T(8,128)(2,1)}, u32[]{:S(2)}) copy-start(bf16[3,8,8,512]{3,2,1,0:T(8,128)(2,1)} %get-tuple-element.111) | copy-start | bytes 589828
  638.3 19.6 %copy-start.16 = (bf16[192,1,16,32]{0,3,1,2:T(8,128)(2,1)S(1)}, bf16[192,1,16,32]{0,3,1,2:T(8,128)(2,1)}, u32[]{:S(2)}) copy-start(bf16[192,1,16,32]{0,3,1,2:T(8,128)(2,1)} %copy.557) | copy-start | bytes 589828
  653.9 20.7 %copy-start.40 = (bf16[27,32,32,1]{2,1,0,3:T(8,128)(2,1)S(1)}, bf16[27,32,32,1]{2,1,0,3:T(8,128)(2,1)}, u32[]{:S(2)}) copy-start(bf16[27,32,32,1]{2,1,0,3:T(8,128)(2,1)} %reshape.745) | copy-start | bytes 165892
  670.6 101.4 %copy-start.1 = (bf16[32,128]{1,0:T(8,128)(2,1)S(1)}, bf16[32,128]{1,0:T(8,128)(2,1)}, u32[]{:S(2)}) copy-start(bf16[32,128]{1,0:T(8,128)(2,1)} %param.20) | copy-start | bytes 24580
  670.6 7.2 copy-start.51
  (18 other events, 42.2 us)
Sparse Core Ops, SparseCore 0:
  490.1 91.1 all-reduce.14
  677.9 87.5 all-reduce.12
where the time goes:
time: 791 us; the launch traced here: 779 us
  local copies, waits for them, and re-layouts  416 us (53%)
  waiting for transfers between devices  211 us (27%)
  other arithmetic  41.4 us (5%)
  starting transfers between devices  41.4 us (5%)
  matrix products  41.3 us (5%)
  between operations  27.7 us (4%)
    another operation x216, local copies, waits for them, and re-layouts, gather_windows(): return jnp.stack(windows, axis=1)  271 us
    psum x2, waiting for transfers between devices, on_device(): lax.psum((grads_one[0], grads_one[1], grads_one[2], grads_two[0], grads_t...  173 us
    unnamed x276, local copies, waits for them, and re-layouts  80.7 us
    all_to_all x4, waiting for transfers between devices, widen(): lax.all_to_all(crossline_send(widened, layout, nspace), 'space', split_ax...  23.8 us
    all_to_all x4, starting transfers between devices, widen(): lax.all_to_all(inline_send(grid_part, layout, nspace), 'space', split_axi...  21.3 us
    slice x12, local copies, waits for them, and re-layouts, gather_windows(): padded[:, lower_inline:lower_inline + edge_cells, lower_cross:lower_cross...  20.2 us
    all_to_all x4, starting transfers between devices, widen(): lax.all_to_all(crossline_send(widened, layout, nspace), 'space', split_ax...  19.6 us
  transfers between devices with their start and end apart: 10, of which 8 were waited for; matrix products, arithmetic and copies ran while one was open for 8% of the time, Pallas kernels for 0%

commit v1 on v0

v1 whole, which is shorter than its diff:
```python
import functools

import jax
import jax.numpy as jnp
from jax import lax
from jax.experimental import pallas as pl
from jax.experimental.pallas import tpu as pltpu
from jax.sharding import PartitionSpec as P

BF = jnp.bfloat16
F32 = jnp.float32
SUB = 8
LIMIT = 40 * 1024 * 1024


class Dims:
    def __init__(self, nspace, slots, edge, times, channels, rank, pairs, row_runs):
        self.nspace, self.slots, self.edge, self.times = nspace, slots, edge, times
        self.channels, self.rank, self.pairs, self.row_runs = channels, rank, pairs, row_runs
        self.lanes = channels
        self.group = channels // rank
        self.tiles = times // self.group
        self.width = slots * edge
        self.rows = edge * self.width
        self.line = self.width + SUB
        self.lines = edge + 2
        self.span = self.lines * self.line
        self.core_rows = edge * self.line
        self.cells = edge * edge * times
        self.taps = 9
        self.t_send = 5
        self.t_recv = self.t_send + 2 * (1 + row_runs)
        self.t_size = self.t_recv + 2 * 3 * (slots + 2)
        self.block = (slots, self.tiles * SUB, channels)
        per_row = rank * rank // channels
        sizes = [27 * per_row, 27 * per_row, rank, rank, rank, rank, SUB]
        self.offsets = [sum(sizes[:i]) for i in range(len(sizes) + 1)]
        self.share = -(-self.offsets[-1] // (nspace * SUB)) * SUB


def dot(a, b):
    return lax.dot_general(a, b, (((1,), (0,)), ((), ())), preferred_element_type=F32)


def dot_nt(a, b):
    return lax.dot_general(a, b, (((1,), (1,)), ((), ())), preferred_element_type=F32)


def dot_tn(a, b):
    return lax.dot_general(a, b, (((0,), (0,)), ((), ())), preferred_element_type=F32)


def sigmoid(v):
    return 0.5 * jnp.tanh(0.5 * v) + 0.5


def block_diag(d, w):
    rows = []
    for j in range(d.group):
        parts = [w if i == j else jnp.zeros_like(w) for i in range(d.group)]
        rows.append(jnp.concatenate(parts, axis=1))
    return jnp.concatenate(rows, axis=0)


def permuted_rows(d, w):
    high = d.rank // d.group
    to = lax.broadcasted_iota(jnp.int32, (d.rank, d.rank), 0)
    at = lax.broadcasted_iota(jnp.int32, (d.rank, d.rank), 1)
    pick = (at == (to % high) * d.group + to // high).astype(F32).astype(BF)
    return dot(pick, w).astype(BF)


def head_rows(d, head, q, twice):
    row = lax.broadcasted_iota(jnp.int32, (d.lanes, d.channels), 0)
    wide = jnp.broadcast_to(head.astype(F32), (d.lanes, d.channels))
    parts = []
    for j in range(d.group):
        t = q * d.group + j
        hit = row == t
        if twice:
            hit = hit | (row == d.times + t)
        parts.append(jnp.where(hit, wide, 0.0))
    return jnp.concatenate(parts, axis=1).astype(BF)


def alive_mask(d, length):
    i = lax.broadcasted_iota(jnp.int32, (d.edge, d.width, d.lanes), 1)
    return (i < length * d.edge).reshape(d.rows, d.lanes)


def times_of(d, ref, q):
    return jnp.concatenate([ref[q * d.group + j] for j in range(d.group)], axis=1)


def diag_sum(d, total):
    out = None
    for j in range(d.group):
        part = total[j * d.rank : (j + 1) * d.rank, j * d.channels : (j + 1) * d.channels]
        out = part if out is None else out + part
    return out


def make_table(d, me, lengths, owner, tab):
    my_run = lax.fori_loop(0, d.nspace, lambda k, s: s + jnp.where(owner[k] == me, k, 0), jnp.int32(0))
    row = my_run // d.row_runs
    place = my_run % d.row_runs
    pair = row // 2
    start = jnp.int32(0)
    total = jnp.int32(0)
    for r in range(d.row_runs):
        one = lengths[pair, r]
        start = start + jnp.where(place > r, one, 0)
        total = total + one
    length = lengths[pair, place]
    row_count = d.nspace // d.row_runs
    tab[0] = length
    tab[1] = (place > 0).astype(jnp.int32)
    tab[2] = owner[jnp.maximum(my_run - 1, 0)]
    tab[3] = (place < d.row_runs - 1).astype(jnp.int32)
    tab[4] = owner[jnp.minimum(my_run + 1, d.nspace - 1)]
    for side, step in ((0, -1), (1, 1)):
        target = row + step
        valid = (target >= 0) & (target < row_count)
        there = jnp.clip(target, 0, row_count - 1)
        base = d.t_send + side * (1 + d.row_runs)
        tab[base] = valid.astype(jnp.int32)
        for r in range(d.row_runs):
            tab[base + 1 + r] = owner[there * d.row_runs + r]
        starts = []
        at = jnp.int32(0)
        for r in range(d.row_runs):
            starts.append(at)
            at = at + lengths[there // 2, r]
        for n in range(d.slots + 2):
            s = n - 1
            p = start + s
            ok = valid & (p >= 0) & (p < total) & (s <= length)
            run, first = jnp.int32(0), jnp.int32(0)
            for r in range(1, d.row_runs):
                past = starts[r] <= p
                run = jnp.where(past, r, run)
                first = jnp.where(past, starts[r], first)
            base = d.t_recv + (side * (d.slots + 2) + n) * 3
            tab[base] = ok.astype(jnp.int32)
            tab[base + 1] = owner[there * d.row_runs + run]
            tab[base + 2] = jnp.where(ok, p - first, 0)


def write_send(d, tab, own, send):
    for side, line in ((0, 0), (1, d.edge - 1)):
        base = d.t_send + side * (1 + d.row_runs)
        blocks = []
        for s in range(d.slots):
            at = line * d.width + s * d.edge
            blocks.append(
                jnp.concatenate([own[q, at : at + d.edge, :] for q in range(d.tiles)], axis=0).astype(BF)
            )

        @pl.when(tab[base] == 1)
        def _(base=base, blocks=blocks):
            for r in range(d.row_runs):
                for s in range(d.slots):
                    send[tab[base + 1 + r], s] = blocks[s]

    length = tab[0]
    for flag, to, at in ((1, 2, 0), (3, 4, length * d.edge - 1)):
        end = jnp.concatenate(
            [own[q, pl.ds(at, d.edge, stride=d.width), :] for q in range(d.tiles)], axis=0
        ).astype(BF)

        @pl.when(tab[flag] == 1)
        def _(to=to, end=end):
            send[tab[to], 0] = end


def fill(d, tab, own, recv, wide, shifted):
    length = tab[0]
    for q in range(d.tiles):
        wide[q] = jnp.zeros((d.span + 2 * SUB, d.lanes), F32)
        value = own[q].astype(F32)
        for c in range(d.edge):
            at = SUB + d.line * (c + 1)
            wide[q, at : at + d.width, :] = value[c * d.width : (c + 1) * d.width]
    first = SUB + d.line
    for flag, source, at in ((1, 2, first - 1), (3, 4, first + length * d.edge)):
        keep = tab[flag] == 1
        end = recv[tab[source], 0].astype(F32)
        end = jnp.where(keep, end, 0.0)
        for q in range(d.tiles):
            wide[q, pl.ds(at, d.edge, stride=d.line), :] = end[q * SUB : (q + 1) * SUB]
    sub = lax.broadcasted_iota(jnp.int32, (SUB, d.lanes), 0)
    for side, line in ((0, 0), (1, d.lines - 1)):
        at = SUB + d.line * line
        for n in range(d.slots + 2):
            s = n - 1
            base = d.t_recv + (side * (d.slots + 2) + n) * 3
            keep = tab[base] == 1
            value = recv[tab[base + 1], tab[base + 2]].astype(F32)
            value = jnp.where(keep, value, 0.0)
            for q in range(d.tiles):
                part = value[q * SUB : (q + 1) * SUB]
                if s < 0:
                    wide[q, at - 1 : at, :] = part[SUB - 1 : SUB]
                elif s == d.slots:
                    wide[q, at + s * SUB : at + s * SUB + 1, :] = part[0:1]
                else:
                    wide[q, at + s * SUB : (at + s * SUB) + SUB, :] = jnp.where((sub == 0) | (s < length), part, 0.0)
    for di in (-1, 0, 1):
        for q in range(d.tiles):
            shifted[di + 1, :, q * d.lanes : (q + 1) * d.lanes] = wide[
                q, SUB + di : SUB + di + d.span, :
            ].astype(BF)


def windows(d, shifted, direction, first, count):
    parts = []
    for di in (-1, 0, 1):
        for dc in (-1, 0, 1):
            at = d.line * (1 + direction * dc)
            parts.append(
                shifted[
                    1 + direction * di, at : at + d.core_rows, first * d.lanes : (first + count) * d.lanes
                ]
            )
    return parts


def convolve(d, shifted, inner, outer, direction, out):
    mul = dot if direction == 1 else dot_nt
    half = d.tiles // 2
    stacked = [
        jnp.concatenate(windows(d, shifted, direction, 2 * p, 2), axis=1) for p in range(half)
    ]
    total = mul(jnp.concatenate(stacked, axis=0), inner[...])
    for p in range(half):
        for n in range(2):
            out[2 * p + n] = total[p * d.core_rows : (p + 1) * d.core_rows, n * d.lanes : (n + 1) * d.lanes]
    for p in range(half - 1):
        total = mul(jnp.concatenate(windows(d, shifted, direction, 2 * p + 1, 2), axis=1), outer[...])
        for n in range(2):
            q = 2 * p + 1 + n
            out[q] = out[q] + total[:, n * d.lanes : (n + 1) * d.lanes]


def trimmed(d, value):
    return value.reshape(d.edge, d.line, d.lanes)[:, : d.width].reshape(d.rows, d.lanes)


def core_gradient(d, own, shifted, out):
    lane = lax.broadcasted_iota(jnp.int32, (1, d.lanes), 1) // d.rank
    tiles = []
    for q in range(d.tiles):
        value = own[q].astype(F32).reshape(d.edge, d.width, d.lanes)
        value = jnp.concatenate([value, jnp.zeros((d.edge, d.line - d.width, d.lanes), F32)], axis=1)
        tiles.append(value.reshape(d.core_rows, d.lanes))
    left = []
    zero = jnp.zeros_like(tiles[0])
    for q in range(d.tiles):
        after = tiles[q + 1] if q + 1 < d.tiles else zero
        before = tiles[q - 1] if q > 0 else zero
        mixed = jnp.where(lane == 0, after, jnp.where(lane == d.group - 1, before, 0.0))
        left.append(jnp.concatenate([tiles[q], mixed], axis=1).astype(BF))
    left = jnp.concatenate(left, axis=0)
    rank, group = d.rank, d.group
    high = rank // group
    wide_lane = lax.broadcasted_iota(jnp.int32, (high, d.lanes), 1) // rank
    for k in range(d.taps):
        right = jnp.concatenate([windows(d, shifted, -1, q, 1)[k] for q in range(d.tiles)], axis=0)
        total = dot_tn(left, right)
        for dt in (-1, 0, 1):
            pieces = []
            for j in range(group):
                if 0 <= j + dt < group:
                    at = (j + dt) * rank
                elif j + dt == group:
                    at = d.lanes
                else:
                    at = d.lanes + (group - 1) * rank
                pieces.append(total[at : at + rank])
            result = None
            for turn in range(group):
                mix = None
                for j in range(group):
                    rl = (j + turn) % group
                    part = pieces[j][rl * high : (rl + 1) * high]
                    mix = part if mix is None else jnp.where(wide_lane == j, part, mix)
                if turn:
                    mix = pltpu.roll(mix, turn * rank, 1)
                result = mix if result is None else result + mix
            o = 3 * k + dt + 1
            out[o * high : (o + 1) * high, :] = result


def bands_kernel(d, core_ref, inner_ref, outer_ref, inner_t_ref, outer_t_ref, flat):
    rank, group, lanes = d.rank, d.group, d.lanes
    high = rank // group
    for rh in range(high):
        flat[pl.ds(rh, 27, stride=high), :] = core_ref[:, rh * lanes : (rh + 1) * lanes].astype(F32)
    rows = flat[...].astype(BF)
    at = lax.broadcasted_iota(jnp.int32, (lanes, lanes), 0)
    to = lax.broadcasted_iota(jnp.int32, (lanes, lanes), 1)
    spread = []
    for rl in range(group):
        pick = (at == rl * rank + to % rank).astype(F32).astype(BF)
        spread.append(dot(rows, pick))
    lane = lax.broadcasted_iota(jnp.int32, (rank, lanes), 1) // rank
    zero = jnp.zeros((rank, lanes), BF)
    size = 2 * lanes
    for k in range(d.taps):
        full = []
        for dt in (-1, 0, 1):
            o = 3 * k + dt + 1
            full.append(
                jnp.concatenate([spread[rl][o * high : (o + 1) * high] for rl in range(group)], axis=0)
            )
        cache = {}
        for delta in range(-1, group + 1):
            value = jnp.zeros((rank, lanes), F32)
            for dt in (-1, 0, 1):
                value = jnp.where(lane == delta - dt, full[dt + 1], value)
            cache[delta] = value.astype(BF)

        def put(down, across, value, inside):
            one, two = (inner_ref, inner_t_ref) if inside else (outer_ref, outer_t_ref)
            one[k * size + down * rank : k * size + (down + 1) * rank, across * lanes : (across + 1) * lanes] = value
            two[down * rank : (down + 1) * rank, k * size + across * lanes : k * size + (across + 1) * lanes] = value

        for down in range(2 * group):
            for across in range(2):
                put(down, across, cache.get(down - across * group, zero), True)
                value = zero
                if down == group - 1 and across == 1:
                    value = cache[-1]
                if down == group and across == 0:
                    value = cache[group]
                put(down, across, value, False)


def first_kernel(d, me, lengths, owner, x_hbm, reduce_ref, tab, xt, own_out, send, xc, xf, own, sems):
    copies = []
    for c in range(d.edge):
        copies.append(pltpu.make_async_copy(x_hbm.at[:, :, c], xc.at[c], sems.at[c]))
    for copy in copies:
        copy.start()
    make_table(d, me[0], lengths, owner, tab)
    weight = block_diag(d, permuted_rows(d, reduce_ref[...]))
    per_line = d.width * d.times
    for c, copy in enumerate(copies):
        copy.wait()
        xf[c * per_line : (c + 1) * per_line, :] = xc[c].reshape(per_line, d.channels).astype(F32)
    alive = alive_mask(d, tab[0])
    for q in range(d.tiles):
        for j in range(d.group):
            t = q * d.group + j
            xt[t] = xf[pl.ds(t, d.rows, stride=d.times), :].astype(BF)
        value = dot_nt(times_of(d, xt, q), weight)
        value = jnp.where(alive, value, 0.0).astype(BF)
        own_out[q] = value
        own[q] = value.astype(F32)
    write_send(d, tab, own, send)


def layer_one_kernel(
    d, tab, own_in, recv, inner, outer, expand_ref, reduce_next, source, mixed, hidden, own_out, send,
    wide, shifted, conv, own,
):
    fill(d, tab, own_in, recv, wide, shifted)
    convolve(d, shifted, inner, outer, 1, conv)
    expand = block_diag(d, expand_ref[...])
    weight = block_diag(d, permuted_rows(d, reduce_next[...]))
    alive = alive_mask(d, tab[0])
    for q in range(d.tiles):
        b = trimmed(d, conv[q]).astype(BF)
        mixed[q] = b
        y = dot(b, expand)
        for j in range(d.group):
            t = q * d.group + j
            v = y[:, j * d.channels : (j + 1) * d.channels]
            hidden[t] = (source[t].astype(F32) + v * sigmoid(v)).astype(BF)
        value = dot_nt(times_of(d, hidden, q), weight)
        value = jnp.where(alive, value, 0.0).astype(BF)
        own_out[q] = value
        own[q] = value.astype(F32)
    write_send(d, tab, own, send)


def layer_two_kernel(
    d, tab, own_in, recv, inner, outer, expand_ref, head_ref, source, labels, own_out, send, chance_out, g_out,
    expand_grad, head_grad, wide, shifted, conv, own, slope, last, mixed,
):
    fill(d, tab, own_in, recv, wide, shifted)
    convolve(d, shifted, inner, outer, 1, conv)
    expand = block_diag(d, expand_ref[...])
    head = head_ref[...]
    logit = jnp.zeros((d.rows, d.lanes), F32)
    for q in range(d.tiles):
        b = trimmed(d, conv[q]).astype(BF)
        mixed[q] = b
        y = dot(b, expand)
        for j in range(d.group):
            t = q * d.group + j
            v = y[:, j * d.channels : (j + 1) * d.channels]
            s = sigmoid(v)
            slope[t] = s * (1.0 + v * (1.0 - s))
            last[t] = (source[t].astype(F32) + v * s).astype(BF)
        logit = logit + dot_nt(times_of(d, last, q), head_rows(d, head, q, False))
    chance = jax.nn.sigmoid(logit)
    lane = lax.broadcasted_iota(jnp.int32, (d.rows, d.lanes), 1)
    live = alive_mask(d, tab[0]) & (lane < d.times)
    chance = jnp.where(live, chance, 0.0)
    chance_out[...] = chance
    g = jnp.where(live, chance - labels[...], 0.0)
    coarse = g.astype(BF).astype(F32)
    pair = (coarse + pltpu.roll(g - coarse, d.times, 1)).astype(BF)
    g_out[...] = pair
    grad_e = jnp.zeros((d.rank, d.channels), F32)
    grad_h = jnp.zeros((1, d.channels), F32)
    for q in range(d.tiles):
        up = dot(pair, head_rows(d, head, q, True))
        delta = jnp.concatenate(
            [
                up[:, j * d.channels : (j + 1) * d.channels] * slope[q * d.group + j]
                for j in range(d.group)
            ],
            axis=1,
        ).astype(BF)
        value = dot_nt(delta, expand).astype(BF)
        own_out[q] = value
        own[q] = value.astype(F32)
        grad_e = grad_e + diag_sum(d, dot_tn(mixed[q], delta))
        total = dot_tn(pair, times_of(d, last, q))
        for j in range(d.group):
            t = q * d.group + j
            at = slice(j * d.channels, (j + 1) * d.channels)
            grad_h = grad_h + total[t : t + 1, at] + total[d.times + t : d.times + t + 1, at]
    expand_grad[...] = grad_e
    head_grad[...] = jnp.concatenate([grad_h, jnp.zeros((SUB - 1, d.channels), F32)], axis=0)
    write_send(d, tab, own, send)


def back_two_kernel(
    d, tab, own_in, recv, inner_t, outer_t, reduce_ref, expand_ref, head_ref, source, mixed, g_in,
    own_out, send, reduce_grad, expand_grad, shifted, wide, conv, own,
):
    fill(d, tab, own_in, recv, wide, shifted)
    convolve(d, shifted, inner_t, outer_t, -1, conv)
    expand = block_diag(d, expand_ref[...])
    weight = block_diag(d, permuted_rows(d, reduce_ref[...]))
    head = head_ref[...]
    alive = alive_mask(d, tab[0])
    pair = g_in[...]
    grad_r = jnp.zeros((d.rank, d.channels), F32)
    grad_e = jnp.zeros((d.rank, d.channels), F32)
    for q in range(d.tiles):
        da = jnp.where(alive, trimmed(d, conv[q]), 0.0).astype(BF)
        grad_r = grad_r + diag_sum(d, dot_tn(da, times_of(d, source, q)))
        up = dot(
            jnp.concatenate([da, pair], axis=1),
            jnp.concatenate([weight, head_rows(d, head, q, True)], axis=0),
        )
        b = mixed[q]
        y = dot(b, expand)
        parts = []
        for j in range(d.group):
            at = slice(j * d.channels, (j + 1) * d.channels)
            v = y[:, at]
            s = sigmoid(v)
            parts.append((up[:, at] * (s * (1.0 + v * (1.0 - s)))).astype(BF))
        delta = jnp.concatenate(parts, axis=1)
        value = dot_nt(delta, expand).astype(BF)
        own_out[q] = value
        own[q] = value.astype(F32)
        grad_e = grad_e + diag_sum(d, dot_tn(b, delta))
    reduce_grad[...] = grad_r
    expand_grad[...] = grad_e
    write_send(d, tab, own, send)


def core_kernel(d, own, shifted, out):
    core_gradient(d, own, shifted, out)


def back_one_kernel(
    d, tab, own_in, recv, inner_t, outer_t, own_first, source, core_two, expand_one, reduce_two, expand_two, head,
    packed, wide, shifted, conv,
):
    fill(d, tab, own_in, recv, wide, shifted)
    convolve(d, shifted, inner_t, outer_t, -1, conv)
    alive = alive_mask(d, tab[0])
    grad_r = jnp.zeros((d.rank, d.channels), F32)
    for q in range(d.tiles):
        da = jnp.where(alive, trimmed(d, conv[q]), 0.0).astype(BF)
        grad_r = grad_r + diag_sum(d, dot_tn(da, times_of(d, source, q)))
    off = d.offsets
    core_gradient(d, own_first, shifted, packed)
    packed[off[1] : off[2], :] = core_two[...]
    packed[off[2] : off[3], :] = grad_r
    packed[off[3] : off[4], :] = expand_one[...]
    packed[off[4] : off[5], :] = reduce_two[...]
    packed[off[5] : off[6], :] = expand_two[...]
    packed[off[6] : off[7], :] = head[...]
    rest = d.nspace * d.share - off[7]
    if rest:
        packed[off[7] :, :] = jnp.zeros((rest, d.channels), F32)


def sum_kernel(d, parts, out):
    total = parts[0]
    for n in range(1, d.nspace):
        total = total + parts[n]
    total = total * (1.0 / d.cells)
    for n in range(d.nspace):
        out[n] = total


def unpack_kernel(d, packed, reduce_one, core_one, expand_one, reduce_two, core_two, expand_two, head):
    off = d.offsets
    high = d.rank // d.group
    for at, core in ((off[0], core_one), (off[1], core_two)):
        for rh in range(high):
            core[:, rh * d.lanes : (rh + 1) * d.lanes] = packed[pl.ds(at + rh, 27, stride=high), :]
    for at, ref in ((off[2], reduce_one), (off[4], reduce_two)):
        for rl in range(d.group):
            ref[pl.ds(rl, high, stride=d.group), :] = packed[at + rl * high : at + (rl + 1) * high, :]
    expand_one[...] = packed[off[3] : off[4], :]
    expand_two[...] = packed[off[5] : off[6], :]
    head[...] = packed[off[6] : off[6] + 1, :]


VM = pl.BlockSpec(memory_space=pltpu.VMEM)
SM = pl.BlockSpec(memory_space=pltpu.SMEM)
HB = pl.BlockSpec(memory_space=pl.ANY)


def call(kernel, d, name, ins, outs, scratch, operands):
    shapes = tuple(jax.ShapeDtypeStruct(s, t) for s, t, _ in outs)
    specs = tuple(m for _, _, m in outs)
    return pl.pallas_call(
        functools.partial(kernel, d),
        out_shape=shapes,
        in_specs=list(ins),
        out_specs=specs,
        scratch_shapes=scratch,
        name=name,
        compiler_params=pltpu.CompilerParams(vmem_limit_bytes=LIMIT),
    )(*operands)


def on_device(
    volume, labels, run_lengths, run_owner, reduce_one, core_one, expand_one, reduce_two, core_two, expand_two,
    head_vector,
):
    nspace = lax.axis_size("space")
    slots, edge, _, times, channels = volume.shape
    rank = reduce_one.shape[0]
    d = Dims(nspace, slots, edge, times, channels, rank, run_lengths.shape[0], run_lengths.shape[1])
    me = lax.axis_index("space").astype(jnp.int32).reshape(1)
    head = head_vector.reshape(1, channels)
    targets = labels.reshape(slots, edge, edge, times).transpose(2, 0, 1, 3).reshape(d.rows, times)
    targets = jnp.pad(targets.astype(F32), ((0, 0), (0, d.lanes - times)))

    own_shape = (d.tiles, d.rows, d.lanes)
    wide_shape = (d.times, d.rows, d.channels)
    send_shape = (nspace,) + d.block
    shifted_shape = (3, d.span, d.tiles * d.lanes)
    own_f = pltpu.VMEM(own_shape, F32)
    rim = pltpu.VMEM((d.tiles, d.span + 2 * SUB, d.lanes), F32)
    shifted = pltpu.VMEM(shifted_shape, BF)
    conv = pltpu.VMEM((d.tiles, d.core_rows, d.lanes), F32)
    small = ((rank, channels), F32, VM)
    size = 2 * d.lanes

    def exchange(send):
        return lax.all_to_all(send, "space", split_axis=0, concat_axis=0, tiled=True)

    def bands(core, name):
        return call(
            bands_kernel, d, name, [VM],
            [((9 * size, size), BF, VM)] * 2 + [((size, 9 * size), BF, VM)] * 2,
            [pltpu.VMEM((27 * rank // d.group, d.lanes), F32)], [core],
        )

    tab, xt, a1, send = call(
        first_kernel, d, "first", [SM, SM, SM, HB, VM],
        [((d.t_size,), jnp.int32, SM), (wide_shape, BF, VM), (own_shape, BF, VM), (send_shape, BF, VM)],
        [
            pltpu.VMEM((edge, slots, edge, times, channels), BF),
            pltpu.VMEM((d.rows * times, channels), F32),
            own_f,
            pltpu.SemaphoreType.DMA((edge,)),
        ],
        [me, run_lengths, run_owner, volume, reduce_one],
    )
    inner1, outer1, inner1t, outer1t = bands(core_one, "bands_one")
    inner2, outer2, inner2t, outer2t = bands(core_two, "bands_two")
    recv = exchange(send)
    b1, h1, a2, send = call(
        layer_one_kernel, d, "layer_one", [SM] + [VM] * 7,
        [(own_shape, BF, VM), (wide_shape, BF, VM), (own_shape, BF, VM), (send_shape, BF, VM)],
        [rim, shifted, conv, own_f],
        [tab, a1, recv, inner1, outer1, expand_one, reduce_two, xt],
    )
    recv = exchange(send)
    db2, send, chance, g, eg2, hg = call(
        layer_two_kernel, d, "layer_two", [SM] + [VM] * 8,
        [
            (own_shape, BF, VM), (send_shape, BF, VM), ((d.rows, d.lanes), F32, VM), ((d.rows, d.lanes), BF, VM),
            small, ((SUB, channels), F32, VM),
        ],
        [rim, shifted, conv, own_f, pltpu.VMEM(wide_shape, F32), pltpu.VMEM(wide_shape, BF), pltpu.VMEM(own_shape, BF)],
        [tab, a2, recv, inner2, outer2, expand_two, head, h1, targets],
    )
    recv = exchange(send)
    db1, send, rg2, eg1, around = call(
        back_two_kernel, d, "back_two", [SM] + [VM] * 10,
        [(own_shape, BF, VM), (send_shape, BF, VM), small, small, (shifted_shape, BF, VM)],
        [rim, conv, own_f],
        [tab, db2, recv, inner2t, outer2t, reduce_two, expand_one, head, h1, b1, g],
    )
    core_shape = (27 * rank // d.group, d.lanes)
    (cg2,) = call(core_kernel, d, "core_two", [VM] * 2, [(core_shape, F32, VM)], [], [a2, around])
    recv = exchange(send)
    (packed,) = call(
        back_one_kernel, d, "back_one", [SM] + [VM] * 11,
        [((nspace * d.share, channels), F32, VM)],
        [rim, shifted, conv],
        [tab, db1, recv, inner1t, outer1t, a1, xt, cg2, eg1, rg2, eg2, hg],
    )
    parts = exchange(packed.reshape(nspace, d.share, channels))
    (sums,) = call(
        sum_kernel, d, "sum_parts", [VM], [((nspace, d.share, channels), F32, VM)], [], [parts]
    )
    whole = exchange(sums).reshape(nspace * d.share, channels)
    core_out = ((27, rank * rank), F32, VM)
    r1, c1, e1, r2, c2, e2, hv = call(
        unpack_kernel, d, "unpack", [VM],
        [small, core_out, small, small, core_out, small, ((1, channels), F32, VM)], [], [whole],
    )
    prob = chance[:, :times].reshape(edge, slots, edge, times).transpose(1, 2, 0, 3).reshape(slots, -1)
    return prob, r1, c1, e1, r2, c2, e2, hv.reshape(channels)


def solution(mesh):
    in_specs = (
        P(("groups", "space"), None, None, None, None),
        P(("groups", "space"), None),
        P("groups", None),
        P("groups"),
    ) + (P(),) * 7
    out_specs = (P(("groups", "space"), None),) + (P("groups", None),) * 6 + (P("groups"),)
    return jax.shard_map(on_device, mesh=mesh, in_specs=in_specs, out_specs=out_specs, check_vma=False)
```

time: 791 us -> 134 us (0.17); the launches traced: 779 us -> 132 us
  local copies, waits for them, and re-layouts: 416 us -> 28.5 us
  waiting for transfers between devices: 211 us -> 29.8 us
  matrix products: 41.3 us -> 0 us
  other arithmetic: 41.4 us -> 1.33 us
  blocking collectives: 0 us -> 30.4 us
  between operations: 27.7 us -> 0.89 us
  Pallas kernels: 0 us -> 23.2 us
  starting transfers between devices: 41.4 us -> 18.4 us
    another operation x216 -> x0, local copies, waits for them, and re-layouts: 271 us -> none  [gather_windows(): return jnp.stack(windows, axis=1)]
    psum x2 -> x0, waiting for transfers between devices: 173 us -> none  [on_device(): lax.psum((grads_one[0], grads_one[1], grads_one[2], grads_two[0], grads_t...]
    unnamed x276 -> x80, local copies, waits for them, and re-layouts: 80.7 us -> 24.8 us
    dot_general x27 -> x0, matrix products: 41.3 us -> none  [the longest x2 10.8 us: layer_backward(): jnp.einsum('notr,nts->ors', columns, grad_rows, preferred_element_type=jn...]
    all_to_all x0 -> x2, blocking collectives: none -> 30.4 us  [exchange(): lax.all_to_all(send, 'space', split_axis=0, concat_axis=0, tiled=True)]
    pallas_call x0 -> x10, Pallas kernels: none -> 23.2 us  [call(): pl.pallas_call(functools.partial(kernel, d), out_shape=shapes, in_specs=l...]
    all_to_all x8 -> x4, starting transfers between devices: 40.9 us -> 18.4 us  [exchange(): lax.all_to_all(send, 'space', split_axis=0, concat_axis=0, tiled=True)]
    slice x16 -> x0, local copies, waits for them, and re-layouts: 20.8 us -> none  [the longest x12 20.2 us: gather_windows(): padded[:, lower_inline:lower_inline + edge_cells, lower_cross:lower_cross...]
  transfers between devices with their start and end apart: 10 -> 4, of which waited for: 8 -> 4; matrix products, arithmetic and copies ran while one was open for 8% -> 4% of each run, Pallas kernels for 0% -> 2%
where the time goes in v1:
time: 134 us; the launch traced here: 132 us
  blocking collectives  30.4 us (23%)
  waiting for transfers between devices  29.8 us (22%)
  local copies, waits for them, and re-layouts  28.5 us (21%)
  Pallas kernels  23.2 us (17%)
  starting transfers between devices  18.4 us (14%)
    all_to_all x2, blocking collectives, exchange(): lax.all_to_all(send, 'space', split_axis=0, concat_axis=0, tiled=True)  30.4 us
    all_to_all x4, waiting for transfers between devices, exchange(): lax.all_to_all(send, 'space', split_axis=0, concat_axis=0, tiled=True)  29.8 us
    unnamed x80, local copies, waits for them, and re-layouts  24.8 us
    pallas_call x10, Pallas kernels, call(): pl.pallas_call(functools.partial(kernel, d), out_shape=shapes, in_specs=l...  23.2 us
    all_to_all x4, starting transfers between devices, exchange(): lax.all_to_all(send, 'space', split_axis=0, concat_axis=0, tiled=True)  18.4 us
  transfers between devices with their start and end apart: 4, of which 4 were waited for; matrix products, arithmetic and copies ran while one was open for 4% of the time, Pallas kernels for 2%

profile of v1, /device:TPU:0, one launch (start us, length us, event | category | flops | bytes accessed | tf_op | source)
XLA Modules:
  0.0 132.4 jit_solution(2458422718973098154)
XLA Ops:
  0.6 0.0 copy-start.16
  0.6 1.1 copy-done.16
  1.8 0.7 copy-done.29
  2.5 0.7 copy-done.38
  3.2 0.7 copy-done.39
  3.8 2.7 %first.1 = (s32[45]{0:T(128)S(1)}, bf16[16,192,128]{2,1,0:T(8,128)(2,1)S(1)}, bf16[4,192,128]{2,1,0:T(8,128)(2,1)S(1)}, bf16[16,3,32,128]{3,2,1,0:T(8,128)(2,1)}) custom-call(s32[1]{0:T(128)} %bitcast.me, s32[2,4]{1,0:T(2,128)S(1)} %copy-done.38, s32[16]{0:T(128)S(1)} %copy-done.39, bf16[3,8,8,16,128]{4,3,2,1,0:T(8,128)(2,1)S(1)} %copy-done.16, ...), custom_call_target="tpu_custom_call" | custom-call | tf_op jit(solution)/shard_map/first/pallas_call | solution.py:538
  6.6 0.0 copy-start.31
  6.6 7.4 %all-to-all-start = ((bf16[16,3,32,128]{3,2,1,0:T(8,128)(2,1)}), bf16[16,3,32,128]{3,2,1,0:T(8,128)(2,1)S(1)}, u32[]{:S(2)}, u32[]{:S(2)}) async-start(bf16[16,3,32,128]{3,2,1,0:T(8,128)(2,1)} %get-tuple-element.44), calls=%async_computation | async-start | bytes 786432 | tf_op jit(solution)/shard_map/all_to_all | solution.py:574
  14.0 0.0 copy-done.23
  14.0 0.8 bands_one.1
  14.8 0.0 copy-start
  14.8 1.1 copy-done
  15.9 1.0 copy-done.10
  16.9 1.0 copy-done.12
  17.9 8.2 %all-to-all-done.recv = bf16[16,3,32,128]{3,2,1,0:T(8,128)(2,1)S(1)} async-done(((bf16[16,3,32,128]{3,2,1,0:T(8,128)(2,1)}), bf16[16,3,32,128]{3,2,1,0:T(8,128)(2,1)S(1)}, u32[]{:S(2)}, u32[]{:S(2)}) %all-to-all-start) | async-done | bytes 393248 | tf_op jit(solution)/shard_map/all_to_all | solution.py:574
  26.2 0.0 copy-done.31
  26.2 0.0 copy-start.11
  26.2 1.3 copy-done.11
  27.5 1.3 copy-done.13
  28.7 0.7 copy-done.32
  29.4 3.0 %layer_one.1 = (bf16[4,192,128]{2,1,0:T(8,128)(2,1)S(1)}, bf16[16,192,128]{2,1,0:T(8,128)(2,1)S(1)}, bf16[4,192,128]{2,1,0:T(8,128)(2,1)S(1)}, bf16[16,3,32,128]{3,2,1,0:T(8,128)(2,1)S(1)}) custom-call(s32[45]{0:T(128)S(1)} %copy-done.32, bf16[4,192,128]{2,1,0:T(8,128)(2,1)S(1)} %get-tuple-element.43.own_in.own_first, ...), custom_call_target="tpu_custom_call" | custom-call | tf_op jit(solution)/shard_map/layer_one/pallas_call | solution.py:538
  32.4 0.7 copy-done.17
  33.2 0.7 copy-done.19
  33.9 3.6 %all-to-all-start.1 = ((bf16[16,3,32,128]{3,2,1,0:T(8,128)(2,1)}), bf16[16,3,32,128]{3,2,1,0:T(8,128)(2,1)S(1)}, u32[]{:S(2)}, u32[]{:S(2)}) async-start(bf16[16,3,32,128]{3,2,1,0:T(8,128)(2,1)} %copy-done.17), calls=%async_computation.1 | async-start | bytes 786432 | tf_op jit(solution)/shard_map/all_to_all | solution.py:574
  37.4 1.3 %convert_element_type.14 = f32[3,1024]{1,0:T(4,128)} convert(s32[3,1024]{1,0:T(4,128)} %param.12) | non-fusion elementwise | flops 3072 | bytes 24576 | tf_op jit(solution)/shard_map/convert_element_type | solution.py:560
  38.7 1.5 %convert_element_type.15 = f32[3,8,8,16]{3,2,1,0:T(8,128)} reshape(f32[3,1024]{1,0:T(4,128)} %convert_element_type.14) | data formatting | bytes 24576 | tf_op jit(solution)/shard_map/convert_element_type | solution.py:560
  40.2 0.9 copy.19
  41.1 0.0 copy-start.24
  41.1 0.8 copy-done.24
  42.0 0.8 bands_two.1
  42.7 1.0 copy-done.2
  43.8 1.0 copy-done.4
  44.8 1.0 copy-done.6
  45.8 1.0 copy-done.8
  46.9 0.6 pad.4.labels
  47.5 2.0 %all-to-all-done.1.recv = bf16[16,3,32,128]{3,2,1,0:T(8,128)(2,1)S(1)} async-done(((bf16[16,3,32,128]{3,2,1,0:T(8,128)(2,1)}), bf16[16,3,32,128]{3,2,1,0:T(8,128)(2,1)S(1)}, u32[]{:S(2)}, u32[]{:S(2)}) %all-to-all-start.1) | async-done | bytes 393248 | tf_op jit(solution)/shard_map/all_to_all | solution.py:574
  49.5 1.3 copy-done.7
  50.8 1.3 copy-done.9
  52.1 0.9 copy-done.18
  53.0 0.7 copy-done.30
  53.7 0.7 copy-done.33
  54.3 0.7 copy-done.37
  55.0 4.3 %layer_two.1 = (bf16[4,192,128]{2,1,0:T(8,128)(2,1)S(1)}, bf16[16,3,32,128]{3,2,1,0:T(8,128)(2,1)S(1)}, f32[192,128]{1,0:T(8,128)S(1)}, bf16[192,128]{1,0:T(8,12...) custom-call(s32[45]{0:T(128)S(1)} %copy-done.33, bf16[4,192,128]{2,1,0:T(8,128)(2,1)S(1)} %get-tuple-element.48.own_in.own, ...), custom_call_target="tpu_custom_call" | custom-call | tf_op jit(solution)/shard_map/layer_two/pallas_call | solution.py:538
  59.3 0.0 copy-start.21
  59.3 0.0 copy-start.27
  59.3 0.0 copy-start.35
  59.3 15.9 %all_to_all.30.recv = bf16[16,3,32,128]{3,2,1,0:T(8,128)(2,1)S(1)} all-to-all(bf16[16,3,32,128]{3,2,1,0:T(8,128)(2,1)S(1)} %get-tuple-element.55), channel_id=1, replica_groups=mesh['groups'=2,'space'=16] {'space'}, dimensions={0} | all-to-all | bytes 786432 | tf_op jit(solution)/shard_map/all_to_all | solution.py:574
  75.3 0.0 copy-done.3
  75.3 4.6 %back_two.1 = (bf16[4,192,128]{2,1,0:T(8,128)(2,1)S(1)}, bf16[16,3,32,128]{3,2,1,0:T(8,128)(2,1)}, f32[32,128]{1,0:T(8,128)S(1)}, f32[32,128]{1,0:T(8,128)S(1)}, bf16[3,320,512]{2,1,0:T(8,128)(2,1)S(1)}) custom-call(s32[45]{0:T(128)S(1)} %copy-done.33, bf16[4,192,128]{2,1,0:T(8,128)(2,1)S(1)} %get-tuple-element.54.own_in, ...), custom_call_target="tpu_custom_call" | custom-call | tf_op jit(solution)/shard_map/back_two/pallas_call | solution.py:538
  79.9 0.0 copy-done.27
  79.9 0.9 copy-done.14
  80.9 3.9 %all-to-all-start.3 = ((bf16[16,3,32,128]{3,2,1,0:T(8,128)(2,1)}), bf16[16,3,32,128]{3,2,1,0:T(8,128)(2,1)S(1)}, u32[]{:S(2)}, u32[]{:S(2)}) async-start(bf16[16,3,32,128]{3,2,1,0:T(8,128)(2,1)} %get-tuple-element.61), calls=%async_computation.3 | async-start | bytes 786432 | tf_op jit(solution)/shard_map/all_to_all | solution.py:574
  84.8 1.2 copy-done.15
  86.0 1.5 %core_two.1 = f32[216,128]{1,0:T(8,128)S(1)} custom-call(bf16[4,192,128]{2,1,0:T(8,128)(2,1)S(1)} %get-tuple-element.48.own_in.own, bf16[3,320,512]{2,1,0:T(8,128)(2,1)S(1)} %copy-done.15), custom_call_target="tpu_custom_call" | custom-call | tf_op jit(solution)/shard_map/core_two/pallas_call | solution.py:538
  87.5 9.3 %all-to-all-done.3.recv = bf16[16,3,32,128]{3,2,1,0:T(8,128)(2,1)S(1)} async-done(((bf16[16,3,32,128]{3,2,1,0:T(8,128)(2,1)}), bf16[16,3,32,128]{3,2,1,0:T(8,128)(2,1)S(1)}, u32[]{:S(2)}, u32[]{:S(2)}) %all-to-all-start.3) | async-done | bytes 393248 | tf_op jit(solution)/shard_map/all_to_all | solution.py:574
  96.7 0.0 copy-start.1
  96.7 1.3 copy-done.1
  98.0 3.9 %back_one.1 = f32[640,128]{1,0:T(8,128)S(1)} custom-call(s32[45]{0:T(128)S(1)} %copy-done.34, bf16[4,192,128]{2,1,0:T(8,128)(2,1)S(1)} %get-tuple-element.60.own_in, bf16[16,3,32,128]{3,2,1,0:T(8,128)(2,1)S(1)} %all-to-all-done.3.recv, bf16[256,2304]{1,0:T(8,128)(2,1)S(1)} %get-tuple-element.62.inner_t, bf16[256,2304]{1,0:T(8,128)(2,1)S(1)} %copy-done.1, ...), custom_call_target="tpu_custom_call" | custom-call | tf_op jit(solution)/shard_map/back_one/pallas_call | solution.py:538
  101.9 14.4 %all_to_all.31.parts = f32[16,40,128]{2,1,0:T(8,128)S(1)} all-to-all(f32[16,40,128]{2,1,0:T(8,128)S(1)} %bitcast.14), channel_id=1, replica_groups=mesh['groups'=2,'space'=16] {'space'}, dimensions={0} | all-to-all | bytes 655360 | tf_op jit(solution)/shard_map/all_to_all | solution.py:574
  116.3 0.8 sum_parts.1
  117.1 3.5 %all-to-all-start.5 = ((f32[16,40,128]{2,1,0:T(8,128)}), f32[16,40,128]{2,1,0:T(8,128)S(1)}, u32[]{:S(2)}, u32[]{:S(2)}) async-start(f32[16,40,128]{2,1,0:T(8,128)} %sum_parts.1), calls=%async_computation.5 | async-start | bytes 655360 | tf_op jit(solution)/shard_map/all_to_all | solution.py:574
  120.7 0.7 reshape.44
  121.4 10.3 %all-to-all-done.5 = f32[16,40,128]{2,1,0:T(8,128)S(1)} async-done(((f32[16,40,128]{2,1,0:T(8,128)}), f32[16,40,128]{2,1,0:T(8,128)S(1)}, u32[]{:S(2)}, u32[]{:S(2)}) %all-to-all-start.5) | async-done | bytes 327712 | tf_op jit(solution)/shard_map/all_to_all | solution.py:574
  131.7 0.8 unpack.1
  (42 shorter events, 0.1 us)
Async XLA Ops:
  0.6 1.1 copy-start.16
  1.8 0.7 copy-start.29
  2.5 0.7 copy-start.38
  3.2 0.7 copy-start.39
  3.8 10.2 %copy-start.23 = (bf16[27,1024]{1,0:T(8,128)(2,1)S(1)}, bf16[27,1024]{1,0:T(8,128)(2,1)}, u32[]{:S(2)}) copy-start(bf16[27,1024]{1,0:T(8,128)(2,1)} %core_ref.2) | copy-start | bytes 165892
  3.8 22.4 %copy-start.25 = (bf16[32,128]{1,0:T(8,128)(2,1)S(1)}, bf16[32,128]{1,0:T(8,128)(2,1)}, u32[]{:S(2)}) copy-start(bf16[32,128]{1,0:T(8,128)(2,1)} %expand_ref.5) | copy-start | bytes 24580
  3.8 22.4 %copy-start.26 = (bf16[32,128]{1,0:T(8,128)(2,1)S(1)}, bf16[32,128]{1,0:T(8,128)(2,1)}, u32[]{:S(2)}) copy-start(bf16[32,128]{1,0:T(8,128)(2,1)} %reduce_ref.3) | copy-start | bytes 24580
  6.6 19.6 %copy-start.31 = (s32[45]{0:T(128)}, s32[45]{0:T(128)S(1)}, u32[]{:S(2)}) copy-start(s32[45]{0:T(128)S(1)} %get-tuple-element.42.tab) | copy-start | bytes 544
  6.6 19.6 %all-to-all-start = ((bf16[16,3,32,128]{3,2,1,0:T(8,128)(2,1)}), bf16[16,3,32,128]{3,2,1,0:T(8,128)(2,1)S(1)}, u32[]{:S(2)}, u32[]{:S(2)}) async-start(bf16[16,3,32,128]{3,2,1,0:T(8,128)(2,1)} %get-tuple-element.44), calls=%async_computation | async-start | bytes 786432 | tf_op jit(solution)/shard_map/all_to_all | solution.py:574
  14.8 1.1 copy-start
  15.9 1.0 copy-start.10
  16.9 1.0 copy-start.12
  26.2 1.3 copy-start.11
  27.4 1.3 copy-start.13
  28.7 0.7 copy-start.32
  32.4 0.8 copy-start.17
  33.2 0.7 copy-start.19
  33.9 15.7 %all-to-all-start.1 = ((bf16[16,3,32,128]{3,2,1,0:T(8,128)(2,1)}), bf16[16,3,32,128]{3,2,1,0:T(8,128)(2,1)S(1)}, u32[]{:S(2)}, u32[]{:S(2)}) async-start(bf16[16,3,32,128]{3,2,1,0:T(8,128)(2,1)} %copy-done.17), calls=%async_computation.1 | async-start | bytes 786432 | tf_op jit(solution)/shard_map/all_to_all | solution.py:574
  41.1 0.8 copy-start.24
  42.7 1.0 copy-start.2
  43.8 1.0 copy-start.4
  44.8 1.0 copy-start.6
  45.8 1.0 copy-start.8
  49.5 1.3 copy-start.7
  50.8 1.3 copy-start.9
  52.1 0.9 copy-start.18
  53.0 0.7 copy-start.30
  53.7 0.7 copy-start.33
  54.3 0.7 copy-start.37
  55.0 20.3 %copy-start.3 = (bf16[256,2304]{1,0:T(8,128)(2,1)S(1)}, bf16[256,2304]{1,0:T(8,128)(2,1)}, u32[]{:S(2)}) copy-start(bf16[256,2304]{1,0:T(8,128)(2,1)} %copy-done.2) | copy-start | bytes 3538948
  55.0 20.3 %copy-start.5 = (bf16[256,2304]{1,0:T(8,128)(2,1)S(1)}, bf16[256,2304]{1,0:T(8,128)(2,1)}, u32[]{:S(2)}) copy-start(bf16[256,2304]{1,0:T(8,128)(2,1)} %copy-done.4) | copy-start | bytes 3538948
  55.0 20.3 %copy-start.20 = (bf16[4,192,128]{2,1,0:T(8,128)(2,1)S(1)}, bf16[4,192,128]{2,1,0:T(8,128)(2,1)}, u32[]{:S(2)}) copy-start(bf16[4,192,128]{2,1,0:T(8,128)(2,1)} %copy-done.19) | copy-start | bytes 589828
  59.3 20.6 %copy-start.21 = (f32[192,128]{1,0:T(8,128)}, f32[192,128]{1,0:T(8,128)S(1)}, u32[]{:S(2)}) copy-start(f32[192,128]{1,0:T(8,128)S(1)} %get-tuple-element.53) | copy-start | bytes 294916
  59.3 20.6 %copy-start.27 = (f32[32,128]{1,0:T(8,128)}, f32[32,128]{1,0:T(8,128)S(1)}, u32[]{:S(2)}) copy-start(f32[32,128]{1,0:T(8,128)S(1)} %get-tuple-element.67.expand_two) | copy-start | bytes 49156
  59.3 20.6 %copy-start.35 = (f32[8,128]{1,0:T(8,128)}, f32[8,128]{1,0:T(8,128)S(1)}, u32[]{:S(2)}) copy-start(f32[8,128]{1,0:T(8,128)S(1)} %get-tuple-element.68.head) | copy-start | bytes 12292
  79.9 1.0 copy-start.14
  80.9 15.8 %copy-start.34 = (s32[45]{0:T(128)S(1)}, s32[45]{0:T(128)}, u32[]{:S(2)}) copy-start(s32[45]{0:T(128)} %copy-done.31) | copy-start | bytes 544
  80.9 15.8 %copy-start.28 = (f32[32,128]{1,0:T(8,128)S(1)}, f32[32,128]{1,0:T(8,128)}, u32[]{:S(2)}) copy-start(f32[32,128]{1,0:T(8,128)} %copy-done.27) | copy-start | bytes 49156
  80.9 15.8 %copy-start.36 = (f32[8,128]{1,0:T(8,128)S(1)}, f32[8,128]{1,0:T(8,128)}, u32[]{:S(2)}) copy-start(f32[8,128]{1,0:T(8,128)} %copy-done.35) | copy-start | bytes 12292
  80.9 15.8 %all-to-all-start.3 = ((bf16[16,3,32,128]{3,2,1,0:T(8,128)(2,1)}), bf16[16,3,32,128]{3,2,1,0:T(8,128)(2,1)S(1)}, u32[]{:S(2)}, u32[]{:S(2)}) async-start(bf16[16,3,32,128]{3,2,1,0:T(8,128)(2,1)} %get-tuple-element.61), calls=%async_computation.3 | async-start | bytes 786432 | tf_op jit(solution)/shard_map/all_to_all | solution.py:574
  84.8 1.2 copy-start.15
  96.7 1.3 copy-start.1
  101.9 18.8 %copy-start.22 = (f32[192,128]{1,0:T(8,128)S(1)}, f32[192,128]{1,0:T(8,128)}, u32[]{:S(2)}) copy-start(f32[192,128]{1,0:T(8,128)} %copy-done.21) | copy-start | bytes 294916
  117.1 14.6 %all-to-all-start.5 = ((f32[16,40,128]{2,1,0:T(8,128)}), f32[16,40,128]{2,1,0:T(8,128)S(1)}, u32[]{:S(2)}, u32[]{:S(2)}) async-start(f32[16,40,128]{2,1,0:T(8,128)} %sum_parts.1), calls=%async_computation.5 | async-start | bytes 655360 | tf_op jit(solution)/shard_map/all_to_all | solution.py:574

commit v2 on v1

--- a/solution.py
+++ b/solution.py
@@ -10,7 +10,7 @@
 BF = jnp.bfloat16
 F32 = jnp.float32
 SUB = 8
-LIMIT = 40 * 1024 * 1024
+LIMIT = 24 * 1024 * 1024
 
 
 class Dims:
@@ -31,9 +31,10 @@
         self.t_send = 5
         self.t_recv = self.t_send + 2 * (1 + row_runs)
         self.t_size = self.t_recv + 2 * 3 * (slots + 2)
-        self.block = (slots, self.tiles * SUB, channels)
+        self.part = self.tiles * SUB
+        self.block = slots * self.part
         per_row = rank * rank // channels
-        sizes = [27 * per_row, 27 * per_row, rank, rank, rank, rank, SUB]
+        sizes = [27 * per_row, 27 * per_row, rank, rank, rank, SUB]
         self.offsets = [sum(sizes[:i]) for i in range(len(sizes) + 1)]
         self.share = -(-self.offsets[-1] // (nspace * SUB)) * SUB
 
@@ -160,7 +161,7 @@
         def _(base=base, blocks=blocks):
             for r in range(d.row_runs):
                 for s in range(d.slots):
-                    send[tab[base + 1 + r], s] = blocks[s]
+                    send[tab[base + 1 + r], s * d.part : (s + 1) * d.part, :] = blocks[s]
 
     length = tab[0]
     for flag, to, at in ((1, 2, 0), (3, 4, length * d.edge - 1)):
@@ -170,7 +171,7 @@
 
         @pl.when(tab[flag] == 1)
         def _(to=to, end=end):
-            send[tab[to], 0] = end
+            send[tab[to], : d.part, :] = end
 
 
 def fill(d, tab, own, recv, wide, shifted):
@@ -184,7 +185,7 @@
     first = SUB + d.line
     for flag, source, at in ((1, 2, first - 1), (3, 4, first + length * d.edge)):
         keep = tab[flag] == 1
-        end = recv[tab[source], 0].astype(F32)
+        end = recv[tab[source], : d.part, :].astype(F32)
         end = jnp.where(keep, end, 0.0)
         for q in range(d.tiles):
             wide[q, pl.ds(at, d.edge, stride=d.line), :] = end[q * SUB : (q + 1) * SUB]
@@ -195,8 +196,8 @@
             s = n - 1
             base = d.t_recv + (side * (d.slots + 2) + n) * 3
             keep = tab[base] == 1
-            value = recv[tab[base + 1], tab[base + 2]].astype(F32)
-            value = jnp.where(keep, value, 0.0)
+            value = recv[tab[base + 1], pl.ds(pl.multiple_of(tab[base + 2] * d.part, d.part), d.part), :]
+            value = jnp.where(keep, value.astype(F32), 0.0)
             for q in range(d.tiles):
                 part = value[q * SUB : (q + 1) * SUB]
                 if s < 0:
@@ -225,77 +226,11 @@
     return parts
 
 
-def convolve(d, shifted, inner, outer, direction, out):
-    mul = dot if direction == 1 else dot_nt
-    half = d.tiles // 2
-    stacked = [
-        jnp.concatenate(windows(d, shifted, direction, 2 * p, 2), axis=1) for p in range(half)
-    ]
-    total = mul(jnp.concatenate(stacked, axis=0), inner[...])
-    for p in range(half):
-        for n in range(2):
-            out[2 * p + n] = total[p * d.core_rows : (p + 1) * d.core_rows, n * d.lanes : (n + 1) * d.lanes]
-    for p in range(half - 1):
-        total = mul(jnp.concatenate(windows(d, shifted, direction, 2 * p + 1, 2), axis=1), outer[...])
-        for n in range(2):
-            q = 2 * p + 1 + n
-            out[q] = out[q] + total[:, n * d.lanes : (n + 1) * d.lanes]
-
-
-def trimmed(d, value):
-    return value.reshape(d.edge, d.line, d.lanes)[:, : d.width].reshape(d.rows, d.lanes)
-
-
-def core_gradient(d, own, shifted, out):
-    lane = lax.broadcasted_iota(jnp.int32, (1, d.lanes), 1) // d.rank
-    tiles = []
-    for q in range(d.tiles):
-        value = own[q].astype(F32).reshape(d.edge, d.width, d.lanes)
-        value = jnp.concatenate([value, jnp.zeros((d.edge, d.line - d.width, d.lanes), F32)], axis=1)
-        tiles.append(value.reshape(d.core_rows, d.lanes))
-    left = []
-    zero = jnp.zeros_like(tiles[0])
-    for q in range(d.tiles):
-        after = tiles[q + 1] if q + 1 < d.tiles else zero
-        before = tiles[q - 1] if q > 0 else zero
-        mixed = jnp.where(lane == 0, after, jnp.where(lane == d.group - 1, before, 0.0))
-        left.append(jnp.concatenate([tiles[q], mixed], axis=1).astype(BF))
-    left = jnp.concatenate(left, axis=0)
-    rank, group = d.rank, d.group
-    high = rank // group
-    wide_lane = lax.broadcasted_iota(jnp.int32, (high, d.lanes), 1) // rank
-    for k in range(d.taps):
-        right = jnp.concatenate([windows(d, shifted, -1, q, 1)[k] for q in range(d.tiles)], axis=0)
-        total = dot_tn(left, right)
-        for dt in (-1, 0, 1):
-            pieces = []
-            for j in range(group):
-                if 0 <= j + dt < group:
-                    at = (j + dt) * rank
-                elif j + dt == group:
-                    at = d.lanes
-                else:
-                    at = d.lanes + (group - 1) * rank
-                pieces.append(total[at : at + rank])
-            result = None
-            for turn in range(group):
-                mix = None
-                for j in range(group):
-                    rl = (j + turn) % group
-                    part = pieces[j][rl * high : (rl + 1) * high]
-                    mix = part if mix is None else jnp.where(wide_lane == j, part, mix)
-                if turn:
-                    mix = pltpu.roll(mix, turn * rank, 1)
-                result = mix if result is None else result + mix
-            o = 3 * k + dt + 1
-            out[o * high : (o + 1) * high, :] = result
-
-
-def bands_kernel(d, core_ref, inner_ref, outer_ref, inner_t_ref, outer_t_ref, flat):
+def bands(d, core, flat, inner, outer, across_taps):
     rank, group, lanes = d.rank, d.group, d.lanes
     high = rank // group
     for rh in range(high):
-        flat[pl.ds(rh, 27, stride=high), :] = core_ref[:, rh * lanes : (rh + 1) * lanes].astype(F32)
+        flat[pl.ds(rh, 27, stride=high), :] = core[:, rh * lanes : (rh + 1) * lanes].astype(F32)
     rows = flat[...].astype(BF)
     at = lax.broadcasted_iota(jnp.int32, (lanes, lanes), 0)
     to = lax.broadcasted_iota(jnp.int32, (lanes, lanes), 1)
@@ -319,34 +254,117 @@
             for dt in (-1, 0, 1):
                 value = jnp.where(lane == delta - dt, full[dt + 1], value)
             cache[delta] = value.astype(BF)
-
-        def put(down, across, value, inside):
-            one, two = (inner_ref, inner_t_ref) if inside else (outer_ref, outer_t_ref)
-            one[k * size + down * rank : k * size + (down + 1) * rank, across * lanes : (across + 1) * lanes] = value
-            two[down * rank : (down + 1) * rank, k * size + across * lanes : k * size + (across + 1) * lanes] = value
-
+        down0, across0 = (0, k * size) if across_taps else (k * size, 0)
         for down in range(2 * group):
             for across in range(2):
-                put(down, across, cache.get(down - across * group, zero), True)
                 value = zero
                 if down == group - 1 and across == 1:
                     value = cache[-1]
                 if down == group and across == 0:
                     value = cache[group]
-                put(down, across, value, False)
-
-
-def first_kernel(d, me, lengths, owner, x_hbm, reduce_ref, tab, xt, own_out, send, xc, xf, own, sems):
-    copies = []
-    for c in range(d.edge):
-        copies.append(pltpu.make_async_copy(x_hbm.at[:, :, c], xc.at[c], sems.at[c]))
-    for copy in copies:
-        copy.start()
+                row = slice(down0 + down * rank, down0 + (down + 1) * rank)
+                col = slice(across0 + across * lanes, across0 + (across + 1) * lanes)
+                inner[row, col] = cache.get(down - across * group, zero)
+                outer[row, col] = value
+
+
+def convolve(d, shifted, inner, outer, direction, out):
+    mul = dot if direction == 1 else dot_nt
+    half = d.tiles // 2
+    stacked = [
+        jnp.concatenate(windows(d, shifted, direction, 2 * p, 2), axis=1) for p in range(half)
+    ]
+    total = mul(jnp.concatenate(stacked, axis=0), inner[...])
+    for p in range(half):
+        for n in range(2):
+            out[2 * p + n] = total[p * d.core_rows : (p + 1) * d.core_rows, n * d.lanes : (n + 1) * d.lanes]
+    for p in range(half - 1):
+        total = mul(jnp.concatenate(windows(d, shifted, direction, 2 * p + 1, 2), axis=1), outer[...])
+        for n in range(2):
+            q = 2 * p + 1 + n
+            out[q] = out[q] + total[:, n * d.lanes : (n + 1) * d.lanes]
+
+
+def trimmed(d, value):
+    return value.reshape(d.edge, d.line, d.lanes)[:, : d.width].reshape(d.rows, d.lanes)
+
+
+def core_gradient(d, shifted, own, out):
+    lane = lax.broadcasted_iota(jnp.int32, (1, d.lanes), 1) // d.rank
+    tiles = []
+    for q in range(d.tiles):
+        value = own[q].astype(F32).reshape(d.edge, d.width, d.lanes)
+        value = jnp.concatenate([value, jnp.zeros((d.edge, d.line - d.width, d.lanes), F32)], axis=1)
+        tiles.append(value.reshape(d.core_rows, d.lanes))
+    right = []
+    zero = jnp.zeros_like(tiles[0])
+    for q in range(d.tiles):
+        after = tiles[q + 1] if q + 1 < d.tiles else zero
+        before = tiles[q - 1] if q > 0 else zero
+        mixed = jnp.where(lane == 0, after, jnp.where(lane == d.group - 1, before, 0.0))
+        right.append(jnp.concatenate([tiles[q], mixed], axis=1).astype(BF))
+    right = jnp.concatenate(right, axis=0)
+    rank, group = d.rank, d.group
+    high = rank // group
+    wide_lane = lax.broadcasted_iota(jnp.int32, (high, d.lanes), 1) // rank
+    for k in range(d.taps):
+        left = jnp.concatenate([windows(d, shifted, 1, q, 1)[k] for q in range(d.tiles)], axis=0)
+        total = dot_tn(left, right)
+        for dt in (-1, 0, 1):
+            pieces = []
+            for j in range(group):
+                if 0 <= j + dt < group:
+                    row, col = j + dt, 0
+                elif j + dt == group:
+                    row, col = 0, 1
+                else:
+                    row, col = group - 1, 1
+                pieces.append(total[row * rank : (row + 1) * rank, col * d.lanes : (col + 1) * d.lanes])
+            result = None
+            for turn in range(group):
+                mix = None
+                for j in range(group):
+                    rl = (j + turn) % group
+                    part = pieces[j][rl * high : (rl + 1) * high]
+                    mix = part if mix is None else jnp.where(wide_lane == j, part, mix)
+                if turn:
+                    mix = pltpu.roll(mix, turn * rank, 1)
+                result = mix if result is None else result + mix
+            o = 3 * k + dt + 1
+            out[o * high : (o + 1) * high, :] = result
+
+
+class Copies:
+    def __init__(self, sems, pairs):
+        self.all = [pltpu.make_async_copy(a, b, sems.at[n]) for n, (a, b) in enumerate(pairs)]
+        for one in self.all:
+            one.start()
+
+    def wait(self, *which):
+        for n in which:
+            self.all[n].wait()
+
+
+def first_kernel(
+    d, me, lengths_hbm, owner_hbm, x_hbm, reduce_hbm, tab_out, xt, own_out, send, xc, xf, own, reduce_ref, lengths, owner,
+    tab, sems,
+):
+    e = d.edge
+    copies = Copies(
+        sems,
+        [(lengths_hbm, lengths), (owner_hbm, owner)]
+        + [(x_hbm.at[:, :, c], xc.at[c]) for c in range(e)]
+        + [(reduce_hbm, reduce_ref)],
+    )
+    copies.wait(0, 1)
     make_table(d, me[0], lengths, owner, tab)
+    save = pltpu.make_async_copy(tab, tab_out, sems.at[e + 3])
+    save.start()
+    copies.wait(e + 2)
     weight = block_diag(d, permuted_rows(d, reduce_ref[...]))
     per_line = d.width * d.times
-    for c, copy in enumerate(copies):
-        copy.wait()
+    for c in range(e):
+        copies.wait(2 + c)
         xf[c * per_line : (c + 1) * per_line, :] = xc[c].reshape(per_line, d.channels).astype(F32)
     alive = alive_mask(d, tab[0])
     for q in range(d.tiles):
@@ -358,13 +376,22 @@
         own_out[q] = value
         own[q] = value.astype(F32)
     write_send(d, tab, own, send)
+    save.wait()
 
 
 def layer_one_kernel(
-    d, tab, own_in, recv, inner, outer, expand_ref, reduce_next, source, mixed, hidden, own_out, send,
-    wide, shifted, conv, own,
+    d, tab_in, own_in, recv, core_hbm, expand_hbm, reduce_hbm, source, mixed, hidden, own_out, send, around,
+    wide, shifted, conv, own, flat, inner, outer, core, expand_ref, reduce_next, tab, sems,
 ):
+    copies = Copies(
+        sems, [(tab_in, tab), (core_hbm, core), (expand_hbm, expand_ref), (reduce_hbm, reduce_next)]
+    )
+    copies.wait(0)
     fill(d, tab, own_in, recv, wide, shifted)
+    save = pltpu.make_async_copy(shifted, around, sems.at[4])
+    save.start()
+    copies.wait(1, 2, 3)
+    bands(d, core, flat, inner, outer, False)
     convolve(d, shifted, inner, outer, 1, conv)
     expand = block_diag(d, expand_ref[...])
     weight = block_diag(d, permuted_rows(d, reduce_next[...]))
@@ -382,13 +409,42 @@
         own_out[q] = value
         own[q] = value.astype(F32)
     write_send(d, tab, own, send)
+    save.wait()
+
+
+def read_labels(d, labels, plane):
+    for i in range(d.edge):
+        part = labels[:, i * d.lanes : (i + 1) * d.lanes].astype(F32)
+        plane[pl.ds(i, d.slots, stride=d.edge), :] = part
+    value = plane[...]
+    lines = [value if c == 0 else pltpu.roll(value, d.lanes - c * d.times, 1) for c in range(d.edge)]
+    return jnp.concatenate(lines, axis=0)
+
+
+def write_prob(d, chance, plane, prob):
+    total = chance[: d.width]
+    for c in range(1, d.edge):
+        total = total + pltpu.roll(chance[c * d.width : (c + 1) * d.width], c * d.times, 1)
+    plane[...] = total
+    for i in range(d.edge):
+        prob[:, i * d.lanes : (i + 1) * d.lanes] = plane[pl.ds(i, d.slots, stride=d.edge), :]
 
 
 def layer_two_kernel(
-    d, tab, own_in, recv, inner, outer, expand_ref, head_ref, source, labels, own_out, send, chance_out, g_out,
-    expand_grad, head_grad, wide, shifted, conv, own, slope, last, mixed,
+    d, tab_in, own_in, recv, core_hbm, expand_hbm, head_hbm, source, labels_hbm, own_out, send, prob, g_out,
+    expand_grad, head_grad, around, wide, shifted, conv, own, slope, last, mixed, flat, inner, outer, core,
+    expand_ref, head_ref, labels, plane, tab, sems,
 ):
+    copies = Copies(
+        sems,
+        [(tab_in, tab), (core_hbm, core), (expand_hbm, expand_ref), (head_hbm, head_ref), (labels_hbm, labels)],
+    )
+    copies.wait(0)
     fill(d, tab, own_in, recv, wide, shifted)
+    save = pltpu.make_async_copy(shifted, around, sems.at[5])
+    save.start()
+    copies.wait(1, 2, 3, 4)
+    bands(d, core, flat, inner, outer, False)
     convolve(d, shifted, inner, outer, 1, conv)
     expand = block_diag(d, expand_ref[...])
     head = head_ref[...]
@@ -408,8 +464,8 @@
     lane = lax.broadcasted_iota(jnp.int32, (d.rows, d.lanes), 1)
     live = alive_mask(d, tab[0]) & (lane < d.times)
     chance = jnp.where(live, chance, 0.0)
-    chance_out[...] = chance
-    g = jnp.where(live, chance - labels[...], 0.0)
+    write_prob(d, chance, plane, prob)
+    g = jnp.where(live, chance - read_labels(d, labels, plane), 0.0)
     coarse = g.astype(BF).astype(F32)
     pair = (coarse + pltpu.roll(g - coarse, d.times, 1)).astype(BF)
     g_out[...] = pair
@@ -436,14 +492,32 @@
     expand_grad[...] = grad_e
     head_grad[...] = jnp.concatenate([grad_h, jnp.zeros((SUB - 1, d.channels), F32)], axis=0)
     write_send(d, tab, own, send)
+    save.wait()
+
+
+def core_kernel(d, around_hbm, own, out, shifted, sems):
+    copies = Copies(sems, [(around_hbm, shifted)])
+    copies.wait(0)
+    core_gradient(d, shifted, own, out)
 
 
 def back_two_kernel(
-    d, tab, own_in, recv, inner_t, outer_t, reduce_ref, expand_ref, head_ref, source, mixed, g_in,
-    own_out, send, reduce_grad, expand_grad, shifted, wide, conv, own,
+    d, tab_in, own_in, recv, core_hbm, reduce_hbm, expand_hbm, head_hbm, source, mixed, g_in, around_hbm, core_two,
+    expand_two, head_grad, own_out, send, wide, shifted, conv, own, flat, inner, outer, core, reduce_ref, expand_ref,
+    head_ref, around, packed, tab, sems,
 ):
+    copies = Copies(
+        sems,
+        [
+            (tab_in, tab), (core_hbm, core), (reduce_hbm, reduce_ref), (expand_hbm, expand_ref),
+            (head_hbm, head_ref), (around_hbm, around),
+        ],
+    )
+    copies.wait(0)
     fill(d, tab, own_in, recv, wide, shifted)
-    convolve(d, shifted, inner_t, outer_t, -1, conv)
+    copies.wait(1, 2, 3, 4)
+    bands(d, core, flat, inner, outer, True)
+    convolve(d, shifted, inner, outer, -1, conv)
     expand = block_diag(d, expand_ref[...])
     weight = block_diag(d, permuted_rows(d, reduce_ref[...]))
     head = head_ref[...]
@@ -471,68 +545,84 @@
         own_out[q] = value
         own[q] = value.astype(F32)
         grad_e = grad_e + diag_sum(d, dot_tn(b, delta))
-    reduce_grad[...] = grad_r
-    expand_grad[...] = grad_e
+    copies.wait(5)
+    off = d.offsets
+    core_gradient(d, around, own_out, packed)
+    packed[off[1] : off[2], :] = core_two[...]
+    packed[off[2] : off[3], :] = grad_e
+    packed[off[3] : off[4], :] = grad_r
+    packed[off[4] : off[5], :] = expand_two[...]
+    packed[off[5] : off[6], :] = head_grad[...]
+    rest = d.nspace * d.share - off[6]
+    if rest:
+        packed[off[6] :, :] = jnp.zeros((rest, d.channels), F32)
     write_send(d, tab, own, send)
 
-
-def core_kernel(d, own, shifted, out):
-    core_gradient(d, own, shifted, out)
+    def put(n, carry):
+        at = pl.multiple_of(n * d.share, SUB)
+        send[n, d.block :, :] = packed[pl.ds(at, d.share), :].astype(BF)
+        return carry
+
+    lax.fori_loop(0, d.nspace, put, 0)
 
 
 def back_one_kernel(
-    d, tab, own_in, recv, inner_t, outer_t, own_first, source, core_two, expand_one, reduce_two, expand_two, head,
-    packed, wide, shifted, conv,
+    d, tab_in, own_in, recv, core_hbm, source, send, wide, shifted, conv, flat, inner, outer, core, tab, sems
 ):
+    copies = Copies(sems, [(tab_in, tab), (core_hbm, core)])
+    copies.wait(0)
     fill(d, tab, own_in, recv, wide, shifted)
-    convolve(d, shifted, inner_t, outer_t, -1, conv)
+    copies.wait(1)
+    bands(d, core, flat, inner, outer, True)
+    convolve(d, shifted, inner, outer, -1, conv)
     alive = alive_mask(d, tab[0])
     grad_r = jnp.zeros((d.rank, d.channels), F32)
     for q in range(d.tiles):
         da = jnp.where(alive, trimmed(d, conv[q]), 0.0).astype(BF)
         grad_r = grad_r + diag_sum(d, dot_tn(da, times_of(d, source, q)))
-    off = d.offsets
-    core_gradient(d, own_first, shifted, packed)
-    packed[off[1] : off[2], :] = core_two[...]
-    packed[off[2] : off[3], :] = grad_r
-    packed[off[3] : off[4], :] = expand_one[...]
-    packed[off[4] : off[5], :] = reduce_two[...]
-    packed[off[5] : off[6], :] = expand_two[...]
-    packed[off[6] : off[7], :] = head[...]
-    rest = d.nspace * d.share - off[7]
-    if rest:
-        packed[off[7] :, :] = jnp.zeros((rest, d.channels), F32)
-
-
-def sum_kernel(d, parts, out):
-    total = parts[0]
-    for n in range(1, d.nspace):
-        total = total + parts[n]
-    total = total * (1.0 / d.cells)
-    for n in range(d.nspace):
-        out[n] = total
-
-
-def unpack_kernel(d, packed, reduce_one, core_one, expand_one, reduce_two, core_two, expand_two, head):
+
+    def add(n, total):
+        return total + recv[n, d.block :, :].astype(F32)
+
+    shares = lax.fori_loop(0, d.nspace, add, jnp.zeros((d.share, d.channels), F32))
+    out = jnp.concatenate([grad_r, shares], axis=0).astype(BF)
+
+    def put(n, carry):
+        send[n] = out
+        return carry
+
+    lax.fori_loop(0, d.nspace, put, 0)
+
+
+def unpack_kernel(d, recv, reduce_one, core_one, expand_one, reduce_two, core_two, expand_two, head, packed):
     off = d.offsets
     high = d.rank // d.group
+    scale = 1.0 / d.cells
+
+    def take(n, total):
+        at = pl.multiple_of(n * d.share, SUB)
+        packed[pl.ds(at, d.share), :] = recv[n, d.rank :, :].astype(F32) * scale
+        return total + recv[n, : d.rank, :].astype(F32)
+
+    first = lax.fori_loop(0, d.nspace, take, jnp.zeros((d.rank, d.channels), F32)) * scale
     for at, core in ((off[0], core_one), (off[1], core_two)):
         for rh in range(high):
             core[:, rh * d.lanes : (rh + 1) * d.lanes] = packed[pl.ds(at + rh, 27, stride=high), :]
-    for at, ref in ((off[2], reduce_one), (off[4], reduce_two)):
+    second = packed[off[3] : off[4], :]
+    for value, ref in ((first, reduce_one), (second, reduce_two)):
         for rl in range(d.group):
-            ref[pl.ds(rl, high, stride=d.group), :] = packed[at + rl * high : at + (rl + 1) * high, :]
-    expand_one[...] = packed[off[3] : off[4], :]
-    expand_two[...] = packed[off[5] : off[6], :]
-    head[...] = packed[off[6] : off[6] + 1, :]
+            ref[pl.ds(rl, high, stride=d.group), :] = value[rl * high : (rl + 1) * high]
+    expand_one[...] = packed[off[2] : off[3], :]
+    expand_two[...] = packed[off[4] : off[5], :]
+    head[...] = packed[off[5] : off[5] + 1, :]
 
 
 VM = pl.BlockSpec(memory_space=pltpu.VMEM)
 SM = pl.BlockSpec(memory_space=pltpu.SMEM)
-HB = pl.BlockSpec(memory_space=pl.ANY)
-
-
-def call(kernel, d, name, ins, outs, scratch, operands):
+HB = pl.BlockSpec(memory_space=pltpu.HBM)
+
+
+def call(kernel, d, name, ins, outs, scratch, operands, limit=LIMIT):
     shapes = tuple(jax.ShapeDtypeStruct(s, t) for s, t, _ in outs)
     specs = tuple(m for _, _, m in outs)
     return pl.pallas_call(
@@ -542,7 +632,7 @@
         out_specs=specs,
         scratch_shapes=scratch,
         name=name,
-        compiler_params=pltpu.CompilerParams(vmem_limit_bytes=LIMIT),
+        compiler_params=pltpu.CompilerParams(vmem_limit_bytes=limit),
     )(*operands)
 
 
@@ -556,87 +646,95 @@
     d = Dims(nspace, slots, edge, times, channels, rank, run_lengths.shape[0], run_lengths.shape[1])
     me = lax.axis_index("space").astype(jnp.int32).reshape(1)
     head = head_vector.reshape(1, channels)
-    targets = labels.reshape(slots, edge, edge, times).transpose(2, 0, 1, 3).reshape(d.rows, times)
-    targets = jnp.pad(targets.astype(F32), ((0, 0), (0, d.lanes - times)))
-
     own_shape = (d.tiles, d.rows, d.lanes)
     wide_shape = (d.times, d.rows, d.channels)
-    send_shape = (nspace,) + d.block
+    send_shape = (nspace, d.block, channels)
     shifted_shape = (3, d.span, d.tiles * d.lanes)
+    size = 2 * d.lanes
+    core_shape = (27 * rank // d.group, d.lanes)
     own_f = pltpu.VMEM(own_shape, F32)
     rim = pltpu.VMEM((d.tiles, d.span + 2 * SUB, d.lanes), F32)
     shifted = pltpu.VMEM(shifted_shape, BF)
     conv = pltpu.VMEM((d.tiles, d.core_rows, d.lanes), F32)
+    flat = pltpu.VMEM(core_shape, F32)
+    down = [pltpu.VMEM((9 * size, size), BF)] * 2
+    across = [pltpu.VMEM((size, 9 * size), BF)] * 2
+    core_v = pltpu.VMEM(core_one.shape, BF)
+    factor = pltpu.VMEM((rank, channels), BF)
+    tab_s = pltpu.SMEM((d.t_size,), jnp.int32)
     small = ((rank, channels), F32, VM)
-    size = 2 * d.lanes
+
+    def sems(n):
+        return pltpu.SemaphoreType.DMA((n,))
 
     def exchange(send):
         return lax.all_to_all(send, "space", split_axis=0, concat_axis=0, tiled=True)
 
-    def bands(core, name):
-        return call(
-            bands_kernel, d, name, [VM],
-            [((9 * size, size), BF, VM)] * 2 + [((size, 9 * size), BF, VM)] * 2,
-            [pltpu.VMEM((27 * rank // d.group, d.lanes), F32)], [core],
-        )
-
     tab, xt, a1, send = call(
-        first_kernel, d, "first", [SM, SM, SM, HB, VM],
-        [((d.t_size,), jnp.int32, SM), (wide_shape, BF, VM), (own_shape, BF, VM), (send_shape, BF, VM)],
+        first_kernel, d, "first", [SM, HB, HB, HB, HB],
+        [((d.t_size,), jnp.int32, VM), (wide_shape, BF, VM), (own_shape, BF, VM), (send_shape, BF, VM)],
         [
             pltpu.VMEM((edge, slots, edge, times, channels), BF),
             pltpu.VMEM((d.rows * times, channels), F32),
-            own_f,
-            pltpu.SemaphoreType.DMA((edge,)),
+            own_f, factor, pltpu.SMEM(run_lengths.shape, jnp.int32), pltpu.SMEM(run_owner.shape, jnp.int32), tab_s,
+            sems(edge + 4),
         ],
         [me, run_lengths, run_owner, volume, reduce_one],
     )
-    inner1, outer1, inner1t, outer1t = bands(core_one, "bands_one")
-    inner2, outer2, inner2t, outer2t = bands(core_two, "bands_two")
     recv = exchange(send)
-    b1, h1, a2, send = call(
-        layer_one_kernel, d, "layer_one", [SM] + [VM] * 7,
-        [(own_shape, BF, VM), (wide_shape, BF, VM), (own_shape, BF, VM), (send_shape, BF, VM)],
-        [rim, shifted, conv, own_f],
-        [tab, a1, recv, inner1, outer1, expand_one, reduce_two, xt],
+    b1, h1, a2, send, around1 = call(
+        layer_one_kernel, d, "layer_one", [VM, VM, VM, HB, HB, HB, VM],
+        [
+            (own_shape, BF, VM), (wide_shape, BF, VM), (own_shape, BF, VM), (send_shape, BF, VM),
+            (shifted_shape, BF, HB),
+        ],
+        [rim, shifted, conv, own_f, flat] + down + [core_v, factor, factor, tab_s, sems(5)],
+        [tab, a1, recv, core_one, expand_one, reduce_two, xt],
     )
     recv = exchange(send)
-    db2, send, chance, g, eg2, hg = call(
-        layer_two_kernel, d, "layer_two", [SM] + [VM] * 8,
+    db2, send, prob, g, eg2, hg, around2 = call(
+        layer_two_kernel, d, "layer_two", [VM, VM, VM, HB, HB, HB, VM, HB],
         [
-            (own_shape, BF, VM), (send_shape, BF, VM), ((d.rows, d.lanes), F32, VM), ((d.rows, d.lanes), BF, VM),
-            small, ((SUB, channels), F32, VM),
+            (own_shape, BF, VM), (send_shape, BF, VM), (labels.shape, F32, VM), ((d.rows, d.lanes), BF, VM),
+            small, ((SUB, channels), F32, VM), (shifted_shape, BF, HB),
         ],
-        [rim, shifted, conv, own_f, pltpu.VMEM(wide_shape, F32), pltpu.VMEM(wide_shape, BF), pltpu.VMEM(own_shape, BF)],
-        [tab, a2, recv, inner2, outer2, expand_two, head, h1, targets],
+        [
+            rim, shifted, conv, own_f, pltpu.VMEM(wide_shape, F32), pltpu.VMEM(wide_shape, BF),
+            pltpu.VMEM(own_shape, BF), flat,
+        ]
+        + down
+        + [core_v, factor, pltpu.VMEM((1, channels), BF), pltpu.VMEM(labels.shape, jnp.int32), pltpu.VMEM((d.width, d.lanes), F32), tab_s, sems(6)],
+        [tab, a2, recv, core_two, expand_two, head, h1, labels],
     )
     recv = exchange(send)
-    db1, send, rg2, eg1, around = call(
-        back_two_kernel, d, "back_two", [SM] + [VM] * 10,
-        [(own_shape, BF, VM), (send_shape, BF, VM), small, small, (shifted_shape, BF, VM)],
-        [rim, conv, own_f],
-        [tab, db2, recv, inner2t, outer2t, reduce_two, expand_one, head, h1, b1, g],
-    )
-    core_shape = (27 * rank // d.group, d.lanes)
-    (cg2,) = call(core_kernel, d, "core_two", [VM] * 2, [(core_shape, F32, VM)], [], [a2, around])
+    (cg2,) = call(
+        core_kernel, d, "core_two", [HB, VM], [(core_shape, F32, VM)], [shifted, sems(1)], [around2, db2]
+    )
+    db1, send = call(
+        back_two_kernel, d, "back_two", [VM, VM, VM, HB, HB, HB, HB, VM, VM, VM, HB, VM, VM, VM],
+        [(own_shape, BF, VM), ((nspace, d.block + d.share, channels), BF, VM)],
+        [rim, shifted, conv, own_f, flat]
+        + across
+        + [
+            core_v, factor, factor, pltpu.VMEM((1, channels), BF), shifted,
+            pltpu.VMEM((nspace * d.share, channels), F32), tab_s, sems(6),
+        ],
+        [tab, db2, recv, core_two, reduce_two, expand_one, head, h1, b1, g, around1, cg2, eg2, hg],
+    )
     recv = exchange(send)
-    (packed,) = call(
-        back_one_kernel, d, "back_one", [SM] + [VM] * 11,
-        [((nspace * d.share, channels), F32, VM)],
-        [rim, shifted, conv],
-        [tab, db1, recv, inner1t, outer1t, a1, xt, cg2, eg1, rg2, eg2, hg],
-    )
-    parts = exchange(packed.reshape(nspace, d.share, channels))
-    (sums,) = call(
-        sum_kernel, d, "sum_parts", [VM], [((nspace, d.share, channels), F32, VM)], [], [parts]
-    )
-    whole = exchange(sums).reshape(nspace * d.share, channels)
+    (send,) = call(
+        back_one_kernel, d, "back_one", [VM, VM, VM, HB, VM],
+        [((nspace, rank + d.share, channels), BF, VM)],
+        [rim, shifted, conv, flat] + across + [core_v, tab_s, sems(2)],
+        [tab, db1, recv, core_one, xt],
+    )
+    recv = exchange(send)
     core_out = ((27, rank * rank), F32, VM)
     r1, c1, e1, r2, c2, e2, hv = call(
         unpack_kernel, d, "unpack", [VM],
-        [small, core_out, small, small, core_out, small, ((1, channels), F32, VM)], [], [whole],
-    )
-    prob = chance[:, :times].reshape(edge, slots, edge, times).transpose(1, 2, 0, 3).reshape(slots, -1)
+        [small, core_out, small, small, core_out, small, ((1, channels), F32, VM)],
+        [pltpu.VMEM((nspace * d.share, channels), F32)], [recv],
+    )
     return prob, r1, c1, e1, r2, c2, e2, hv.reshape(channels)
 
 

time: 134 us -> 113 us (0.84)
  blocking collectives: 30.4 us -> 68.3 us
  local copies, waits for them, and re-layouts: 28.5 us -> 5.97 us
  waiting for transfers between devices: 29.8 us -> 10.7 us
  starting transfers between devices: 18.4 us -> 3.74 us
    all_to_all x2 -> x4, blocking collectives: 30.4 us -> 68.3 us  [exchange(): lax.all_to_all(send, 'space', split_axis=0, concat_axis=0, tiled=True)]
    all_to_all x4 -> x1, waiting for transfers between devices: 29.8 us -> 10.7 us  [exchange(): lax.all_to_all(send, 'space', split_axis=0, concat_axis=0, tiled=True)]
    unnamed x80 -> x30, local copies, waits for them, and re-layouts: 24.8 us -> 5.97 us
    all_to_all x4 -> x1, starting transfers between devices: 18.4 us -> 3.74 us  [exchange(): lax.all_to_all(send, 'space', split_axis=0, concat_axis=0, tiled=True)]
    convert_element_type x2 -> x0, local copies, waits for them, and re-layouts: 2.37 us -> none  [on_device(): targets = jnp.pad(targets.astype(F32), ((0, 0), (0, d.lanes - times)))]
    pallas_call x10 -> x7, Pallas kernels: 23.2 us -> 22.6 us  [call(): pl.pallas_call(functools.partial(kernel, d), out_shape=shapes, in_specs=l...]
  transfers between devices with their start and end apart: 4 -> 1, of which waited for: 4 -> 1; matrix products, arithmetic and copies ran while one was open for 4% -> 0% of each run, Pallas kernels for 2% -> 1%
where the time goes in v2:
time: 113 us; the launch traced here: 112 us
  blocking collectives  68.3 us (60%)
  Pallas kernels  22.6 us (20%)
  waiting for transfers between devices  10.7 us (9%)
  local copies, waits for them, and re-layouts  5.97 us (5%)
  starting transfers between devices  3.74 us (3%)
    all_to_all x4, blocking collectives, exchange(): lax.all_to_all(send, 'space', split_axis=0, concat_axis=0, tiled=True)  68.3 us
    pallas_call x7, Pallas kernels, call(): pl.pallas_call(functools.partial(kernel, d), out_shape=shapes, in_specs=l...  22.6 us
    all_to_all x1, waiting for transfers between devices, exchange(): lax.all_to_all(send, 'space', split_axis=0, concat_axis=0, tiled=True)  10.7 us
    unnamed x30, local copies, waits for them, and re-layouts  5.97 us
    all_to_all x1, starting transfers between devices, exchange(): lax.all_to_all(send, 'space', split_axis=0, concat_axis=0, tiled=True)  3.74 us
  transfers between devices with their start and end apart: 1, of which 1 were waited for; matrix products, arithmetic and copies ran while one was open for 0% of the time, Pallas kernels for 1%

profile of v2, /device:TPU:0, one launch (start us, length us, event | category | flops | bytes accessed | tf_op | source)
XLA Modules:
  0.0 112.1 jit_solution(9825875899881864189)
XLA Ops:
  0.6 0.0 copy-start.13
  0.6 0.0 copy-start.14
  0.7 0.7 copy-done.13
  1.3 0.0 copy-done.14
  1.3 0.0 copy-start.2
  1.3 1.1 %copy-done.2 = bf16[3,8,8,16,128]{4,3,2,1,0:T(8,128)(2,1)S(1)} copy-done((bf16[3,8,8,16,128]{4,3,2,1,0:T(8,128)(2,1)S(1)}, bf16[3,8,8,16,128]{4,3,2,1,0:T(8,128)(2,1)}, u32[]{:S(2)}) %copy-start.2) | copy-done | bytes 786456
  2.5 0.0 copy-start.10
  2.5 0.7 copy-done.10
  3.2 2.0 %first.1 = (s32[45]{0:T(128)S(1)}, bf16[16,192,128]{2,1,0:T(8,128)(2,1)S(1)}, bf16[4,192,128]{2,1,0:T(8,128)(2,1)S(1)}, bf16[16,96,128]{2,1,0:T(8,128)(2,1)S(1)}) custom-call(s32[1]{0:T(128)} %bitcast.me, s32[2,4]{1,0:T(2,128)S(1)} %copy-done.13, s32[16]{0:T(128)S(1)} %copy-done.14, bf16[3,8,8,16,128]{4,3,2,1,0:T(8,128)(2,1)S(1)} %copy-done.2, ...), custom_call_target="tpu_custom_call" | custom-call | tf_op jit(solution)/shard_map/first/pallas_call | solution.py:628
  5.2 0.0 copy-start.4
  5.2 0.0 copy-start.7
  5.2 0.0 copy-start.8
  5.2 19.5 %all_to_all.25.recv = bf16[16,96,128]{2,1,0:T(8,128)(2,1)S(1)} all-to-all(bf16[16,96,128]{2,1,0:T(8,128)(2,1)S(1)} %get-tuple-element.35), channel_id=1, replica_groups=mesh['groups'=2,'space'=16] {'space'}, dimensions={0} | all-to-all | bytes 786432 | tf_op jit(solution)/shard_map/all_to_all | solution.py:671
  24.7 0.0 copy-done.4
  24.7 0.0 copy-done.7
  24.7 0.0 copy-done.8
  24.7 3.9 %layer_one.1 = (bf16[4,192,128]{2,1,0:T(8,128)(2,1)S(1)}, bf16[16,192,128]{2,1,0:T(8,128)(2,1)S(1)}, bf16[4,192,128]{2,1,0:T(8,128)(2,1)S(1)}, bf16[16,96,128]{2,1,0:T(8,128)(2,1)S(1)}, bf16[3,320,512]{2,1,0:T(8,128)(2,1)S(1)}) custom-call(s32[45]{0:T(128)S(1)} %get-tuple-element.33.tab_in, bf16[4,192,128]{2,1,0:T(8,128)(2,1)S(1)} %get-tuple-element.34.own_in, ...), custom_call_target="tpu_custom_call" | custom-call | tf_op jit(solution)/shard_map/layer_one/pallas_call | solution.py:628
  28.6 0.0 copy-start.5
  28.6 0.7 copy-done.5
  29.3 0.0 copy-start
  29.3 0.0 copy-start.3
  29.3 0.0 copy-start.9
  29.3 0.0 copy-start.11
  29.3 15.5 %all_to_all.26.recv = bf16[16,96,128]{2,1,0:T(8,128)(2,1)S(1)} all-to-all(bf16[16,96,128]{2,1,0:T(8,128)(2,1)S(1)} %get-tuple-element.38), channel_id=1, replica_groups=mesh['groups'=2,'space'=16] {'space'}, dimensions={0} | all-to-all | bytes 786432 | tf_op jit(solution)/shard_map/all_to_all | solution.py:671
  44.9 0.0 copy-start.12
  44.9 0.0 copy-done.3
  44.9 0.0 copy-done.9
  44.9 0.0 copy-done.11
  44.9 0.6 copy-done.12
  45.5 6.2 %layer_two.1 = (bf16[4,192,128]{2,1,0:T(8,128)(2,1)S(1)}, bf16[16,96,128]{2,1,0:T(8,128)(2,1)}, f32[3,1024]{1,0:T(4,128)}, bf16[192,128]{1,0:T(8,128)(2,1)S(1)},...) custom-call(s32[45]{0:T(128)S(1)} %get-tuple-element.33.tab_in, ...), custom_call_target="tpu_custom_call" | custom-call | tf_op jit(solution)/shard_map/layer_two/pallas_call | solution.py:628
  51.7 0.0 copy-done
  51.7 3.7 %all-to-all-start.2 = ((bf16[16,96,128]{2,1,0:T(8,128)(2,1)}), bf16[16,96,128]{2,1,0:T(8,128)(2,1)S(1)}, u32[]{:S(2)}, u32[]{:S(2)}) async-start(bf16[16,96,128]{2,1,0:T(8,128)(2,1)} %get-tuple-element.42), calls=%async_computation.2 | async-start | bytes 786432 | tf_op jit(solution)/shard_map/all_to_all | solution.py:671
  55.5 1.2 %core_two.1 = f32[216,128]{1,0:T(8,128)S(1)} custom-call(bf16[3,320,512]{2,1,0:T(8,128)(2,1)S(1)} %get-tuple-element.46.around_hbm, bf16[4,192,128]{2,1,0:T(8,128)(2,1)S(1)} %get-tuple-element.41.own.own_in), custom_call_target="tpu_custom_call" | custom-call | tf_op jit(solution)/shard_map/core_two/pallas_call | solution.py:628
  56.7 10.7 %all-to-all-done.2.recv = bf16[16,96,128]{2,1,0:T(8,128)(2,1)S(1)} async-done(((bf16[16,96,128]{2,1,0:T(8,128)(2,1)}), bf16[16,96,128]{2,1,0:T(8,128)(2,1)S(1)}, u32[]{:S(2)}, u32[]{:S(2)}) %all-to-all-start.2) | async-done | bytes 393248 | tf_op jit(solution)/shard_map/all_to_all | solution.py:671
  67.4 0.0 copy-start.1
  67.4 1.2 %copy-done.1 = bf16[3,320,512]{2,1,0:T(8,128)(2,1)S(1)} copy-done((bf16[3,320,512]{2,1,0:T(8,128)(2,1)S(1)}, bf16[3,320,512]{2,1,0:T(8,128)(2,1)}, u32[]{:S(2)}) %copy-start.1) | copy-done | bytes 983064
  68.6 0.0 copy-start.6
  68.6 0.9 copy-done.6
  69.6 5.5 %back_two.1 = (bf16[4,192,128]{2,1,0:T(8,128)(2,1)S(1)}, bf16[16,136,128]{2,1,0:T(8,128)(2,1)S(1)}) custom-call(s32[45]{0:T(128)S(1)} %get-tuple-element.33.tab_in, bf16[4,192,128]{2,1,0:T(8,128)(2,1)S(1)} %get-tuple-element.41.own.own_in, bf16[16,96,128]{2,1,0:T(8,128)(2,1)S(1)} %all-to-all-done.2.recv, bf16[27,1024]{1,0:T(8,128)(2,1)S(1)} %copy-done.3, ...), custom_call_target="tpu_custom_call" | custom-call | tf_op jit(solution)/shard_map/back_two/pallas_call | solution.py:628
  75.0 19.9 %all_to_all.27.recv = bf16[16,136,128]{2,1,0:T(8,128)(2,1)S(1)} all-to-all(bf16[16,136,128]{2,1,0:T(8,128)(2,1)S(1)} %get-tuple-element.50), channel_id=1, replica_groups=mesh['groups'=2,'space'=16] {'space'}, dimensions={0} | all-to-all | bytes 1114112 | tf_op jit(solution)/shard_map/all_to_all | solution.py:671
  95.0 3.0 %back_one.1 = bf16[16,72,128]{2,1,0:T(8,128)(2,1)S(1)} custom-call(s32[45]{0:T(128)S(1)} %get-tuple-element.33.tab_in, bf16[4,192,128]{2,1,0:T(8,128)(2,1)S(1)} %get-tuple-element.49.own_in, bf16[16,136,128]{2,1,0:T(8,128)(2,1)S(1)} %all_to_all.27.recv, bf16[27,1024]{1,0:T(8,128)(2,1)S(1)} %copy-done.4, bf16[16,192,128]{2,1,0:T(8,128)(2,1)S(1)} %get-tuple-element.36.source), custom_call_target="tpu_custom_call" | custom-call | tf_op jit(solution)/shard_map/back_one/pallas_call | solution.py:628
  97.9 13.3 %all_to_all.28.recv = bf16[16,72,128]{2,1,0:T(8,128)(2,1)S(1)} all-to-all(bf16[16,72,128]{2,1,0:T(8,128)(2,1)S(1)} %back_one.1), channel_id=1, replica_groups=mesh['groups'=2,'space'=16] {'space'}, dimensions={0} | all-to-all | bytes 589824 | tf_op jit(solution)/shard_map/all_to_all | solution.py:671
  111.2 0.9 unpack.1
Async XLA Ops:
  0.6 0.7 copy-start.13
  0.6 0.7 copy-start.14
  1.3 1.1 %copy-start.2 = (bf16[3,8,8,16,128]{4,3,2,1,0:T(8,128)(2,1)S(1)}, bf16[3,8,8,16,128]{4,3,2,1,0:T(8,128)(2,1)}, u32[]{:S(2)}) copy-start(bf16[3,8,8,16,128]{4,3,2,1,0:T(8,128)(2,1)} %x_hbm.1) | copy-start | bytes 2359300
  2.5 0.7 copy-start.10
  5.2 19.6 %copy-start.4 = (bf16[27,1024]{1,0:T(8,128)(2,1)S(1)}, bf16[27,1024]{1,0:T(8,128)(2,1)}, u32[]{:S(2)}) copy-start(bf16[27,1024]{1,0:T(8,128)(2,1)} %core_hbm.7) | copy-start | bytes 165892
  5.2 19.5 %copy-start.7 = (bf16[32,128]{1,0:T(8,128)(2,1)S(1)}, bf16[32,128]{1,0:T(8,128)(2,1)}, u32[]{:S(2)}) copy-start(bf16[32,128]{1,0:T(8,128)(2,1)} %expand_hbm.5) | copy-start | bytes 24580
  5.2 19.5 %copy-start.8 = (bf16[32,128]{1,0:T(8,128)(2,1)S(1)}, bf16[32,128]{1,0:T(8,128)(2,1)}, u32[]{:S(2)}) copy-start(bf16[32,128]{1,0:T(8,128)(2,1)} %reduce_hbm.5) | copy-start | bytes 24580
  28.6 0.7 copy-start.5
  29.3 22.4 %copy-start = (bf16[3,320,512]{2,1,0:T(8,128)(2,1)}, bf16[3,320,512]{2,1,0:T(8,128)(2,1)S(1)}, u32[]{:S(2)}) copy-start(bf16[3,320,512]{2,1,0:T(8,128)(2,1)S(1)} %get-tuple-element.45.around_hbm) | copy-start | bytes 2949124
  29.3 15.5 %copy-start.3 = (bf16[27,1024]{1,0:T(8,128)(2,1)S(1)}, bf16[27,1024]{1,0:T(8,128)(2,1)}, u32[]{:S(2)}) copy-start(bf16[27,1024]{1,0:T(8,128)(2,1)} %core_hbm.6) | copy-start | bytes 165892
  29.3 15.5 %copy-start.9 = (s32[3,1024]{1,0:T(4,128)S(1)}, s32[3,1024]{1,0:T(4,128)}, u32[]{:S(2)}) copy-start(s32[3,1024]{1,0:T(4,128)} %labels_hbm.1) | copy-start | bytes 36868
  29.3 15.5 %copy-start.11 = (bf16[32,128]{1,0:T(8,128)(2,1)S(1)}, bf16[32,128]{1,0:T(8,128)(2,1)}, u32[]{:S(2)}) copy-start(bf16[32,128]{1,0:T(8,128)(2,1)} %expand_hbm.4) | copy-start | bytes 24580
  44.9 0.7 copy-start.12
  51.7 15.7 %all-to-all-start.2 = ((bf16[16,96,128]{2,1,0:T(8,128)(2,1)}), bf16[16,96,128]{2,1,0:T(8,128)(2,1)S(1)}, u32[]{:S(2)}, u32[]{:S(2)}) async-start(bf16[16,96,128]{2,1,0:T(8,128)(2,1)} %get-tuple-element.42), calls=%async_computation.2 | async-start | bytes 786432 | tf_op jit(solution)/shard_map/all_to_all | solution.py:671
  67.4 1.2 %copy-start.1 = (bf16[3,320,512]{2,1,0:T(8,128)(2,1)S(1)}, bf16[3,320,512]{2,1,0:T(8,128)(2,1)}, u32[]{:S(2)}) copy-start(bf16[3,320,512]{2,1,0:T(8,128)(2,1)} %copy-done) | copy-start | bytes 2949124
  68.6 0.9 copy-start.6

commit v3 on v2

--- a/solution.py
+++ b/solution.py
@@ -25,7 +25,6 @@
         self.line = self.width + SUB
         self.lines = edge + 2
         self.span = self.lines * self.line
-        self.core_rows = edge * self.line
         self.cells = edge * edge * times
         self.taps = 9
         self.t_send = 5
@@ -51,8 +50,16 @@
     return lax.dot_general(a, b, (((0,), (0,)), ((), ())), preferred_element_type=F32)
 
 
-def sigmoid(v):
-    return 0.5 * jnp.tanh(0.5 * v) + 0.5
+def halved(w):
+    return (w.astype(F32) * 0.5).astype(BF)
+
+
+def silu(u):
+    return u + u * jnp.tanh(u)
+
+
+def slope_twice(u, th):
+    return (1.0 + th) * (1.0 + u * (1.0 - th))
 
 
 def block_diag(d, w):
@@ -174,10 +181,14 @@
             send[tab[to], : d.part, :] = end
 
 
-def fill(d, tab, own, recv, wide, shifted):
+def fill(d, tab, own, recv, wide, even, odd):
     length = tab[0]
     for q in range(d.tiles):
-        wide[q] = jnp.zeros((d.span + 2 * SUB, d.lanes), F32)
+        zero = jnp.zeros((SUB, d.lanes), F32)
+        wide[q, :SUB, :] = zero
+        for n in range(d.lines):
+            at = SUB + d.line * n + d.width
+            wide[q, at : at + SUB, :] = zero
         value = own[q].astype(F32)
         for c in range(d.edge):
             at = SUB + d.line * (c + 1)
@@ -208,25 +219,30 @@
                     wide[q, at + s * SUB : (at + s * SUB) + SUB, :] = jnp.where((sub == 0) | (s < length), part, 0.0)
     for di in (-1, 0, 1):
         for q in range(d.tiles):
-            shifted[di + 1, :, q * d.lanes : (q + 1) * d.lanes] = wide[
-                q, SUB + di : SUB + di + d.span, :
-            ].astype(BF)
-
-
-def windows(d, shifted, direction, first, count):
+            lines = [
+                wide[q, SUB + d.line * n + di : SUB + d.line * n + di + d.width, :] for n in range(d.lines)
+            ]
+            at = slice(q * d.lanes, (q + 1) * d.lanes)
+            even[di + 1, :, at] = jnp.concatenate(lines, axis=0).astype(BF)
+            odd[di + 1, :, at] = jnp.concatenate(lines[1:-1], axis=0).astype(BF)
+
+
+def windows(d, views, direction, first, count):
+    even, odd = views
     parts = []
     for di in (-1, 0, 1):
         for dc in (-1, 0, 1):
-            at = d.line * (1 + direction * dc)
-            parts.append(
-                shifted[
-                    1 + direction * di, at : at + d.core_rows, first * d.lanes : (first + count) * d.lanes
-                ]
-            )
+            col = slice(first * d.lanes, (first + count) * d.lanes)
+            n = 1 + direction * di
+            if dc == 0:
+                parts.append(odd[n, :, col])
+            else:
+                at = d.width * (1 + direction * dc)
+                parts.append(even[n, at : at + d.rows, col])
     return parts
 
 
-def bands(d, core, flat, inner, outer, across_taps):
+def bands(d, core, flat, inner, outer, inner_t, outer_t):
     rank, group, lanes = d.rank, d.group, d.lanes
     high = rank // group
     for rh in range(high):
@@ -254,48 +270,44 @@
             for dt in (-1, 0, 1):
                 value = jnp.where(lane == delta - dt, full[dt + 1], value)
             cache[delta] = value.astype(BF)
-        down0, across0 = (0, k * size) if across_taps else (k * size, 0)
         for down in range(2 * group):
+            row = slice(down * rank, (down + 1) * rank)
             for across in range(2):
-                value = zero
-                if down == group - 1 and across == 1:
-                    value = cache[-1]
-                if down == group and across == 0:
-                    value = cache[group]
-                row = slice(down0 + down * rank, down0 + (down + 1) * rank)
-                col = slice(across0 + across * lanes, across0 + (across + 1) * lanes)
-                inner[row, col] = cache.get(down - across * group, zero)
-                outer[row, col] = value
-
-
-def convolve(d, shifted, inner, outer, direction, out):
+                value = cache.get(down - across * group, zero)
+                inner[k * size + down * rank : k * size + (down + 1) * rank, across * lanes : (across + 1) * lanes] = value
+                inner_t[row, k * size + across * lanes : k * size + (across + 1) * lanes] = value
+            far = cache[-1] if down == group - 1 else cache[group] if down == group else zero
+            outer_t[row, k * lanes : (k + 1) * lanes] = far
+        for down in range(group):
+            row = slice(k * lanes + down * rank, k * lanes + (down + 1) * rank)
+            outer[row, :lanes] = cache[group] if down == 0 else zero
+            outer[row, lanes:] = cache[-1] if down == group - 1 else zero
+
+
+def convolve(d, views, inner, outer, direction, out):
     mul = dot if direction == 1 else dot_nt
     half = d.tiles // 2
     stacked = [
-        jnp.concatenate(windows(d, shifted, direction, 2 * p, 2), axis=1) for p in range(half)
+        jnp.concatenate(windows(d, views, direction, 2 * p, 2), axis=1) for p in range(half)
     ]
     total = mul(jnp.concatenate(stacked, axis=0), inner[...])
     for p in range(half):
         for n in range(2):
-            out[2 * p + n] = total[p * d.core_rows : (p + 1) * d.core_rows, n * d.lanes : (n + 1) * d.lanes]
+            out[2 * p + n] = total[p * d.rows : (p + 1) * d.rows, n * d.lanes : (n + 1) * d.lanes]
+    lane = lax.broadcasted_iota(jnp.int32, (d.rows, d.lanes), 1) // d.rank
     for p in range(half - 1):
-        total = mul(jnp.concatenate(windows(d, shifted, direction, 2 * p + 1, 2), axis=1), outer[...])
+        before = windows(d, views, direction, 2 * p + 1, 1)
+        after = windows(d, views, direction, 2 * p + 2, 1)
+        mixed = [jnp.where(lane == d.group - 1, x, y) for x, y in zip(before, after)]
+        total = mul(jnp.concatenate(mixed, axis=1), outer[...])
         for n in range(2):
             q = 2 * p + 1 + n
             out[q] = out[q] + total[:, n * d.lanes : (n + 1) * d.lanes]
 
 
-def trimmed(d, value):
-    return value.reshape(d.edge, d.line, d.lanes)[:, : d.width].reshape(d.rows, d.lanes)
-
-
-def core_gradient(d, shifted, own, out):
+def core_gradient(d, views, own, out):
     lane = lax.broadcasted_iota(jnp.int32, (1, d.lanes), 1) // d.rank
-    tiles = []
-    for q in range(d.tiles):
-        value = own[q].astype(F32).reshape(d.edge, d.width, d.lanes)
-        value = jnp.concatenate([value, jnp.zeros((d.edge, d.line - d.width, d.lanes), F32)], axis=1)
-        tiles.append(value.reshape(d.core_rows, d.lanes))
+    tiles = [own[q].astype(F32) for q in range(d.tiles)]
     right = []
     zero = jnp.zeros_like(tiles[0])
     for q in range(d.tiles):
@@ -308,7 +320,7 @@
     high = rank // group
     wide_lane = lax.broadcasted_iota(jnp.int32, (high, d.lanes), 1) // rank
     for k in range(d.taps):
-        left = jnp.concatenate([windows(d, shifted, 1, q, 1)[k] for q in range(d.tiles)], axis=0)
+        left = jnp.concatenate([windows(d, views, 1, q, 1)[k] for q in range(d.tiles)], axis=0)
         total = dot_tn(left, right)
         for dt in (-1, 0, 1):
             pieces = []
@@ -345,26 +357,35 @@
             self.all[n].wait()
 
 
+def start_kernel(d, me, token):
+    token[...] = jnp.zeros((SUB, d.lanes), F32) + me[0].astype(F32)
+
+
 def first_kernel(
-    d, me, lengths_hbm, owner_hbm, x_hbm, reduce_hbm, tab_out, xt, own_out, send, xc, xf, own, reduce_ref, lengths, owner,
-    tab, sems,
+    d, me, lengths_hbm, owner_hbm, x_hbm, reduce_hbm, core_one_hbm, core_two_hbm, token, *refs
 ):
-    e = d.edge
+    del token
+    tab_out, xt, own_out, send = refs[:4]
+    band_refs = refs[4:12]
+    xc, xf, own, lengths, owner, reduce_ref, core_one, core_two, flat, tab, sems = refs[12:]
     copies = Copies(
         sems,
-        [(lengths_hbm, lengths), (owner_hbm, owner)]
-        + [(x_hbm.at[:, :, c], xc.at[c]) for c in range(e)]
-        + [(reduce_hbm, reduce_ref)],
+        [
+            (lengths_hbm, lengths), (owner_hbm, owner), (reduce_hbm, reduce_ref), (core_one_hbm, core_one),
+            (core_two_hbm, core_two),
+        ]
+        + [(x_hbm.at[:, :, c], xc.at[c]) for c in range(d.edge)],
     )
-    copies.wait(0, 1)
+    copies.wait(0, 1, 2, 3, 4)
     make_table(d, me[0], lengths, owner, tab)
-    save = pltpu.make_async_copy(tab, tab_out, sems.at[e + 3])
+    weight = block_diag(d, permuted_rows(d, reduce_ref[...]))
+    bands(d, core_one, flat, *band_refs[0:4])
+    bands(d, core_two, flat, *band_refs[4:8])
+    save = pltpu.make_async_copy(tab, tab_out, sems.at[d.edge + 5])
     save.start()
-    copies.wait(e + 2)
-    weight = block_diag(d, permuted_rows(d, reduce_ref[...]))
     per_line = d.width * d.times
-    for c in range(e):
-        copies.wait(2 + c)
+    for c in range(d.edge):
+        copies.wait(5 + c)
         xf[c * per_line : (c + 1) * per_line, :] = xc[c].reshape(per_line, d.channels).astype(F32)
     alive = alive_mask(d, tab[0])
     for q in range(d.tiles):
@@ -380,36 +401,29 @@
 
 
 def layer_one_kernel(
-    d, tab_in, own_in, recv, core_hbm, expand_hbm, reduce_hbm, source, mixed, hidden, own_out, send, around,
-    wide, shifted, conv, own, flat, inner, outer, core, expand_ref, reduce_next, tab, sems,
+    d, tab_in, own_in, recv, inner, outer, expand_ref, reduce_next, source, mixed, hidden, own_out, send, even, odd,
+    wide, conv, own, tab, sems,
 ):
-    copies = Copies(
-        sems, [(tab_in, tab), (core_hbm, core), (expand_hbm, expand_ref), (reduce_hbm, reduce_next)]
-    )
-    copies.wait(0)
-    fill(d, tab, own_in, recv, wide, shifted)
-    save = pltpu.make_async_copy(shifted, around, sems.at[4])
-    save.start()
-    copies.wait(1, 2, 3)
-    bands(d, core, flat, inner, outer, False)
-    convolve(d, shifted, inner, outer, 1, conv)
+    Copies(sems, [(tab_in, tab)]).wait(0)
+    fill(d, tab, own_in, recv, wide, even, odd)
+    convolve(d, (even, odd), inner, outer, 1, conv)
     expand = block_diag(d, expand_ref[...])
+    half = halved(expand)
     weight = block_diag(d, permuted_rows(d, reduce_next[...]))
     alive = alive_mask(d, tab[0])
     for q in range(d.tiles):
-        b = trimmed(d, conv[q]).astype(BF)
+        b = conv[q].astype(BF)
         mixed[q] = b
-        y = dot(b, expand)
+        y = dot(b, half)
         for j in range(d.group):
             t = q * d.group + j
-            v = y[:, j * d.channels : (j + 1) * d.channels]
-            hidden[t] = (source[t].astype(F32) + v * sigmoid(v)).astype(BF)
+            u = y[:, j * d.channels : (j + 1) * d.channels]
+            hidden[t] = (source[t].astype(F32) + silu(u)).astype(BF)
         value = dot_nt(times_of(d, hidden, q), weight)
         value = jnp.where(alive, value, 0.0).astype(BF)
         own_out[q] = value
         own[q] = value.astype(F32)
     write_send(d, tab, own, send)
-    save.wait()
 
 
 def read_labels(d, labels, plane):
@@ -431,34 +445,26 @@
 
 
 def layer_two_kernel(
-    d, tab_in, own_in, recv, core_hbm, expand_hbm, head_hbm, source, labels_hbm, own_out, send, prob, g_out,
-    expand_grad, head_grad, around, wide, shifted, conv, own, slope, last, mixed, flat, inner, outer, core,
-    expand_ref, head_ref, labels, plane, tab, sems,
+    d, tab_in, own_in, recv, inner, outer, expand_ref, head_ref, source, labels, own_out, send, prob, g_out,
+    expand_grad, head_grad, core_grad, wide, even, odd, conv, own, slope, last, mixed, plane, tab, sems,
 ):
-    copies = Copies(
-        sems,
-        [(tab_in, tab), (core_hbm, core), (expand_hbm, expand_ref), (head_hbm, head_ref), (labels_hbm, labels)],
-    )
-    copies.wait(0)
-    fill(d, tab, own_in, recv, wide, shifted)
-    save = pltpu.make_async_copy(shifted, around, sems.at[5])
-    save.start()
-    copies.wait(1, 2, 3, 4)
-    bands(d, core, flat, inner, outer, False)
-    convolve(d, shifted, inner, outer, 1, conv)
+    Copies(sems, [(tab_in, tab)]).wait(0)
+    fill(d, tab, own_in, recv, wide, even, odd)
+    convolve(d, (even, odd), inner, outer, 1, conv)
     expand = block_diag(d, expand_ref[...])
+    half = halved(expand)
     head = head_ref[...]
     logit = jnp.zeros((d.rows, d.lanes), F32)
     for q in range(d.tiles):
-        b = trimmed(d, conv[q]).astype(BF)
+        b = conv[q].astype(BF)
         mixed[q] = b
-        y = dot(b, expand)
+        y = dot(b, half)
         for j in range(d.group):
             t = q * d.group + j
-            v = y[:, j * d.channels : (j + 1) * d.channels]
-            s = sigmoid(v)
-            slope[t] = s * (1.0 + v * (1.0 - s))
-            last[t] = (source[t].astype(F32) + v * s).astype(BF)
+            u = y[:, j * d.channels : (j + 1) * d.channels]
+            th = jnp.tanh(u)
+            slope[t] = slope_twice(u, th)
+            last[t] = (source[t].astype(F32) + (u + u * th)).astype(BF)
         logit = logit + dot_nt(times_of(d, last, q), head_rows(d, head, q, False))
     chance = jax.nn.sigmoid(logit)
     lane = lax.broadcasted_iota(jnp.int32, (d.rows, d.lanes), 1)
@@ -472,7 +478,7 @@
     grad_e = jnp.zeros((d.rank, d.channels), F32)
     grad_h = jnp.zeros((1, d.channels), F32)
     for q in range(d.tiles):
-        up = dot(pair, head_rows(d, head, q, True))
+        up = dot(pair, halved(head_rows(d, head, q, True)))
         delta = jnp.concatenate(
             [
                 up[:, j * d.channels : (j + 1) * d.channels] * slope[q * d.group + j]
@@ -491,34 +497,19 @@
             grad_h = grad_h + total[t : t + 1, at] + total[d.times + t : d.times + t + 1, at]
     expand_grad[...] = grad_e
     head_grad[...] = jnp.concatenate([grad_h, jnp.zeros((SUB - 1, d.channels), F32)], axis=0)
+    core_gradient(d, (even, odd), own_out, core_grad)
     write_send(d, tab, own, send)
-    save.wait()
-
-
-def core_kernel(d, around_hbm, own, out, shifted, sems):
-    copies = Copies(sems, [(around_hbm, shifted)])
-    copies.wait(0)
-    core_gradient(d, shifted, own, out)
 
 
 def back_two_kernel(
-    d, tab_in, own_in, recv, core_hbm, reduce_hbm, expand_hbm, head_hbm, source, mixed, g_in, around_hbm, core_two,
-    expand_two, head_grad, own_out, send, wide, shifted, conv, own, flat, inner, outer, core, reduce_ref, expand_ref,
-    head_ref, around, packed, tab, sems,
+    d, tab_in, own_in, recv, inner, outer, reduce_ref, expand_ref, head_ref, source, mixed, g_in, first_even, first_odd,
+    core_two, expand_two, head_grad, own_out, send, wide, even, odd, conv, own, packed, tab, sems,
 ):
-    copies = Copies(
-        sems,
-        [
-            (tab_in, tab), (core_hbm, core), (reduce_hbm, reduce_ref), (expand_hbm, expand_ref),
-            (head_hbm, head_ref), (around_hbm, around),
-        ],
-    )
-    copies.wait(0)
-    fill(d, tab, own_in, recv, wide, shifted)
-    copies.wait(1, 2, 3, 4)
-    bands(d, core, flat, inner, outer, True)
-    convolve(d, shifted, inner, outer, -1, conv)
+    Copies(sems, [(tab_in, tab)]).wait(0)
+    fill(d, tab, own_in, recv, wide, even, odd)
+    convolve(d, (even, odd), inner, outer, -1, conv)
     expand = block_diag(d, expand_ref[...])
+    half = halved(expand)
     weight = block_diag(d, permuted_rows(d, reduce_ref[...]))
     head = head_ref[...]
     alive = alive_mask(d, tab[0])
@@ -526,28 +517,26 @@
     grad_r = jnp.zeros((d.rank, d.channels), F32)
     grad_e = jnp.zeros((d.rank, d.channels), F32)
     for q in range(d.tiles):
-        da = jnp.where(alive, trimmed(d, conv[q]), 0.0).astype(BF)
+        da = jnp.where(alive, conv[q], 0.0).astype(BF)
         grad_r = grad_r + diag_sum(d, dot_tn(da, times_of(d, source, q)))
         up = dot(
             jnp.concatenate([da, pair], axis=1),
-            jnp.concatenate([weight, head_rows(d, head, q, True)], axis=0),
+            halved(jnp.concatenate([weight, head_rows(d, head, q, True)], axis=0)),
         )
         b = mixed[q]
-        y = dot(b, expand)
+        y = dot(b, half)
         parts = []
         for j in range(d.group):
             at = slice(j * d.channels, (j + 1) * d.channels)
-            v = y[:, at]
-            s = sigmoid(v)
-            parts.append((up[:, at] * (s * (1.0 + v * (1.0 - s)))).astype(BF))
+            u = y[:, at]
+            parts.append((up[:, at] * slope_twice(u, jnp.tanh(u))).astype(BF))
         delta = jnp.concatenate(parts, axis=1)
         value = dot_nt(delta, expand).astype(BF)
         own_out[q] = value
         own[q] = value.astype(F32)
         grad_e = grad_e + diag_sum(d, dot_tn(b, delta))
-    copies.wait(5)
     off = d.offsets
-    core_gradient(d, around, own_out, packed)
+    core_gradient(d, (first_even, first_odd), own_out, packed)
     packed[off[1] : off[2], :] = core_two[...]
     packed[off[2] : off[3], :] = grad_e
     packed[off[3] : off[4], :] = grad_r
@@ -566,19 +555,14 @@
     lax.fori_loop(0, d.nspace, put, 0)
 
 
-def back_one_kernel(
-    d, tab_in, own_in, recv, core_hbm, source, send, wide, shifted, conv, flat, inner, outer, core, tab, sems
-):
-    copies = Copies(sems, [(tab_in, tab), (core_hbm, core)])
-    copies.wait(0)
-    fill(d, tab, own_in, recv, wide, shifted)
-    copies.wait(1)
-    bands(d, core, flat, inner, outer, True)
-    convolve(d, shifted, inner, outer, -1, conv)
+def back_one_kernel(d, tab_in, own_in, recv, inner, outer, source, send, wide, even, odd, conv, tab, sems):
+    Copies(sems, [(tab_in, tab)]).wait(0)
+    fill(d, tab, own_in, recv, wide, even, odd)
+    convolve(d, (even, odd), inner, outer, -1, conv)
     alive = alive_mask(d, tab[0])
     grad_r = jnp.zeros((d.rank, d.channels), F32)
     for q in range(d.tiles):
-        da = jnp.where(alive, trimmed(d, conv[q]), 0.0).astype(BF)
+        da = jnp.where(alive, conv[q], 0.0).astype(BF)
         grad_r = grad_r + diag_sum(d, dot_tn(da, times_of(d, source, q)))
 
     def add(n, total):
@@ -622,7 +606,7 @@
 HB = pl.BlockSpec(memory_space=pltpu.HBM)
 
 
-def call(kernel, d, name, ins, outs, scratch, operands, limit=LIMIT):
+def call(kernel, d, name, ins, outs, scratch, operands, cost=None):
     shapes = tuple(jax.ShapeDtypeStruct(s, t) for s, t, _ in outs)
     specs = tuple(m for _, _, m in outs)
     return pl.pallas_call(
@@ -632,7 +616,8 @@
         out_specs=specs,
         scratch_shapes=scratch,
         name=name,
-        compiler_params=pltpu.CompilerParams(vmem_limit_bytes=limit),
+        cost_estimate=cost,
+        compiler_params=pltpu.CompilerParams(vmem_limit_bytes=LIMIT),
     )(*operands)
 
 
@@ -649,20 +634,17 @@
     own_shape = (d.tiles, d.rows, d.lanes)
     wide_shape = (d.times, d.rows, d.channels)
     send_shape = (nspace, d.block, channels)
-    shifted_shape = (3, d.span, d.tiles * d.lanes)
+    even_shape = (3, d.lines * d.width, d.tiles * d.lanes)
+    odd_shape = (3, d.rows, d.tiles * d.lanes)
     size = 2 * d.lanes
     core_shape = (27 * rank // d.group, d.lanes)
     own_f = pltpu.VMEM(own_shape, F32)
     rim = pltpu.VMEM((d.tiles, d.span + 2 * SUB, d.lanes), F32)
-    shifted = pltpu.VMEM(shifted_shape, BF)
-    conv = pltpu.VMEM((d.tiles, d.core_rows, d.lanes), F32)
-    flat = pltpu.VMEM(core_shape, F32)
-    down = [pltpu.VMEM((9 * size, size), BF)] * 2
-    across = [pltpu.VMEM((size, 9 * size), BF)] * 2
-    core_v = pltpu.VMEM(core_one.shape, BF)
-    factor = pltpu.VMEM((rank, channels), BF)
+    views = [pltpu.VMEM(even_shape, BF), pltpu.VMEM(odd_shape, BF)]
     tab_s = pltpu.SMEM((d.t_size,), jnp.int32)
     small = ((rank, channels), F32, VM)
+    own_o, wide_o, send_o = (own_shape, BF, VM), (wide_shape, BF, VM), (send_shape, BF, VM)
+    band_shapes = [(9 * size, size), (9 * d.lanes, size), (size, 9 * size), (size, 9 * d.lanes)] * 2
 
     def sems(n):
         return pltpu.SemaphoreType.DMA((n,))
@@ -670,63 +652,57 @@
     def exchange(send):
         return lax.all_to_all(send, "space", split_axis=0, concat_axis=0, tiled=True)
 
-    tab, xt, a1, send = call(
-        first_kernel, d, "first", [SM, HB, HB, HB, HB],
-        [((d.t_size,), jnp.int32, VM), (wide_shape, BF, VM), (own_shape, BF, VM), (send_shape, BF, VM)],
+    (token,) = call(
+        start_kernel, d, "start", [SM], [((SUB, d.lanes), F32, VM)], [], [me],
+        cost=pl.CostEstimate(flops=10**10, bytes_accessed=0, transcendentals=0),
+    )
+    tab, xt, a1, send, inner1, outer1, inner1t, outer1t, inner2, outer2, inner2t, outer2t = call(
+        first_kernel, d, "first", [SM] + [HB] * 6 + [VM],
+        [((d.t_size,), jnp.int32, VM), wide_o, own_o, send_o] + [(b, BF, VM) for b in band_shapes],
         [
             pltpu.VMEM((edge, slots, edge, times, channels), BF),
             pltpu.VMEM((d.rows * times, channels), F32),
-            own_f, factor, pltpu.SMEM(run_lengths.shape, jnp.int32), pltpu.SMEM(run_owner.shape, jnp.int32), tab_s,
-            sems(edge + 4),
+            own_f, pltpu.SMEM(run_lengths.shape, jnp.int32), pltpu.SMEM(run_owner.shape, jnp.int32),
+            pltpu.VMEM((rank, channels), BF), pltpu.VMEM(core_one.shape, BF), pltpu.VMEM(core_one.shape, BF),
+            pltpu.VMEM(core_shape, F32), tab_s, sems(edge + 6),
         ],
-        [me, run_lengths, run_owner, volume, reduce_one],
+        [me, run_lengths, run_owner, volume, reduce_one, core_one, core_two, token],
     )
     recv = exchange(send)
-    b1, h1, a2, send, around1 = call(
-        layer_one_kernel, d, "layer_one", [VM, VM, VM, HB, HB, HB, VM],
-        [
-            (own_shape, BF, VM), (wide_shape, BF, VM), (own_shape, BF, VM), (send_shape, BF, VM),
-            (shifted_shape, BF, HB),
-        ],
-        [rim, shifted, conv, own_f, flat] + down + [core_v, factor, factor, tab_s, sems(5)],
-        [tab, a1, recv, core_one, expand_one, reduce_two, xt],
+    b1, h1, a2, send, even1, odd1 = call(
+        layer_one_kernel, d, "layer_one", [VM] * 8,
+        [own_o, wide_o, own_o, send_o, (even_shape, BF, VM), (odd_shape, BF, VM)],
+        [rim, own_f, own_f, tab_s, sems(1)],
+        [tab, a1, recv, inner1, outer1, expand_one, reduce_two, xt],
     )
     recv = exchange(send)
-    db2, send, prob, g, eg2, hg, around2 = call(
-        layer_two_kernel, d, "layer_two", [VM, VM, VM, HB, HB, HB, VM, HB],
+    db2, send, prob, g, eg2, hg, cg2 = call(
+        layer_two_kernel, d, "layer_two", [VM] * 9,
         [
-            (own_shape, BF, VM), (send_shape, BF, VM), (labels.shape, F32, VM), ((d.rows, d.lanes), BF, VM),
-            small, ((SUB, channels), F32, VM), (shifted_shape, BF, HB),
+            own_o, send_o, (labels.shape, F32, VM), ((d.rows, d.lanes), BF, VM), small, ((SUB, channels), F32, VM),
+            (core_shape, F32, VM),
         ],
-        [
-            rim, shifted, conv, own_f, pltpu.VMEM(wide_shape, F32), pltpu.VMEM(wide_shape, BF),
-            pltpu.VMEM(own_shape, BF), flat,
-        ]
-        + down
-        + [core_v, factor, pltpu.VMEM((1, channels), BF), pltpu.VMEM(labels.shape, jnp.int32), pltpu.VMEM((d.width, d.lanes), F32), tab_s, sems(6)],
-        [tab, a2, recv, core_two, expand_two, head, h1, labels],
+        [rim]
+        + views
+        + [
+            own_f, own_f, pltpu.VMEM(wide_shape, F32), pltpu.VMEM(wide_shape, BF), pltpu.VMEM(own_shape, BF),
+            pltpu.VMEM((d.width, d.lanes), F32), tab_s, sems(1),
+        ],
+        [tab, a2, recv, inner2, outer2, expand_two, head, h1, labels],
     )
     recv = exchange(send)
-    (cg2,) = call(
-        core_kernel, d, "core_two", [HB, VM], [(core_shape, F32, VM)], [shifted, sems(1)], [around2, db2]
-    )
     db1, send = call(
-        back_two_kernel, d, "back_two", [VM, VM, VM, HB, HB, HB, HB, VM, VM, VM, HB, VM, VM, VM],
-        [(own_shape, BF, VM), ((nspace, d.block + d.share, channels), BF, VM)],
-        [rim, shifted, conv, own_f, flat]
-        + across
-        + [
-            core_v, factor, factor, pltpu.VMEM((1, channels), BF), shifted,
-            pltpu.VMEM((nspace * d.share, channels), F32), tab_s, sems(6),
-        ],
-        [tab, db2, recv, core_two, reduce_two, expand_one, head, h1, b1, g, around1, cg2, eg2, hg],
+        back_two_kernel, d, "back_two", [VM] * 16,
+        [own_o, ((nspace, d.block + d.share, channels), BF, VM)],
+        [rim] + views + [own_f, own_f, pltpu.VMEM((nspace * d.share, channels), F32), tab_s, sems(1)],
+        [tab, db2, recv, inner2t, outer2t, reduce_two, expand_one, head, h1, b1, g, even1, odd1, cg2, eg2, hg],
     )
     recv = exchange(send)
     (send,) = call(
-        back_one_kernel, d, "back_one", [VM, VM, VM, HB, VM],
+        back_one_kernel, d, "back_one", [VM] * 6,
         [((nspace, rank + d.share, channels), BF, VM)],
-        [rim, shifted, conv, flat] + across + [core_v, tab_s, sems(2)],
-        [tab, db1, recv, core_one, xt],
+        [rim] + views + [own_f, tab_s, sems(1)],
+        [tab, db1, recv, inner1t, outer1t, xt],
     )
     recv = exchange(send)
     core_out = ((27, rank * rank), F32, VM)

time: 113 us -> 104 us (0.920)
  blocking collectives: 68.3 us -> 83.3 us
  waiting for transfers between devices: 10.7 us -> 0 us
  local copies, waits for them, and re-layouts: 5.97 us -> 1.11 us
  Pallas kernels: 22.6 us -> 18.7 us
  starting transfers between devices: 3.74 us -> 0 us
    all_to_all x4 -> x5, blocking collectives: 68.3 us -> 83.3 us  [exchange(): lax.all_to_all(send, 'space', split_axis=0, concat_axis=0, tiled=True)]
    all_to_all x1 -> x0, waiting for transfers between devices: 10.7 us -> none  [exchange(): lax.all_to_all(send, 'space', split_axis=0, concat_axis=0, tiled=True)]
    unnamed x30 -> x22, local copies, waits for them, and re-layouts: 5.97 us -> 1.11 us
    pallas_call x7, Pallas kernels: 22.6 us -> 18.7 us  [call(): pl.pallas_call(functools.partial(kernel, d), out_shape=shapes, in_specs=l...]
    all_to_all x1 -> x0, starting transfers between devices: 3.74 us -> none  [exchange(): lax.all_to_all(send, 'space', split_axis=0, concat_axis=0, tiled=True)]
  transfers between devices with their start and end apart: 1 -> 0, of which waited for: 1 -> 0; matrix products, arithmetic and copies ran while one was open for 0% -> 0% of each run, Pallas kernels for 1% -> 0%
where the time goes in v3:
time: 104 us
  blocking collectives  83.3 us (80%)
  Pallas kernels  18.7 us (18%)
  local copies, waits for them, and re-layouts  1.11 us (1%)
    all_to_all x5, blocking collectives, exchange(): lax.all_to_all(send, 'space', split_axis=0, concat_axis=0, tiled=True)  83.3 us
    pallas_call x7, Pallas kernels, call(): pl.pallas_call(functools.partial(kernel, d), out_shape=shapes, in_specs=l...  18.7 us

profile of v3, /device:TPU:0, one launch (start us, length us, event | category | flops | bytes accessed | tf_op | source)
XLA Modules:
  0.0 104.0 jit_solution(5266097909532861598)
XLA Ops:
  0.6 0.0 copy-start
  0.6 0.0 copy-start.1
  0.7 0.0 copy-start.2
  0.7 0.0 copy-start.6
  0.7 0.0 copy-start.9
  0.7 0.0 copy-start.10
  0.7 1.1 %copy-done = bf16[3,8,8,16,128]{4,3,2,1,0:T(8,128)(2,1)S(1)} copy-done((bf16[3,8,8,16,128]{4,3,2,1,0:T(8,128)(2,1)S(1)}, bf16[3,8,8,16,128]{4,3,2,1,0:T(8,128)(2,1)}, u32[]{:S(2)}) %copy-start) | copy-done | bytes 786456
  1.8 0.0 copy-done.1
  1.8 0.0 copy-done.2
  1.8 0.0 copy-done.6
  1.8 0.0 copy-done.9
  1.8 0.0 copy-done.10
  1.8 0.0 copy-start.3
  1.8 0.0 copy-start.4
  1.8 3.0 %first.1 = (s32[45]{0:T(128)S(1)}, bf16[16,192,128]{2,1,0:T(8,128)(2,1)S(1)}, bf16[4,192,128]{2,1,0:T(8,128)(2,1)S(1)}, bf16[16,96,128]{2,1,0:T(8,128)(2,1)S(1)}...) custom-call(s32[1]{0:T(128)} %bitcast.me, ...), custom_call_target="tpu_custom_call" | custom-call | tf_op jit(solution)/shard_map/first/pallas_call | solution.py:612
  4.8 19.4 %all_to_all.25.recv = bf16[16,96,128]{2,1,0:T(8,128)(2,1)S(1)} all-to-all(bf16[16,96,128]{2,1,0:T(8,128)(2,1)S(1)} %get-tuple-element.44), channel_id=1, replica_groups=mesh['groups'=2,'space'=16] {'space'}, dimensions={0} | all-to-all | bytes 786432 | tf_op jit(solution)/shard_map/all_to_all | solution.py:653
  24.2 0.0 copy-done.3
  24.2 0.0 copy-done.4
  24.2 0.0 copy-start.5
  24.2 0.0 copy-start.7
  24.2 0.0 copy-start.8
  24.2 2.9 %layer_one.1 = (bf16[4,192,128]{2,1,0:T(8,128)(2,1)S(1)}, bf16[16,192,128]{2,1,0:T(8,128)(2,1)S(1)}, bf16[4,192,128]{2,1,0:T(8,128)(2,1)S(1)}, bf16[16,96,128]{2...) custom-call(s32[45]{0:T(128)S(1)} %get-tuple-element.42.tab_in, ...), custom_call_target="tpu_custom_call" | custom-call | tf_op jit(solution)/shard_map/layer_one/pallas_call | solution.py:612
  27.1 15.4 %all_to_all.26.recv = bf16[16,96,128]{2,1,0:T(8,128)(2,1)S(1)} all-to-all(bf16[16,96,128]{2,1,0:T(8,128)(2,1)S(1)} %get-tuple-element.49), channel_id=1, replica_groups=mesh['groups'=2,'space'=16] {'space'}, dimensions={0} | all-to-all | bytes 786432 | tf_op jit(solution)/shard_map/all_to_all | solution.py:653
  42.5 0.0 copy-done.5
  42.5 0.0 copy-done.7
  42.5 0.0 copy-done.8
  42.5 5.5 %layer_two.1 = (bf16[4,192,128]{2,1,0:T(8,128)(2,1)S(1)}, bf16[16,96,128]{2,1,0:T(8,128)(2,1)S(1)}, f32[3,1024]{1,0:T(4,128)}, bf16[192,128]{1,0:T(8,128)(2,1)S(...) custom-call(s32[45]{0:T(128)S(1)} %get-tuple-element.42.tab_in, ...), custom_call_target="tpu_custom_call" | custom-call | tf_op jit(solution)/shard_map/layer_two/pallas_call | solution.py:612
  48.0 15.4 %all_to_all.27.recv = bf16[16,96,128]{2,1,0:T(8,128)(2,1)S(1)} all-to-all(bf16[16,96,128]{2,1,0:T(8,128)(2,1)S(1)} %get-tuple-element.55), channel_id=1, replica_groups=mesh['groups'=2,'space'=16] {'space'}, dimensions={0} | all-to-all | bytes 786432 | tf_op jit(solution)/shard_map/all_to_all | solution.py:653
  63.4 4.3 %back_two.1 = (bf16[4,192,128]{2,1,0:T(8,128)(2,1)S(1)}, bf16[16,136,128]{2,1,0:T(8,128)(2,1)S(1)}) custom-call(s32[45]{0:T(128)S(1)} %get-tuple-element.42.tab_in, bf16[4,192,128]{2,1,0:T(8,128)(2,1)S(1)} %get-tuple-element.54.own_in, bf16[16,96,128]{2,1,0:T(8,128)(2,1)S(1)} %all_to_all.27.recv, bf16[256,2304]{1,0:T(8,128)(2,1)S(1)} %get-tuple-element.56.inner, ...), custom_call_target="tpu_custom_call" | custom-call | tf_op jit(solution)/shard_map/back_two/pallas_call | solution.py:612
  67.7 19.9 %all_to_all.28.recv = bf16[16,136,128]{2,1,0:T(8,128)(2,1)S(1)} all-to-all(bf16[16,136,128]{2,1,0:T(8,128)(2,1)S(1)} %get-tuple-element.66), channel_id=1, replica_groups=mesh['groups'=2,'space'=16] {'space'}, dimensions={0} | all-to-all | bytes 1114112 | tf_op jit(solution)/shard_map/all_to_all | solution.py:653
  87.6 2.2 %back_one.1 = bf16[16,72,128]{2,1,0:T(8,128)(2,1)S(1)} custom-call(s32[45]{0:T(128)S(1)} %get-tuple-element.42.tab_in, bf16[4,192,128]{2,1,0:T(8,128)(2,1)S(1)} %get-tuple-element.65.own_in, bf16[16,136,128]{2,1,0:T(8,128)(2,1)S(1)} %all_to_all.28.recv, bf16[256,2304]{1,0:T(8,128)(2,1)S(1)} %get-tuple-element.67.inner, ...), custom_call_target="tpu_custom_call" | custom-call | tf_op jit(solution)/shard_map/back_one/pallas_call | solution.py:612
  89.8 13.3 %all_to_all.29.recv = bf16[16,72,128]{2,1,0:T(8,128)(2,1)S(1)} all-to-all(bf16[16,72,128]{2,1,0:T(8,128)(2,1)S(1)} %back_one.1), channel_id=1, replica_groups=mesh['groups'=2,'space'=16] {'space'}, dimensions={0} | all-to-all | bytes 589824 | tf_op jit(solution)/shard_map/all_to_all | solution.py:653
  103.1 0.9 unpack.1
  (1 shorter events, 0.0 us)
Async XLA Ops:
  0.6 1.1 %copy-start = (bf16[3,8,8,16,128]{4,3,2,1,0:T(8,128)(2,1)S(1)}, bf16[3,8,8,16,128]{4,3,2,1,0:T(8,128)(2,1)}, u32[]{:S(2)}) copy-start(bf16[3,8,8,16,128]{4,3,2,1,0:T(8,128)(2,1)} %x_hbm.1) | copy-start | bytes 2359300
  0.6 1.1 %copy-start.1 = (bf16[27,1024]{1,0:T(8,128)(2,1)S(1)}, bf16[27,1024]{1,0:T(8,128)(2,1)}, u32[]{:S(2)}) copy-start(bf16[27,1024]{1,0:T(8,128)(2,1)} %core_one_hbm.1) | copy-start | bytes 165892
  0.7 1.1 %copy-start.2 = (bf16[27,1024]{1,0:T(8,128)(2,1)S(1)}, bf16[27,1024]{1,0:T(8,128)(2,1)}, u32[]{:S(2)}) copy-start(bf16[27,1024]{1,0:T(8,128)(2,1)} %core_two_hbm.1) | copy-start | bytes 165892
  0.7 1.1 %copy-start.6 = (bf16[32,128]{1,0:T(8,128)(2,1)S(1)}, bf16[32,128]{1,0:T(8,128)(2,1)}, u32[]{:S(2)}) copy-start(bf16[32,128]{1,0:T(8,128)(2,1)} %reduce_hbm.1) | copy-start | bytes 24580
  0.7 1.1 %copy-start.9 = (s32[2,4]{1,0:T(2,128)S(1)}, s32[2,4]{1,0:T(2,128)}, u32[]{:S(2)}) copy-start(s32[2,4]{1,0:T(2,128)} %lengths_hbm.1) | copy-start | bytes 100
  0.7 1.1 %copy-start.10 = (s32[16]{0:T(128)S(1)}, s32[16]{0:T(128)}, u32[]{:S(2)}) copy-start(s32[16]{0:T(128)} %owner_hbm.1) | copy-start | bytes 196
  1.8 22.4 %copy-start.3 = (bf16[32,128]{1,0:T(8,128)(2,1)S(1)}, bf16[32,128]{1,0:T(8,128)(2,1)}, u32[]{:S(2)}) copy-start(bf16[32,128]{1,0:T(8,128)(2,1)} %expand_ref.5) | copy-start | bytes 24580
  1.8 22.4 %copy-start.4 = (bf16[32,128]{1,0:T(8,128)(2,1)S(1)}, bf16[32,128]{1,0:T(8,128)(2,1)}, u32[]{:S(2)}) copy-start(bf16[32,128]{1,0:T(8,128)(2,1)} %reduce_ref.1) | copy-start | bytes 24580
  24.2 18.3 %copy-start.5 = (s32[3,1024]{1,0:T(4,128)S(1)}, s32[3,1024]{1,0:T(4,128)}, u32[]{:S(2)}) copy-start(s32[3,1024]{1,0:T(4,128)} %labels.1) | copy-start | bytes 36868
  24.2 18.3 %copy-start.7 = (bf16[32,128]{1,0:T(8,128)(2,1)S(1)}, bf16[32,128]{1,0:T(8,128)(2,1)}, u32[]{:S(2)}) copy-start(bf16[32,128]{1,0:T(8,128)(2,1)} %expand_ref.4) | copy-start | bytes 24580
  24.2 18.3 %copy-start.8 = (bf16[128]{0:T(256)(128)(2,1)S(1)}, bf16[128]{0:T(256)(128)(2,1)}, u32[]{:S(2)}) copy-start(bf16[128]{0:T(256)(128)(2,1)} %param.21) | copy-start | bytes 772

commit v4 on v3

--- a/solution.py
+++ b/solution.py
@@ -32,10 +32,11 @@
         self.t_size = self.t_recv + 2 * 3 * (slots + 2)
         self.part = self.tiles * SUB
         self.block = slots * self.part
-        per_row = rank * rank // channels
-        sizes = [27 * per_row, 27 * per_row, rank, rank, rank, SUB]
-        self.offsets = [sum(sizes[:i]) for i in range(len(sizes) + 1)]
-        self.share = -(-self.offsets[-1] // (nspace * SUB)) * SUB
+        core = 27 * rank * rank // channels
+        self.two = [0, core, core + rank, core + rank + SUB]
+        self.one = [0, core, core + rank, core + 2 * rank]
+        self.share_two = -(-self.two[-1] // (nspace * SUB)) * SUB
+        self.share_one = -(-self.one[-1] // (nspace * SUB)) * SUB
 
 
 def dot(a, b):
@@ -154,6 +155,26 @@
             tab[base + 2] = jnp.where(ok, p - first, 0)
 
 
+def write_shares(d, packed, used, share, send):
+    rest = d.nspace * share - used
+    if rest:
+        packed[used:, :] = jnp.zeros((rest, d.channels), F32)
+
+    def put(n, carry):
+        at = pl.multiple_of(n * share, SUB)
+        send[n, d.block :, :] = packed[pl.ds(at, share), :].astype(BF)
+        return carry
+
+    lax.fori_loop(0, d.nspace, put, 0)
+
+
+def sum_shares(d, share, recv):
+    def add(n, total):
+        return total + recv[n, d.block :, :].astype(F32)
+
+    return lax.fori_loop(0, d.nspace, add, jnp.zeros((share, d.channels), F32))
+
+
 def write_send(d, tab, own, send):
     for side, line in ((0, 0), (1, d.edge - 1)):
         base = d.t_send + side * (1 + d.row_runs)
@@ -222,27 +243,29 @@
             lines = [
                 wide[q, SUB + d.line * n + di : SUB + d.line * n + di + d.width, :] for n in range(d.lines)
             ]
-            at = slice(q * d.lanes, (q + 1) * d.lanes)
-            even[di + 1, :, at] = jnp.concatenate(lines, axis=0).astype(BF)
-            odd[di + 1, :, at] = jnp.concatenate(lines[1:-1], axis=0).astype(BF)
-
-
-def windows(d, views, direction, first, count):
+            even[di + 1, q] = jnp.concatenate(lines, axis=0).astype(BF)
+            odd[di + 1, q] = jnp.concatenate(lines[1:-1], axis=0).astype(BF)
+
+
+def windows(d, views, direction, q):
     even, odd = views
     parts = []
     for di in (-1, 0, 1):
         for dc in (-1, 0, 1):
-            col = slice(first * d.lanes, (first + count) * d.lanes)
             n = 1 + direction * di
             if dc == 0:
-                parts.append(odd[n, :, col])
+                parts.append(odd[n, q])
             else:
                 at = d.width * (1 + direction * dc)
-                parts.append(even[n, at : at + d.rows, col])
+                parts.append(even[n, q, at : at + d.rows, :])
     return parts
 
 
-def bands(d, core, flat, inner, outer, inner_t, outer_t):
+def beside(ref):
+    return jnp.concatenate([ref[n] for n in range(ref.shape[0])], axis=1)
+
+
+def bands(d, core, flat, inner, outer, outer_t):
     rank, group, lanes = d.rank, d.group, d.lanes
     high = rank // group
     for rh in range(high):
@@ -271,38 +294,61 @@
                 value = jnp.where(lane == delta - dt, full[dt + 1], value)
             cache[delta] = value.astype(BF)
         for down in range(2 * group):
-            row = slice(down * rank, (down + 1) * rank)
             for across in range(2):
                 value = cache.get(down - across * group, zero)
-                inner[k * size + down * rank : k * size + (down + 1) * rank, across * lanes : (across + 1) * lanes] = value
-                inner_t[row, k * size + across * lanes : k * size + (across + 1) * lanes] = value
+                inner[across, k * size + down * rank : k * size + (down + 1) * rank, :] = value
             far = cache[-1] if down == group - 1 else cache[group] if down == group else zero
-            outer_t[row, k * lanes : (k + 1) * lanes] = far
+            outer_t[k, down * rank : (down + 1) * rank, :] = far
         for down in range(group):
             row = slice(k * lanes + down * rank, k * lanes + (down + 1) * rank)
-            outer[row, :lanes] = cache[group] if down == 0 else zero
-            outer[row, lanes:] = cache[-1] if down == group - 1 else zero
-
-
-def convolve(d, views, inner, outer, direction, out):
-    mul = dot if direction == 1 else dot_nt
-    half = d.tiles // 2
-    stacked = [
-        jnp.concatenate(windows(d, views, direction, 2 * p, 2), axis=1) for p in range(half)
-    ]
-    total = mul(jnp.concatenate(stacked, axis=0), inner[...])
-    for p in range(half):
+            outer[0, row, :] = cache[group] if down == 0 else zero
+            outer[1, row, :] = cache[-1] if down == group - 1 else zero
+
+
+class Conv:
+    def __init__(self, d, views, inner, outer, direction, out):
+        self.d, self.inner, self.direction, self.out = d, inner, direction, out
+        self.tiles = [windows(d, views, direction, q) for q in range(d.tiles)]
+        self.mul = dot if direction == 1 else dot_nt
+        self.half = d.tiles // 2
+        lane = lax.broadcasted_iota(jnp.int32, (d.rows, d.lanes), 1) // d.rank
+        for p in range(self.half - 1):
+            mixed = [
+                jnp.where(lane == d.group - 1, x, y)
+                for x, y in zip(self.tiles[2 * p + 1], self.tiles[2 * p + 2])
+            ]
+            total = self.mul(jnp.concatenate(mixed, axis=1), beside(outer))
+            for n in range(2):
+                out[2 * p + 1 + n] = total[:, n * d.lanes : (n + 1) * d.lanes]
+
+    def left(self, p):
+        parts = [
+            part for k in range(self.d.taps) for part in (self.tiles[2 * p][k], self.tiles[2 * p + 1][k])
+        ]
+        return jnp.concatenate(parts, axis=1)
+
+    def put(self, p, total):
+        d = self.d
         for n in range(2):
-            out[2 * p + n] = total[p * d.rows : (p + 1) * d.rows, n * d.lanes : (n + 1) * d.lanes]
-    lane = lax.broadcasted_iota(jnp.int32, (d.rows, d.lanes), 1) // d.rank
-    for p in range(half - 1):
-        before = windows(d, views, direction, 2 * p + 1, 1)
-        after = windows(d, views, direction, 2 * p + 2, 1)
-        mixed = [jnp.where(lane == d.group - 1, x, y) for x, y in zip(before, after)]
-        total = mul(jnp.concatenate(mixed, axis=1), outer[...])
-        for n in range(2):
-            q = 2 * p + 1 + n
-            out[q] = out[q] + total[:, n * d.lanes : (n + 1) * d.lanes]
+            q = 2 * p + n
+            part = total[:, n * d.lanes : (n + 1) * d.lanes]
+            if 0 < q < d.tiles - 1:
+                part = self.out[q] + part
+            self.out[q] = part
+
+    def tile(self, q):
+        d = self.d
+        if self.direction == 1 and q % 2 == 0:
+            self.put(q // 2, dot(self.left(q // 2), beside(self.inner)))
+        if self.direction == -1 and q == 0:
+            size = 2 * d.lanes
+            right = jnp.concatenate(
+                [self.inner[n, k * size : (k + 1) * size, :] for k in range(d.taps) for n in range(2)], axis=1
+            )
+            total = dot_nt(jnp.concatenate([self.left(p) for p in range(self.half)], axis=0), right)
+            for p in range(self.half):
+                self.put(p, total[p * d.rows : (p + 1) * d.rows])
+        return self.out[q]
 
 
 def core_gradient(d, views, own, out):
@@ -319,9 +365,10 @@
     rank, group = d.rank, d.group
     high = rank // group
     wide_lane = lax.broadcasted_iota(jnp.int32, (high, d.lanes), 1) // rank
+    left = [jnp.concatenate(windows(d, views, 1, q), axis=1) for q in range(d.tiles)]
+    every = dot_tn(jnp.concatenate(left, axis=0), right)
     for k in range(d.taps):
-        left = jnp.concatenate([windows(d, views, 1, q, 1)[k] for q in range(d.tiles)], axis=0)
-        total = dot_tn(left, right)
+        total = every[k * d.lanes : (k + 1) * d.lanes]
         for dt in (-1, 0, 1):
             pieces = []
             for j in range(group):
@@ -366,8 +413,8 @@
 ):
     del token
     tab_out, xt, own_out, send = refs[:4]
-    band_refs = refs[4:12]
-    xc, xf, own, lengths, owner, reduce_ref, core_one, core_two, flat, tab, sems = refs[12:]
+    band_refs = refs[4:10]
+    xc, xf, own, lengths, owner, reduce_ref, core_one, core_two, flat, tab, sems = refs[10:]
     copies = Copies(
         sems,
         [
@@ -379,23 +426,27 @@
     copies.wait(0, 1, 2, 3, 4)
     make_table(d, me[0], lengths, owner, tab)
     weight = block_diag(d, permuted_rows(d, reduce_ref[...]))
-    bands(d, core_one, flat, *band_refs[0:4])
-    bands(d, core_two, flat, *band_refs[4:8])
     save = pltpu.make_async_copy(tab, tab_out, sems.at[d.edge + 5])
     save.start()
     per_line = d.width * d.times
+    copies.wait(*range(5, 5 + d.edge))
     for c in range(d.edge):
-        copies.wait(5 + c)
         xf[c * per_line : (c + 1) * per_line, :] = xc[c].reshape(per_line, d.channels).astype(F32)
     alive = alive_mask(d, tab[0])
     for q in range(d.tiles):
+        parts = []
         for j in range(d.group):
             t = q * d.group + j
-            xt[t] = xf[pl.ds(t, d.rows, stride=d.times), :].astype(BF)
-        value = dot_nt(times_of(d, xt, q), weight)
+            parts.append(xf[pl.ds(t, d.rows, stride=d.times), :].astype(BF))
+            xt[t] = parts[-1]
+        value = dot_nt(jnp.concatenate(parts, axis=1), weight)
         value = jnp.where(alive, value, 0.0).astype(BF)
         own_out[q] = value
         own[q] = value.astype(F32)
+        if q == 0:
+            bands(d, core_one, flat, *band_refs[0:3])
+        if q == d.tiles // 2:
+            bands(d, core_two, flat, *band_refs[3:6])
     write_send(d, tab, own, send)
     save.wait()
 
@@ -406,20 +457,22 @@
 ):
     Copies(sems, [(tab_in, tab)]).wait(0)
     fill(d, tab, own_in, recv, wide, even, odd)
-    convolve(d, (even, odd), inner, outer, 1, conv)
+    mixing = Conv(d, (even, odd), inner, outer, 1, conv)
     expand = block_diag(d, expand_ref[...])
     half = halved(expand)
     weight = block_diag(d, permuted_rows(d, reduce_next[...]))
     alive = alive_mask(d, tab[0])
     for q in range(d.tiles):
-        b = conv[q].astype(BF)
+        b = mixing.tile(q).astype(BF)
         mixed[q] = b
         y = dot(b, half)
+        parts = []
         for j in range(d.group):
             t = q * d.group + j
             u = y[:, j * d.channels : (j + 1) * d.channels]
-            hidden[t] = (source[t].astype(F32) + silu(u)).astype(BF)
-        value = dot_nt(times_of(d, hidden, q), weight)
+            parts.append((source[t].astype(F32) + silu(u)).astype(BF))
+            hidden[t] = parts[-1]
+        value = dot_nt(jnp.concatenate(parts, axis=1), weight)
         value = jnp.where(alive, value, 0.0).astype(BF)
         own_out[q] = value
         own[q] = value.astype(F32)
@@ -446,26 +499,28 @@
 
 def layer_two_kernel(
     d, tab_in, own_in, recv, inner, outer, expand_ref, head_ref, source, labels, own_out, send, prob, g_out,
-    expand_grad, head_grad, core_grad, wide, even, odd, conv, own, slope, last, mixed, plane, tab, sems,
+    wide, even, odd, conv, own, slope, last, mixed, plane, packed, tab, sems,
 ):
     Copies(sems, [(tab_in, tab)]).wait(0)
     fill(d, tab, own_in, recv, wide, even, odd)
-    convolve(d, (even, odd), inner, outer, 1, conv)
+    mixing = Conv(d, (even, odd), inner, outer, 1, conv)
     expand = block_diag(d, expand_ref[...])
     half = halved(expand)
     head = head_ref[...]
     logit = jnp.zeros((d.rows, d.lanes), F32)
     for q in range(d.tiles):
-        b = conv[q].astype(BF)
+        b = mixing.tile(q).astype(BF)
         mixed[q] = b
         y = dot(b, half)
+        parts = []
         for j in range(d.group):
             t = q * d.group + j
             u = y[:, j * d.channels : (j + 1) * d.channels]
             th = jnp.tanh(u)
             slope[t] = slope_twice(u, th)
-            last[t] = (source[t].astype(F32) + (u + u * th)).astype(BF)
-        logit = logit + dot_nt(times_of(d, last, q), head_rows(d, head, q, False))
+            parts.append((source[t].astype(F32) + (u + u * th)).astype(BF))
+            last[t] = parts[-1]
+        logit = logit + dot_nt(jnp.concatenate(parts, axis=1), head_rows(d, head, q, False))
     chance = jax.nn.sigmoid(logit)
     lane = lax.broadcasted_iota(jnp.int32, (d.rows, d.lanes), 1)
     live = alive_mask(d, tab[0]) & (lane < d.times)
@@ -495,19 +550,21 @@
             t = q * d.group + j
             at = slice(j * d.channels, (j + 1) * d.channels)
             grad_h = grad_h + total[t : t + 1, at] + total[d.times + t : d.times + t + 1, at]
-    expand_grad[...] = grad_e
-    head_grad[...] = jnp.concatenate([grad_h, jnp.zeros((SUB - 1, d.channels), F32)], axis=0)
-    core_gradient(d, (even, odd), own_out, core_grad)
+    off = d.two
+    core_gradient(d, (even, odd), own_out, packed)
+    packed[off[1] : off[2], :] = grad_e
+    packed[off[2] : off[3], :] = jnp.concatenate([grad_h, jnp.zeros((SUB - 1, d.channels), F32)], axis=0)
     write_send(d, tab, own, send)
+    write_shares(d, packed, off[-1], d.share_two, send)
 
 
 def back_two_kernel(
     d, tab_in, own_in, recv, inner, outer, reduce_ref, expand_ref, head_ref, source, mixed, g_in, first_even, first_odd,
-    core_two, expand_two, head_grad, own_out, send, wide, even, odd, conv, own, packed, tab, sems,
+    own_out, send, shares, wide, even, odd, conv, own, packed, tab, sems,
 ):
     Copies(sems, [(tab_in, tab)]).wait(0)
     fill(d, tab, own_in, recv, wide, even, odd)
-    convolve(d, (even, odd), inner, outer, -1, conv)
+    mixing = Conv(d, (even, odd), inner, outer, -1, conv)
     expand = block_diag(d, expand_ref[...])
     half = halved(expand)
     weight = block_diag(d, permuted_rows(d, reduce_ref[...]))
@@ -517,7 +574,7 @@
     grad_r = jnp.zeros((d.rank, d.channels), F32)
     grad_e = jnp.zeros((d.rank, d.channels), F32)
     for q in range(d.tiles):
-        da = jnp.where(alive, conv[q], 0.0).astype(BF)
+        da = jnp.where(alive, mixing.tile(q), 0.0).astype(BF)
         grad_r = grad_r + diag_sum(d, dot_tn(da, times_of(d, source, q)))
         up = dot(
             jnp.concatenate([da, pair], axis=1),
@@ -535,41 +592,26 @@
         own_out[q] = value
         own[q] = value.astype(F32)
         grad_e = grad_e + diag_sum(d, dot_tn(b, delta))
-    off = d.offsets
+    off = d.one
     core_gradient(d, (first_even, first_odd), own_out, packed)
-    packed[off[1] : off[2], :] = core_two[...]
-    packed[off[2] : off[3], :] = grad_e
-    packed[off[3] : off[4], :] = grad_r
-    packed[off[4] : off[5], :] = expand_two[...]
-    packed[off[5] : off[6], :] = head_grad[...]
-    rest = d.nspace * d.share - off[6]
-    if rest:
-        packed[off[6] :, :] = jnp.zeros((rest, d.channels), F32)
+    packed[off[1] : off[2], :] = grad_e
+    packed[off[2] : off[3], :] = grad_r
     write_send(d, tab, own, send)
-
-    def put(n, carry):
-        at = pl.multiple_of(n * d.share, SUB)
-        send[n, d.block :, :] = packed[pl.ds(at, d.share), :].astype(BF)
-        return carry
-
-    lax.fori_loop(0, d.nspace, put, 0)
-
-
-def back_one_kernel(d, tab_in, own_in, recv, inner, outer, source, send, wide, even, odd, conv, tab, sems):
+    write_shares(d, packed, off[-1], d.share_one, send)
+    shares[...] = sum_shares(d, d.share_two, recv)
+
+
+def back_one_kernel(d, tab_in, own_in, recv, inner, outer, source, shares, send, wide, even, odd, conv, tab, sems):
     Copies(sems, [(tab_in, tab)]).wait(0)
     fill(d, tab, own_in, recv, wide, even, odd)
-    convolve(d, (even, odd), inner, outer, -1, conv)
+    mixing = Conv(d, (even, odd), inner, outer, -1, conv)
     alive = alive_mask(d, tab[0])
     grad_r = jnp.zeros((d.rank, d.channels), F32)
     for q in range(d.tiles):
-        da = jnp.where(alive, conv[q], 0.0).astype(BF)
+        da = jnp.where(alive, mixing.tile(q), 0.0).astype(BF)
         grad_r = grad_r + diag_sum(d, dot_tn(da, times_of(d, source, q)))
 
-    def add(n, total):
-        return total + recv[n, d.block :, :].astype(F32)
-
-    shares = lax.fori_loop(0, d.nspace, add, jnp.zeros((d.share, d.channels), F32))
-    out = jnp.concatenate([grad_r, shares], axis=0).astype(BF)
+    out = jnp.concatenate([grad_r, shares[...], sum_shares(d, d.share_one, recv)], axis=0).astype(BF)
 
     def put(n, carry):
         send[n] = out
@@ -578,27 +620,31 @@
     lax.fori_loop(0, d.nspace, put, 0)
 
 
-def unpack_kernel(d, recv, reduce_one, core_one, expand_one, reduce_two, core_two, expand_two, head, packed):
-    off = d.offsets
+def unpack_kernel(
+    d, recv, reduce_one, core_one, expand_one, reduce_two, core_two, expand_two, head, pack_one, pack_two
+):
     high = d.rank // d.group
     scale = 1.0 / d.cells
+    middle = d.rank + d.share_two
 
     def take(n, total):
-        at = pl.multiple_of(n * d.share, SUB)
-        packed[pl.ds(at, d.share), :] = recv[n, d.rank :, :].astype(F32) * scale
+        at = pl.multiple_of(n * d.share_two, SUB)
+        pack_two[pl.ds(at, d.share_two), :] = recv[n, d.rank : middle, :].astype(F32) * scale
+        at = pl.multiple_of(n * d.share_one, SUB)
+        pack_one[pl.ds(at, d.share_one), :] = recv[n, middle:, :].astype(F32) * scale
         return total + recv[n, : d.rank, :].astype(F32)
 
     first = lax.fori_loop(0, d.nspace, take, jnp.zeros((d.rank, d.channels), F32)) * scale
-    for at, core in ((off[0], core_one), (off[1], core_two)):
+    for packed, core in ((pack_one, core_one), (pack_two, core_two)):
         for rh in range(high):
-            core[:, rh * d.lanes : (rh + 1) * d.lanes] = packed[pl.ds(at + rh, 27, stride=high), :]
-    second = packed[off[3] : off[4], :]
+            core[:, rh * d.lanes : (rh + 1) * d.lanes] = packed[pl.ds(rh, 27, stride=high), :]
+    second = pack_one[d.one[2] : d.one[3], :]
     for value, ref in ((first, reduce_one), (second, reduce_two)):
         for rl in range(d.group):
             ref[pl.ds(rl, high, stride=d.group), :] = value[rl * high : (rl + 1) * high]
-    expand_one[...] = packed[off[2] : off[3], :]
-    expand_two[...] = packed[off[4] : off[5], :]
-    head[...] = packed[off[5] : off[5] + 1, :]
+    expand_one[...] = pack_one[d.one[1] : d.one[2], :]
+    expand_two[...] = pack_two[d.two[1] : d.two[2], :]
+    head[...] = pack_two[d.two[2] : d.two[2] + 1, :]
 
 
 VM = pl.BlockSpec(memory_space=pltpu.VMEM)
@@ -634,8 +680,8 @@
     own_shape = (d.tiles, d.rows, d.lanes)
     wide_shape = (d.times, d.rows, d.channels)
     send_shape = (nspace, d.block, channels)
-    even_shape = (3, d.lines * d.width, d.tiles * d.lanes)
-    odd_shape = (3, d.rows, d.tiles * d.lanes)
+    even_shape = (3, d.tiles, d.lines * d.width, d.lanes)
+    odd_shape = (3, d.tiles, d.rows, d.lanes)
     size = 2 * d.lanes
     core_shape = (27 * rank // d.group, d.lanes)
     own_f = pltpu.VMEM(own_shape, F32)
@@ -644,7 +690,11 @@
     tab_s = pltpu.SMEM((d.t_size,), jnp.int32)
     small = ((rank, channels), F32, VM)
     own_o, wide_o, send_o = (own_shape, BF, VM), (wide_shape, BF, VM), (send_shape, BF, VM)
-    band_shapes = [(9 * size, size), (9 * d.lanes, size), (size, 9 * size), (size, 9 * d.lanes)] * 2
+    band_shapes = [
+        (2, d.taps * size, d.lanes), (2, d.taps * d.lanes, d.lanes), (d.taps, size, d.lanes)
+    ] * 2
+    pack_one = pltpu.VMEM((nspace * d.share_one, channels), F32)
+    pack_two = pltpu.VMEM((nspace * d.share_two, channels), F32)
 
     def sems(n):
         return pltpu.SemaphoreType.DMA((n,))
@@ -656,7 +706,7 @@
         start_kernel, d, "start", [SM], [((SUB, d.lanes), F32, VM)], [], [me],
         cost=pl.CostEstimate(flops=10**10, bytes_accessed=0, transcendentals=0),
     )
-    tab, xt, a1, send, inner1, outer1, inner1t, outer1t, inner2, outer2, inner2t, outer2t = call(
+    tab, xt, a1, send, inner1, outer1, outer1t, inner2, outer2, outer2t = call(
         first_kernel, d, "first", [SM] + [HB] * 6 + [VM],
         [((d.t_size,), jnp.int32, VM), wide_o, own_o, send_o] + [(b, BF, VM) for b in band_shapes],
         [
@@ -676,40 +726,40 @@
         [tab, a1, recv, inner1, outer1, expand_one, reduce_two, xt],
     )
     recv = exchange(send)
-    db2, send, prob, g, eg2, hg, cg2 = call(
+    db2, send, prob, g = call(
         layer_two_kernel, d, "layer_two", [VM] * 9,
         [
-            own_o, send_o, (labels.shape, F32, VM), ((d.rows, d.lanes), BF, VM), small, ((SUB, channels), F32, VM),
-            (core_shape, F32, VM),
+            own_o, ((nspace, d.block + d.share_two, channels), BF, VM), (labels.shape, F32, VM),
+            ((d.rows, d.lanes), BF, VM),
         ],
         [rim]
         + views
         + [
             own_f, own_f, pltpu.VMEM(wide_shape, F32), pltpu.VMEM(wide_shape, BF), pltpu.VMEM(own_shape, BF),
-            pltpu.VMEM((d.width, d.lanes), F32), tab_s, sems(1),
+            pltpu.VMEM((d.width, d.lanes), F32), pack_two, tab_s, sems(1),
         ],
         [tab, a2, recv, inner2, outer2, expand_two, head, h1, labels],
     )
     recv = exchange(send)
-    db1, send = call(
-        back_two_kernel, d, "back_two", [VM] * 16,
-        [own_o, ((nspace, d.block + d.share, channels), BF, VM)],
-        [rim] + views + [own_f, own_f, pltpu.VMEM((nspace * d.share, channels), F32), tab_s, sems(1)],
-        [tab, db2, recv, inner2t, outer2t, reduce_two, expand_one, head, h1, b1, g, even1, odd1, cg2, eg2, hg],
+    db1, send, shares = call(
+        back_two_kernel, d, "back_two", [VM] * 13,
+        [own_o, ((nspace, d.block + d.share_one, channels), BF, VM), ((d.share_two, channels), F32, VM)],
+        [rim] + views + [own_f, own_f, pack_one, tab_s, sems(1)],
+        [tab, db2, recv, inner2, outer2t, reduce_two, expand_one, head, h1, b1, g, even1, odd1],
     )
     recv = exchange(send)
     (send,) = call(
-        back_one_kernel, d, "back_one", [VM] * 6,
-        [((nspace, rank + d.share, channels), BF, VM)],
+        back_one_kernel, d, "back_one", [VM] * 7,
+        [((nspace, rank + d.share_two + d.share_one, channels), BF, VM)],
         [rim] + views + [own_f, tab_s, sems(1)],
-        [tab, db1, recv, inner1t, outer1t, xt],
+        [tab, db1, recv, inner1, outer1t, xt, shares],
     )
     recv = exchange(send)
     core_out = ((27, rank * rank), F32, VM)
     r1, c1, e1, r2, c2, e2, hv = call(
         unpack_kernel, d, "unpack", [VM],
         [small, core_out, small, small, core_out, small, ((1, channels), F32, VM)],
-        [pltpu.VMEM((nspace * d.share, channels), F32)], [recv],
+        [pack_one, pack_two], [recv],
     )
     return prob, r1, c1, e1, r2, c2, e2, hv.reshape(channels)
 

time: 104 us -> 103 us (level)
  Pallas kernels: 18.7 us -> 17.4 us
    pallas_call x7, Pallas kernels: 18.7 us -> 17.4 us  [call(): pl.pallas_call(functools.partial(kernel, d), out_shape=shapes, in_specs=l...]
where the time goes in v4:
time: 103 us; the launch traced here: 102 us
  blocking collectives  82.9 us (80%)
  Pallas kernels  17.4 us (17%)
  local copies, waits for them, and re-layouts  1.11 us (1%)
    all_to_all x5, blocking collectives, exchange(): lax.all_to_all(send, 'space', split_axis=0, concat_axis=0, tiled=True)  82.9 us
    pallas_call x7, Pallas kernels, call(): pl.pallas_call(functools.partial(kernel, d), out_shape=shapes, in_specs=l...  17.4 us

profile of v4, /device:TPU:0, one launch (start us, length us, event | category | flops | bytes accessed | tf_op | source)
XLA Modules:
  0.0 102.2 jit_solution(12311755774624376060)
XLA Ops:
  0.6 0.0 copy-start
  0.6 0.0 copy-start.1
  0.7 0.0 copy-start.2
  0.7 0.0 copy-start.6
  0.7 0.0 copy-start.9
  0.7 0.0 copy-start.10
  0.7 1.1 %copy-done = bf16[3,8,8,16,128]{4,3,2,1,0:T(8,128)(2,1)S(1)} copy-done((bf16[3,8,8,16,128]{4,3,2,1,0:T(8,128)(2,1)S(1)}, bf16[3,8,8,16,128]{4,3,2,1,0:T(8,128)(2,1)}, u32[]{:S(2)}) %copy-start) | copy-done | bytes 786456
  1.8 0.0 copy-done.1
  1.8 0.0 copy-done.2
  1.8 0.0 copy-done.6
  1.8 0.0 copy-done.9
  1.8 0.0 copy-done.10
  1.8 0.0 copy-start.3
  1.8 0.0 copy-start.4
  1.8 2.2 %first.1 = (s32[45]{0:T(128)S(1)}, bf16[16,192,128]{2,1,0:T(8,128)(2,1)S(1)}, bf16[4,192,128]{2,1,0:T(8,128)(2,1)S(1)}, bf16[16,96,128]{2,1,0:T(8,128)(2,1)S(1)}...) custom-call(s32[1]{0:T(128)} %bitcast.me, ...), custom_call_target="tpu_custom_call" | custom-call | tf_op jit(solution)/shard_map/first/pallas_call | solution.py:658
  4.1 19.4 %all_to_all.25.recv = bf16[16,96,128]{2,1,0:T(8,128)(2,1)S(1)} all-to-all(bf16[16,96,128]{2,1,0:T(8,128)(2,1)S(1)} %get-tuple-element.40), channel_id=1, replica_groups=mesh['groups'=2,'space'=16] {'space'}, dimensions={0} | all-to-all | bytes 786432 | tf_op jit(solution)/shard_map/all_to_all | solution.py:703
  23.4 0.0 copy-done.3
  23.4 0.0 copy-done.4
  23.4 0.0 copy-start.5
  23.5 0.0 copy-start.7
  23.5 0.0 copy-start.8
  23.5 2.6 %layer_one.1 = (bf16[4,192,128]{2,1,0:T(8,128)(2,1)S(1)}, bf16[16,192,128]{2,1,0:T(8,128)(2,1)S(1)}, bf16[4,192,128]{2,1,0:T(8,128)(2,1)S(1)}, bf16[16,96,128]{2...) custom-call(s32[45]{0:T(128)S(1)} %get-tuple-element.38.tab_in, ...), custom_call_target="tpu_custom_call" | custom-call | tf_op jit(solution)/shard_map/layer_one/pallas_call | solution.py:658
  26.1 15.4 %all_to_all.26.recv = bf16[16,96,128]{2,1,0:T(8,128)(2,1)S(1)} all-to-all(bf16[16,96,128]{2,1,0:T(8,128)(2,1)S(1)} %get-tuple-element.45), channel_id=1, replica_groups=mesh['groups'=2,'space'=16] {'space'}, dimensions={0} | all-to-all | bytes 786432 | tf_op jit(solution)/shard_map/all_to_all | solution.py:703
  41.5 0.0 copy-done.5
  41.5 0.0 copy-done.7
  41.5 0.0 copy-done.8
  41.5 5.2 %layer_two.1 = (bf16[4,192,128]{2,1,0:T(8,128)(2,1)S(1)}, bf16[16,112,128]{2,1,0:T(8,128)(2,1)S(1)}, f32[3,1024]{1,0:T(4,128)}, bf16[192,128]{1,0:T(8,128)(2,1)S(1)}) custom-call(s32[45]{0:T(128)S(1)} %get-tuple-element.38.tab_in, bf16[4,192,128]{2,1,0:T(8,128)(2,1)S(1)} %get-tuple-element.44.own_in, bf16[16,96,128]{2,1,0:T(8,128)(2,1)S(1)} %all_to_all.26.recv, ...), custom_call_target="tpu_custom_call" | custom-call | tf_op jit(solution)/shard_map/layer_two/pallas_call | solution.py:658
  46.7 16.4 %all_to_all.27.recv = bf16[16,112,128]{2,1,0:T(8,128)(2,1)S(1)} all-to-all(bf16[16,112,128]{2,1,0:T(8,128)(2,1)S(1)} %get-tuple-element.51), channel_id=1, replica_groups=mesh['groups'=2,'space'=16] {'space'}, dimensions={0} | all-to-all | bytes 917504 | tf_op jit(solution)/shard_map/all_to_all | solution.py:703
  63.1 4.4 %back_two.1 = (bf16[4,192,128]{2,1,0:T(8,128)(2,1)S(1)}, bf16[16,120,128]{2,1,0:T(8,128)(2,1)S(1)}, f32[16,128]{1,0:T(8,128)S(1)}) custom-call(s32[45]{0:T(128)S(1)} %get-tuple-element.38.tab_in, bf16[4,192,128]{2,1,0:T(8,128)(2,1)S(1)} %get-tuple-element.50.own_in, bf16[16,112,128]{2,1,0:T(8,128)(2,1)S(1)} %all_to_all.27.recv, ...), custom_call_target="tpu_custom_call" | custom-call | tf_op jit(solution)/shard_map/back_two/pallas_call | solution.py:658
  67.5 17.3 %all_to_all.28.recv = bf16[16,120,128]{2,1,0:T(8,128)(2,1)S(1)} all-to-all(bf16[16,120,128]{2,1,0:T(8,128)(2,1)S(1)} %get-tuple-element.58), channel_id=1, replica_groups=mesh['groups'=2,'space'=16] {'space'}, dimensions={0} | all-to-all | bytes 983040 | tf_op jit(solution)/shard_map/all_to_all | solution.py:703
  84.9 2.1 %back_one.1 = bf16[16,72,128]{2,1,0:T(8,128)(2,1)S(1)} custom-call(s32[45]{0:T(128)S(1)} %get-tuple-element.38.tab_in, bf16[4,192,128]{2,1,0:T(8,128)(2,1)S(1)} %get-tuple-element.57.own_in, bf16[16,120,128]{2,1,0:T(8,128)(2,1)S(1)} %all_to_all.28.recv, bf16[2,2304,128]{2,1,0:T(8,128)(2,1)S(1)} %get-tuple-element.41.inner, ...), custom_call_target="tpu_custom_call" | custom-call | tf_op jit(solution)/shard_map/back_one/pallas_call | solution.py:658
  87.0 14.3 %all_to_all.29.recv = bf16[16,72,128]{2,1,0:T(8,128)(2,1)S(1)} all-to-all(bf16[16,72,128]{2,1,0:T(8,128)(2,1)S(1)} %back_one.1), channel_id=1, replica_groups=mesh['groups'=2,'space'=16] {'space'}, dimensions={0} | all-to-all | bytes 589824 | tf_op jit(solution)/shard_map/all_to_all | solution.py:703
  101.3 0.9 unpack.1
  (1 shorter events, 0.0 us)
Async XLA Ops:
  0.6 1.1 %copy-start = (bf16[3,8,8,16,128]{4,3,2,1,0:T(8,128)(2,1)S(1)}, bf16[3,8,8,16,128]{4,3,2,1,0:T(8,128)(2,1)}, u32[]{:S(2)}) copy-start(bf16[3,8,8,16,128]{4,3,2,1,0:T(8,128)(2,1)} %x_hbm.1) | copy-start | bytes 2359300
  0.6 1.1 %copy-start.1 = (bf16[27,1024]{1,0:T(8,128)(2,1)S(1)}, bf16[27,1024]{1,0:T(8,128)(2,1)}, u32[]{:S(2)}) copy-start(bf16[27,1024]{1,0:T(8,128)(2,1)} %core_one_hbm.1) | copy-start | bytes 165892
  0.7 1.1 %copy-start.2 = (bf16[27,1024]{1,0:T(8,128)(2,1)S(1)}, bf16[27,1024]{1,0:T(8,128)(2,1)}, u32[]{:S(2)}) copy-start(bf16[27,1024]{1,0:T(8,128)(2,1)} %core_two_hbm.1) | copy-start | bytes 165892
  0.7 1.1 %copy-start.6 = (bf16[32,128]{1,0:T(8,128)(2,1)S(1)}, bf16[32,128]{1,0:T(8,128)(2,1)}, u32[]{:S(2)}) copy-start(bf16[32,128]{1,0:T(8,128)(2,1)} %reduce_hbm.1) | copy-start | bytes 24580
  0.7 1.1 %copy-start.9 = (s32[2,4]{1,0:T(2,128)S(1)}, s32[2,4]{1,0:T(2,128)}, u32[]{:S(2)}) copy-start(s32[2,4]{1,0:T(2,128)} %lengths_hbm.1) | copy-start | bytes 100
  0.7 1.1 %copy-start.10 = (s32[16]{0:T(128)S(1)}, s32[16]{0:T(128)}, u32[]{:S(2)}) copy-start(s32[16]{0:T(128)} %owner_hbm.1) | copy-start | bytes 196
  1.8 21.6 %copy-start.3 = (bf16[32,128]{1,0:T(8,128)(2,1)S(1)}, bf16[32,128]{1,0:T(8,128)(2,1)}, u32[]{:S(2)}) copy-start(bf16[32,128]{1,0:T(8,128)(2,1)} %expand_ref.5) | copy-start | bytes 24580
  1.8 21.6 %copy-start.4 = (bf16[32,128]{1,0:T(8,128)(2,1)S(1)}, bf16[32,128]{1,0:T(8,128)(2,1)}, u32[]{:S(2)}) copy-start(bf16[32,128]{1,0:T(8,128)(2,1)} %reduce_ref.1) | copy-start | bytes 24580
  23.4 18.0 %copy-start.5 = (s32[3,1024]{1,0:T(4,128)S(1)}, s32[3,1024]{1,0:T(4,128)}, u32[]{:S(2)}) copy-start(s32[3,1024]{1,0:T(4,128)} %labels.1) | copy-start | bytes 36868
  23.5 18.0 %copy-start.7 = (bf16[32,128]{1,0:T(8,128)(2,1)S(1)}, bf16[32,128]{1,0:T(8,128)(2,1)}, u32[]{:S(2)}) copy-start(bf16[32,128]{1,0:T(8,128)(2,1)} %expand_ref.4) | copy-start | bytes 24580
  23.5 18.0 %copy-start.8 = (bf16[128]{0:T(256)(128)(2,1)S(1)}, bf16[128]{0:T(256)(128)(2,1)}, u32[]{:S(2)}) copy-start(bf16[128]{0:T(256)(128)(2,1)} %param.21) | copy-start | bytes 772
